TPU v7x, 32 devices: a whole 2x2x4 slice. The times are simulated.
32 devices in a mesh: au: 4 (over y, x), row: 8 (over z, core).
Axes of the slice: x: 2, y: 2, z: 4, core: 2. Of those that a mesh axis runs over, the one named last changes fastest.
Arguments:
- tokens: bfloat16 [2, 2560, 2048], P(None, ('row', 'au')), may hold values from -6 to 6
- permutation: int32 [2, 2560], replicated, may hold values from 0 to 2559, each once within a row
- lengths: int32 [2, 4], replicated, may hold values from 1 to 2240, 2560 in all within a row
- w_query: bfloat16 [2048, 2048], P(('row', 'au')), may hold values from -0.125 to 0.125
- w_keyval: bfloat16 [2048, 256], P(('row', 'au')), may hold values from -0.125 to 0.125
- w_out: bfloat16 [2048, 2048], P(('row', 'au')), may hold values from -0.75 to 0.75
- w_gate: bfloat16 [2048, 5632], P(('row', 'au')), may hold values from -0.125 to 0.125
- w_up: bfloat16 [2048, 5632], P(('row', 'au')), may hold values from -0.125 to 0.125
- w_down: bfloat16 [5632, 2048], P(('row', 'au')), may hold values from -0.078125 to 0.078125
- attn_gain: bfloat16 [2048], P(('row', 'au')), may hold values from 0.5 to 1.5
- mlp_gain: bfloat16 [2048], P(('row', 'au')), may hold values from 0.5 to 1.5
- out_grad: bfloat16 [2, 2560, 2048], P(None, ('row', 'au')), may hold values from -6 to 6
- kv_partner: bfloat16 [2, 2560, 256], P(None, ('row', 'au')), may hold values from -6 to 6
Outputs:
- result: bfloat16 [2, 2560, 2048], P(None, ('row', 'au'))
- grad_tokens: bfloat16 [2, 2560, 2048], P(None, ('row', 'au'))
- grad_query: float32 [2048, 2048], P(('row', 'au'))
- grad_keyval: float32 [2048, 256], P(('row', 'au'))
- output_weight_gradient: float32 [2048, 2048], P(('row', 'au'))
- grad_gate: float32 [2048, 5632], P(('row', 'au'))
- grad_up: float32 [2048, 5632], P(('row', 'au'))
- grad_down: float32 [5632, 2048], P(('row', 'au'))
- grad_attn_gain: float32 [2048], P(('row', 'au'))
- grad_mlp_gain: float32 [2048], P(('row', 'au'))
Inputs may be any that keep to these rules, and one draw needn't show every extreme that they name: `permutation`: each row names every place of its micro-batch once. Each row's 4 lengths sum to 2560; the longest is exactly 2240.
All inputs are finite; a program needn't handle non-finite values.
Results may differ from a plain program's by a relative error of at most 0.019.
Values may be sent and summed in bfloat16 or wider, within the bound.
No kernel may reach another device: no remote copies, remote signals or barrier semaphores. Data moves between devices by JAX's collectives and lax.ppermute only.
A program may use at most 448 MiB of HBM per device.

v0:
```python
import math

import jax
import jax.numpy as jnp
from jax import lax
from jax.sharding import PartitionSpec as P

HQ = 16
HEAD_WIDTH = 128


norm_eps = 1e-05
theta_base = 10000.0


def rotate(values, cosine, sine):
    half = values.shape[-1] // 2
    first = values[..., :half]
    second = values[..., half:]
    return jnp.concatenate(
        [first * cosine - second * sine, second * cosine + first * sine], axis=-1
    )


def rotate_back(grads, cosine, sine):
    half = grads.shape[-1] // 2
    first = grads[..., :half]
    second = grads[..., half:]
    return jnp.concatenate(
        [first * cosine + second * sine, second * cosine - first * sine], axis=-1
    )


def document_info(places, lengths_row):
    starts = jnp.cumsum(lengths_row) - lengths_row
    inside = places[:, None] >= starts[None, :]
    documents = jnp.sum(inside.astype(jnp.int32), axis=1) - 1
    begins = jnp.max(jnp.where(inside, starts[None, :], 0), axis=1)
    return (documents, places - begins)


def angle_table(positions):
    half = HEAD_WIDTH // 2
    inverse_freq = jnp.exp(
        -math.log(theta_base) * (2.0 * jnp.arange(half, dtype=jnp.float32) / HEAD_WIDTH)
    )
    angles = positions.astype(jnp.float32)[..., None] * inverse_freq
    return (jnp.cos(angles), jnp.sin(angles))


def token_dot(left, right):
    return lax.dot_general(
        left, right, (((0, 1), (0, 1)), ((), ())), preferred_element_type=jnp.float32
    )


def back_dot(left, right):
    return lax.dot_general(
        left, right, (((2,), (1,)), ((), ())), preferred_element_type=jnp.float32
    )


def on_device(
    tokens,
    permutation,
    lengths,
    w_query,
    w_keyval,
    w_out,
    w_gate,
    w_up,
    w_down,
    attn_gain,
    mlp_gain,
    out_grad,
    kv_partner,
):
    batches, local_rows, width = tokens.shape
    across = lax.axis_size("au")
    slot_count = permutation.shape[1]
    group_rows = across * local_rows
    row_index = lax.axis_index("row")
    au_index = lax.axis_index("au")
    first_slot = (row_index * across + au_index) * local_rows
    group_first = row_index * group_rows
    score_scale = HEAD_WIDTH ** (-0.5)
    key_rows = min(512, slot_count)
    key_blocks = slot_count // key_rows
    slot_docs = []
    local_positions = []
    for batch_index in range(batches):
        documents, _ = document_info(permutation[batch_index], lengths[batch_index])
        slot_docs.append(documents)
        local_places = lax.dynamic_slice_in_dim(permutation[batch_index], first_slot, local_rows)
        _, positions = document_info(local_places, lengths[batch_index])
        local_positions.append(positions)
    slot_docs = jnp.stack(slot_docs)
    cosine, sine = angle_table(jnp.stack(local_positions))
    query_docs = lax.dynamic_slice_in_dim(slot_docs, group_first, group_rows, 1)
    query_places = lax.dynamic_slice_in_dim(permutation, group_first, group_rows, 1)

    def visibility(offset, count):
        key_docs = lax.dynamic_slice_in_dim(slot_docs, offset, count, 1)
        key_places = lax.dynamic_slice_in_dim(permutation, offset, count, 1)
        return (query_docs[:, :, None] == key_docs[:, None, :]) & (
            key_places[:, None, :] <= query_places[:, :, None]
        )

    query_full, keyval_full, out_full, first_norm_gain = (
        lax.all_gather(w_query, ("row", "au"), axis=0, tiled=True),
        lax.all_gather(w_keyval, ("row", "au"), axis=0, tiled=True),
        lax.all_gather(w_out, ("row", "au"), axis=0, tiled=True),
        lax.all_gather(attn_gain, ("row", "au"), axis=0, tiled=True),
    )
    inputs_wide = tokens.astype(jnp.float32)
    inverse_one = lax.rsqrt(jnp.mean(inputs_wide * inputs_wide, axis=-1, keepdims=True) + norm_eps)
    unit_one = inputs_wide * inverse_one
    normed = (unit_one * first_norm_gain.astype(jnp.float32)).astype(jnp.bfloat16)
    query_pre = jnp.dot(normed, query_full, preferred_element_type=jnp.float32).reshape(
        batches, local_rows, HQ, HEAD_WIDTH
    )
    keyval_pre = jnp.dot(normed, keyval_full, preferred_element_type=jnp.float32)
    query = rotate(query_pre, cosine[:, :, None], sine[:, :, None]).astype(jnp.bfloat16)
    key_rot = rotate(keyval_pre[..., :HEAD_WIDTH], cosine, sine)
    keyval = jnp.concatenate([key_rot, keyval_pre[..., HEAD_WIDTH:]], axis=-1).astype(jnp.bfloat16)
    query_head_rows = lax.all_to_all(query, "au", split_axis=2, concat_axis=1, tiled=True)
    keyval_all = lax.all_gather(keyval, ("row", "au"), axis=1, tiled=True)
    heads_here = query_head_rows.shape[2]
    start_state = (
        jnp.zeros((batches, group_rows, heads_here, HEAD_WIDTH), jnp.float32),
        jnp.full((batches, group_rows, heads_here), -1e30, jnp.float32),
        jnp.zeros((batches, group_rows, heads_here), jnp.float32),
    )

    def absorb(running, block_index):
        weighted, highest, denominator = running
        offset = block_index * key_rows
        incoming_values = lax.dynamic_slice_in_dim(keyval_all, offset, key_rows, 1)
        visible = visibility(offset, key_rows)[:, :, None, :]
        scores = (
            jnp.einsum(
                "azol,atl->azot",
                query_head_rows,
                incoming_values[..., :HEAD_WIDTH],
                preferred_element_type=jnp.float32,
            )
            * score_scale
        )
        scores = jnp.where(visible, scores, -1e30)
        new_high = jnp.maximum(highest, jnp.max(scores, axis=-1))
        rescale = jnp.exp(highest - new_high)
        weights = jnp.where(visible, jnp.exp(scores - new_high[..., None]), 0.0)
        denominator = denominator * rescale + jnp.sum(weights, axis=-1)
        weighted = weighted * rescale[..., None] + jnp.einsum(
            "cisz,czn->cisn",
            weights.astype(jnp.bfloat16),
            incoming_values[..., HEAD_WIDTH:],
            preferred_element_type=jnp.float32,
        )
        return ((weighted, new_high, denominator), None)

    (weighted, highest, denominator), _ = lax.scan(
        absorb, start_state, jnp.arange(key_blocks, dtype=jnp.int32)
    )
    attended_heads = weighted / denominator[..., None]
    log_mass = highest + jnp.log(denominator)
    attended = lax.all_to_all(
        attended_heads.astype(jnp.bfloat16), "au", split_axis=1, concat_axis=2, tiled=True
    )
    attended = attended.reshape(batches, local_rows, HQ * HEAD_WIDTH)
    hidden = inputs_wide + jnp.dot(attended, out_full, preferred_element_type=jnp.float32)
    gate_full, up_full, down_full, gain_two = (
        lax.all_gather(w_gate, ("row", "au"), axis=0, tiled=True),
        lax.all_gather(w_up, ("row", "au"), axis=0, tiled=True),
        lax.all_gather(w_down, ("row", "au"), axis=0, tiled=True),
        lax.all_gather(mlp_gain, ("row", "au"), axis=0, tiled=True),
    )
    inverse_two = lax.rsqrt(jnp.mean(hidden * hidden, axis=-1, keepdims=True) + norm_eps)
    unit_two = hidden * inverse_two
    normed_two = (unit_two * gain_two.astype(jnp.float32)).astype(jnp.bfloat16)
    gate = jnp.dot(normed_two, gate_full, preferred_element_type=jnp.float32)
    up_part = jnp.dot(normed_two, up_full, preferred_element_type=jnp.float32)
    inner = (jax.nn.silu(gate) * up_part).astype(jnp.bfloat16)
    result = hidden + jnp.dot(inner, down_full, preferred_element_type=jnp.float32)
    grad_inner = back_dot(out_grad, down_full)
    sigmoid_gate = jax.nn.sigmoid(gate)
    grad_gate = (grad_inner * up_part * sigmoid_gate * (1.0 + gate * (1.0 - sigmoid_gate))).astype(
        jnp.bfloat16
    )
    grad_up = (grad_inner * gate * sigmoid_gate).astype(jnp.bfloat16)
    grad_down_term = token_dot(inner, out_grad)
    grad_gate_term = token_dot(normed_two, grad_gate)
    grad_up_term = token_dot(normed_two, grad_up)
    grad_normed_two = back_dot(grad_gate, gate_full) + back_dot(grad_up, up_full)
    scaled_two = grad_normed_two * gain_two.astype(jnp.float32)
    grad_gain_two = jnp.sum(grad_normed_two * unit_two, axis=(0, 1))
    grad_hidden = out_grad.astype(jnp.float32) + inverse_two * (
        scaled_two - unit_two * jnp.mean(scaled_two * unit_two, axis=-1, keepdims=True)
    )
    shard_gate, shard_up, shard_down, shard_gain_two = (
        lax.psum_scatter(grad_gate_term, ("row", "au"), scatter_dimension=0, tiled=True),
        lax.psum_scatter(grad_up_term, ("row", "au"), scatter_dimension=0, tiled=True),
        lax.psum_scatter(grad_down_term, ("row", "au"), scatter_dimension=0, tiled=True),
        lax.psum_scatter(grad_gain_two, ("row", "au"), scatter_dimension=0, tiled=True),
    )
    grad_branch = grad_hidden.astype(jnp.bfloat16)
    grad_out_term = token_dot(attended, grad_branch)
    grad_attended = (
        back_dot(grad_branch, out_full)
        .astype(jnp.bfloat16)
        .reshape(batches, local_rows, HQ, HEAD_WIDTH)
    )
    gradient_per_head = lax.all_to_all(grad_attended, "au", split_axis=2, concat_axis=1, tiled=True)
    settle = jnp.sum(gradient_per_head.astype(jnp.float32) * attended_heads, axis=-1)

    def key_block(carried, block_index):
        grad_query_acc, grad_keyval_acc = carried
        first_row = block_index * key_rows
        incoming_values = lax.dynamic_slice_in_dim(keyval_all, first_row, key_rows, 1)
        visible = visibility(first_row, key_rows)[:, :, None, :]
        scores = (
            jnp.einsum(
                "azol,atl->azot",
                query_head_rows,
                incoming_values[..., :HEAD_WIDTH],
                preferred_element_type=jnp.float32,
            )
            * score_scale
        )
        weights = jnp.where(visible, jnp.exp(scores - log_mass[..., None]), 0.0)
        grad_value = jnp.einsum(
            "fepu,fepc->fuc",
            weights.astype(jnp.bfloat16),
            gradient_per_head,
            preferred_element_type=jnp.float32,
        )
        grad_weights = jnp.einsum(
            "azol,atl->azot",
            gradient_per_head,
            incoming_values[..., HEAD_WIDTH:],
            preferred_element_type=jnp.float32,
        )
        score_gradient = (weights * (grad_weights - settle[..., None])).astype(jnp.bfloat16)
        grad_query_acc = (
            grad_query_acc
            + jnp.einsum(
                "cisz,czn->cisn",
                score_gradient,
                incoming_values[..., :HEAD_WIDTH],
                preferred_element_type=jnp.float32,
            )
            * score_scale
        )
        grad_key = (
            jnp.einsum(
                "fepu,fepc->fuc",
                score_gradient,
                query_head_rows,
                preferred_element_type=jnp.float32,
            )
            * score_scale
        )
        grad_keyval_acc = lax.dynamic_update_slice_in_dim(
            grad_keyval_acc, jnp.concatenate([grad_key, grad_value], axis=-1), first_row, 1
        )
        return ((grad_query_acc, grad_keyval_acc), None)

    start_grads = (
        jnp.zeros((batches, group_rows, heads_here, HEAD_WIDTH), jnp.float32),
        jnp.zeros((batches, slot_count, 2 * HEAD_WIDTH), jnp.float32),
    )
    (grad_query_heads, grad_keyval_term), _ = lax.scan(
        key_block, start_grads, jnp.arange(key_blocks, dtype=jnp.int32)
    )
    grad_keyval_local = lax.psum_scatter(
        grad_keyval_term, ("row", "au"), scatter_dimension=1, tiled=True
    )
    grad_keyval_local = (grad_keyval_local + kv_partner.astype(jnp.float32)).astype(jnp.bfloat16)
    grad_key_pre = rotate_back(
        grad_keyval_local[..., :HEAD_WIDTH].astype(jnp.float32), cosine, sine
    )
    grad_keyval_pre = jnp.concatenate(
        [grad_key_pre, grad_keyval_local[..., HEAD_WIDTH:].astype(jnp.float32)], axis=-1
    ).astype(jnp.bfloat16)
    grad_query_tokens = lax.all_to_all(
        grad_query_heads.astype(jnp.bfloat16), "au", split_axis=1, concat_axis=2, tiled=True
    )
    grad_query_pre = rotate_back(
        grad_query_tokens.astype(jnp.float32), cosine[:, :, None], sine[:, :, None]
    )
    grad_query_pre = grad_query_pre.astype(jnp.bfloat16).reshape(
        batches, local_rows, HQ * HEAD_WIDTH
    )
    grad_query_term = token_dot(normed, grad_query_pre)
    grad_keyval_weight = token_dot(normed, grad_keyval_pre)
    grad_normed = back_dot(grad_query_pre, query_full) + back_dot(grad_keyval_pre, keyval_full)
    scaled_one = grad_normed * first_norm_gain.astype(jnp.float32)
    grad_gain_one = jnp.sum(grad_normed * unit_one, axis=(0, 1))
    grad_inputs = grad_hidden + inverse_one * (
        scaled_one - unit_one * jnp.mean(scaled_one * unit_one, axis=-1, keepdims=True)
    )
    shard_query, shard_keyval, shard_out, shard_gain_one = (
        lax.psum_scatter(grad_query_term, ("row", "au"), scatter_dimension=0, tiled=True),
        lax.psum_scatter(grad_keyval_weight, ("row", "au"), scatter_dimension=0, tiled=True),
        lax.psum_scatter(grad_out_term, ("row", "au"), scatter_dimension=0, tiled=True),
        lax.psum_scatter(grad_gain_one, ("row", "au"), scatter_dimension=0, tiled=True),
    )
    return (
        result.astype(jnp.bfloat16),
        grad_inputs.astype(jnp.bfloat16),
        shard_query,
        shard_keyval,
        shard_out,
        shard_gate,
        shard_up,
        shard_down,
        shard_gain_one,
        shard_gain_two,
    )


def solution(mesh):
    return jax.shard_map(
        on_device,
        mesh=mesh,
        in_specs=(
            P(None, ("row", "au"), None),
            P(),
            P(),
            P(("row", "au"), None),
            P(("row", "au"), None),
            P(("row", "au"), None),
            P(("row", "au"), None),
            P(("row", "au"), None),
            P(("row", "au"), None),
            P(("row", "au")),
            P(("row", "au")),
            P(None, ("row", "au"), None),
            P(None, ("row", "au"), None),
        ),
        out_specs=(
            P(None, ("row", "au"), None),
            P(None, ("row", "au"), None),
            P(("row", "au"), None),
            P(("row", "au"), None),
            P(("row", "au"), None),
            P(("row", "au"), None),
            P(("row", "au"), None),
            P(("row", "au"), None),
            P(("row", "au")),
            P(("row", "au")),
        ),
        check_vma=False,
    )
```

profile of v0, /device:TPU:0, one launch (start us, length us, event | category | flops | bytes accessed | tf_op | source)
XLA Modules:
  0.0 4822.2 jit_solution(8141116756005571074)
XLA Ops:
  13.5 42.1 all-reduce.5
  59.0 8.7 all-gather.8.cloned.1.call-done
  73.4 73.6 %all-gather.12.cloned.1.call-done = bf16[2048,2048]{1,0:T(8,128)(2,1)} async-done(((bf16[64,2048]{1,0:T(8,128)(2,1)}), bf16[2048,2048]{1,0:T(8,128)(2,1)}) %all-gather.12.cloned.1.call-update) | async-done | bytes 8388624 | tf_op jit(solution)/shard_map/all_gather | solution.py:110
  147.0 4.9 fusion.50
  158.4 9.9 all-to-all-done
  170.3 39.0 all-gather.10.cloned.1.call-done
  209.4 68.5 %while.28 = (s32[]{:T(128)}, f32[2,320,4,128]{3,1,2,0:T(8,128)S(1)}, f32[2,320,4]{1,2,0:T(4,128)S(1)}, f32[2,320,4]{1,2,0:T(4,128)S(1)}, s32[2,320]{1,0:T(2,128)...) while((s32[]{:T(128)}, ...), condition=%wide.region_10.11_spmd.clone, body=%wide.region_7.10_spmd.clone.sunk | while | flops 690106880 | bytes 21034240 | solution.py:162
  211.0 4.3 fusion.161
  218.9 4.2 fusion.164
  224.7 4.3 fusion.161
  238.4 4.3 fusion.161
  252.1 4.3 fusion.161
  265.8 4.3 fusion.161
  285.0 10.0 all-to-all-done.1
  296.6 6.0 multiply_reduce_fusion.3
  302.8 131.8 %all-gather.18.cloned.1.call-done = bf16[2048,5632]{1,0:T(8,128)(2,1)} async-done(((bf16[64,5632]{1,0:T(8,128)(2,1)}), bf16[2048,5632]{1,0:T(8,128)(2,1)}) %all-gather.18.cloned.1.call-update) | async-done | bytes 23068688 | tf_op jit(solution)/shard_map/all_gather | solution.py:174
  434.6 11.4 fusion.38
  446.0 134.2 %all-gather.20.cloned.1.call-done = bf16[5632,2048]{1,0:T(8,128)(2,1)} async-done(((bf16[176,2048]{1,0:T(8,128)(2,1)}), bf16[5632,2048]{1,0:T(8,128)(2,1)}) %all-gather.20.cloned.1.call-update) | async-done | bytes 23068688 | tf_op jit(solution)/shard_map/all_gather | solution.py:175
  580.2 13.5 fusion.32
  593.6 132.2 %all-gather.16.cloned.1.call-done = bf16[2048,5632]{1,0:T(8,128)(2,1)} async-done(((bf16[64,5632]{1,0:T(8,128)(2,1)}), bf16[2048,5632]{1,0:T(8,128)(2,1)}) %all-gather.16.cloned.1.call-update) | async-done | bytes 23068688 | tf_op jit(solution)/shard_map/all_gather | solution.py:173
  725.9 14.1 multiply_convert_fusion.1
  739.9 13.7 fusion.36
  753.7 14.4 multiply_reduce_fusion
  769.8 6.8 fusion.79
  781.1 10.0 all-to-all-done.2
  798.1 96.1 %while.29 = (s32[]{:T(128)}, f32[2,320,4,128]{3,1,2,0:T(8,128)}, f32[2,2560,256]{2,1,0:T(8,128)}, s32[2,320]{1,0:T(2,128)S(1)}, s32[5]{0:T(128)S(1)}, /*index=5*...) while((s32[]{:T(128)}, f32[2,320,4,128]{3,1,2,0:T(8,128)}, ...), condition=%wide.region_15.16_spmd.clone, body=%wide.region_14.15_spmd.clone.sunk | while | flops 1693188096 | bytes 58977584 | solution.py:272
  799.3 4.2 fusion.172
  804.6 4.5 fusion.173
  823.5 4.5 fusion.173
  842.8 4.5 fusion.173
  862.1 4.5 fusion.173
  876.2 4.2 fusion.172
  881.4 4.5 fusion.173
  894.3 142.0 %reduce-scatter.8.cloned.1.call-done = f32[2,80,256]{2,1,0:T(8,128)} async-done(((f32[2,2560,256]{2,1,0:T(8,128)}), f32[2,80,256]{2,1,0:T(8,128)}) %reduce-scatter.8.cloned.1.call-update) | async-done | bytes 163856 | tf_op jit(solution)/shard_map/reduce_scatter | solution.py:275
  1041.1 8.2 convolution_bitcast_fusion.4
  1051.5 12.5 all_to_all.60
  1066.5 8.3 convolution_bitcast_fusion.5
  1075.9 19.4 convolution_bitcast_fusion.2
  1095.3 19.4 convolution_bitcast_fusion.1
  1115.8 19.6 convolution_bitcast_fusion.3
  1136.8 13.0 fusion.61
  1149.8 6.5 fusion.48
  1157.1 39.5 all-reduce.4
  1199.0 333.9 %reduce-scatter.14.cloned.1.call-done = f32[64,2048]{1,0:T(8,128)} async-done(((f32[2048,2048]{1,0:T(8,128)}), f32[64,2048]{1,0:T(8,128)}) %reduce-scatter.14.cloned.1.call-update) | async-done | bytes 524304 | tf_op jit(solution)/shard_map/reduce_scatter | solution.py:305
  1532.9 361.9 %reduce-scatter.10.cloned.1.call-done = f32[64,2048]{1,0:T(8,128)} async-done(((f32[2048,2048]{1,0:T(8,128)}), f32[64,2048]{1,0:T(8,128)}) %reduce-scatter.10.cloned.1.call-update) | async-done | bytes 524304 | tf_op jit(solution)/shard_map/reduce_scatter | solution.py:303
  1894.9 972.9 %reduce-scatter.16.cloned.1.call-done = f32[64,5632]{1,0:T(8,128)} async-done(((f32[2048,5632]{1,0:T(8,128)}), f32[64,5632]{1,0:T(8,128)}) %reduce-scatter.16.cloned.1.call-update) | async-done | bytes 1441808 | tf_op jit(solution)/shard_map/reduce_scatter | solution.py:201
  2867.8 973.8 %reduce-scatter.18.cloned.1.call-done = f32[64,5632]{1,0:T(8,128)} async-done(((f32[2048,5632]{1,0:T(8,128)}), f32[64,5632]{1,0:T(8,128)}) %reduce-scatter.18.cloned.1.call-update) | async-done | bytes 1441808 | tf_op jit(solution)/shard_map/reduce_scatter | solution.py:202
  3841.6 973.6 %reduce-scatter.20.cloned.1.call-done = f32[176,2048]{1,0:T(8,128)} async-done(((f32[5632,2048]{1,0:T(8,128)}), f32[176,2048]{1,0:T(8,128)}) %reduce-scatter.20.cloned.1.call-update) | async-done | bytes 1441808 | tf_op jit(solution)/shard_map/reduce_scatter | solution.py:203
  (273 shorter events, 161.3 us)
Async XLA Ops:
  7.2 60.5 %all-gather.8.cloned.1.call-start = ((), (), s32[]{:S(2)}) async-start(), calls=%async_computation.11 | async-start | bytes 1081344 | tf_op jit(solution)/shard_map/all_gather | solution.py:111
  7.9 139.1 %all-gather.12.cloned.1.call-start = ((), (), s32[]{:S(2)}) async-start(), calls=%async_computation.13 | async-start | bytes 8650752 | tf_op jit(solution)/shard_map/all_gather | solution.py:110
  8.7 200.7 %all-gather.10.cloned.1.call-start = ((), (), s32[]{:S(2)}) async-start(), calls=%async_computation.12 | async-start | bytes 2703360 | tf_op jit(solution)/shard_map/all_gather | solution.py:127
  55.6 91.4 %copy-start.26 = (f32[2048]{0:T(1024)}, f32[2048]{0:T(1024)S(1)}, u32[]{:S(2)}) copy-start(f32[2048]{0:T(1024)S(1)} %convert_element_type.105) | copy-start | bytes 24580
  55.6 13.9 copy-start.35
  57.7 11.8 copy-start.33
  59.0 88.0 %copy-start.29 = (f32[2,80]{1,0:T(2,128)}, f32[2,80]{1,0:T(2,128)S(1)}, u32[]{:S(2)}) copy-start(f32[2,80]{1,0:T(2,128)S(1)} %add_rsqrt_fusion.1) | copy-start | bytes 1924
  69.9 82.7 %copy-start.22 = (f32[2,80,64]{2,1,0:T(8,128)}, f32[2,80,64]{2,1,0:T(8,128)S(1)}, u32[]{:S(2)}) copy-start(f32[2,80,64]{2,1,0:T(8,128)S(1)} %get-tuple-element.342) | copy-start | bytes 122884
  70.0 82.7 %copy-start.24 = (f32[2,80,64]{2,1,0:T(8,128)}, f32[2,80,64]{2,1,0:T(8,128)S(1)}, u32[]{:S(2)}) copy-start(f32[2,80,64]{2,1,0:T(8,128)S(1)} %get-tuple-element.343) | copy-start | bytes 122884
  70.7 76.3 %copy-start.2 = (bf16[2,80,2048]{2,1,0:T(8,128)(2,1)S(1)}, bf16[2,80,2048]{2,1,0:T(8,128)(2,1)}, u32[]{:S(2)}) copy-start(bf16[2,80,2048]{2,1,0:T(8,128)(2,1)} %param.17) | copy-start | bytes 1966084
  70.7 225.8 %all-gather.14.cloned.1.call-start = ((), (), s32[]{:S(2)}) async-start(), calls=%async_computation.14 | async-start | bytes 8650752 | tf_op jit(solution)/shard_map/all_gather | solution.py:112
  71.3 363.3 %all-gather.18.cloned.1.call-start = ((), (), s32[]{:S(2)}) async-start(), calls=%async_computation.16 | async-start | bytes 23789568 | tf_op jit(solution)/shard_map/all_gather | solution.py:174
  71.9 508.3 %all-gather.20.cloned.1.call-start = ((), (), s32[]{:S(2)}) async-start(), calls=%async_computation.17 | async-start | bytes 23789568 | tf_op jit(solution)/shard_map/all_gather | solution.py:175
  72.5 653.4 %all-gather.16.cloned.1.call-start = ((), (), s32[]{:S(2)}) async-start(), calls=%async_computation.15 | async-start | bytes 23789568 | tf_op jit(solution)/shard_map/all_gather | solution.py:173
  153.5 4.8 copy-start.28
  154.7 13.6 all-to-all-start
  277.8 3.3 copy-start.18
  281.1 13.9 all-to-all-start.1
  302.5 465.6 %copy-start.4 = (f32[2,80,2048]{2,1,0:T(8,128)}, f32[2,80,2048]{2,1,0:T(8,128)S(1)}, u32[]{:S(2)}) copy-start(f32[2,80,2048]{2,1,0:T(8,128)S(1)} %get-tuple-element.353) | copy-start | bytes 3932164
  302.8 423.1 %copy-start.8 = (bf16[2,80,2048]{2,1,0:T(8,128)(2,1)}, bf16[2,80,2048]{2,1,0:T(8,128)(2,1)S(1)}, u32[]{:S(2)}) copy-start(bf16[2,80,2048]{2,1,0:T(8,128)(2,1)S(1)} %multiply_convert_fusion.3) | copy-start | bytes 1966084
  739.9 13.8 copy-start.10
  753.7 14.4 copy-start.11
  769.8 6.8 copy-start.6
  777.5 13.6 all-to-all-start.2
  781.0 255.3 %reduce-scatter.8.cloned.1.call-start = ((), (), s32[]{:S(2)}) async-start(), calls=%async_computation.18 | async-start | bytes 5406720 | tf_op jit(solution)/shard_map/reduce_scatter | solution.py:275
  791.1 1.3 copy-start.19
  809.1 3.0 copy-start
  828.0 3.5 copy-start
  847.3 3.5 copy-start
  866.6 3.5 copy-start
  885.9 3.5 copy-start
  894.2 142.1 %copy-start.31 = (bf16[2,80,256]{2,1,0:T(8,128)(2,1)S(1)}, bf16[2,80,256]{2,1,0:T(8,128)(2,1)}, u32[]{:S(2)}) copy-start(bf16[2,80,256]{2,1,0:T(8,128)(2,1)} %param.29) | copy-start | bytes 245764
  894.2 143.0 %copy-start.34 = (f32[2,80]{1,0:T(2,128)S(1)}, f32[2,80]{1,0:T(2,128)}, u32[]{:S(2)}) copy-start(f32[2,80]{1,0:T(2,128)} %copy-done.33) | copy-start | bytes 1924
  894.2 143.1 %copy-start.36 = (f32[64]{0:T(128)S(1)}, f32[64]{0:T(128)}, u32[]{:S(2)}) copy-start(f32[64]{0:T(128)} %copy-done.35) | copy-start | bytes 772
  894.2 143.5 %copy-start.3 = (bf16[2,80,2048]{2,1,0:T(8,128)(2,1)S(1)}, bf16[2,80,2048]{2,1,0:T(8,128)(2,1)}, u32[]{:S(2)}) copy-start(bf16[2,80,2048]{2,1,0:T(8,128)(2,1)} %param.17) | copy-start | bytes 1966084
  894.2 143.5 %copy-start.27 = (f32[2048]{0:T(1024)S(1)}, f32[2048]{0:T(1024)}, u32[]{:S(2)}) copy-start(f32[2048]{0:T(1024)} %copy-done.26) | copy-start | bytes 24580
  894.2 143.5 %copy-start.30 = (f32[2,80]{1,0:T(2,128)S(1)}, f32[2,80]{1,0:T(2,128)}, u32[]{:S(2)}) copy-start(f32[2,80]{1,0:T(2,128)} %copy-done.29) | copy-start | bytes 1924
  894.3 304.7 %reduce-scatter.12.cloned.1.call-start = ((), (), s32[]{:S(2)}) async-start(), calls=%async_computation.20 | async-start | bytes 2162688 | tf_op jit(solution)/shard_map/reduce_scatter | solution.py:304
  1039.6 1.5 copy-start.13
  1039.6 493.3 %reduce-scatter.14.cloned.1.call-start = ((), (), s32[]{:S(2)}) async-start(), calls=%async_computation.21 | async-start | bytes 17301504 | tf_op jit(solution)/shard_map/reduce_scatter | solution.py:305
  1049.3 845.5 %reduce-scatter.10.cloned.1.call-start = ((), (), s32[]{:S(2)}) async-start(), calls=%async_computation.19 | async-start | bytes 17301504 | tf_op jit(solution)/shard_map/reduce_scatter | solution.py:303
  1074.8 1793.0 %reduce-scatter.16.cloned.1.call-start = ((), (), s32[]{:S(2)}) async-start(), calls=%async_computation.22 | async-start | bytes 47579136 | tf_op jit(solution)/shard_map/reduce_scatter | solution.py:201
  1095.3 2746.3 %reduce-scatter.18.cloned.1.call-start = ((), (), s32[]{:S(2)}) async-start(), calls=%async_computation.23 | async-start | bytes 47579136 | tf_op jit(solution)/shard_map/reduce_scatter | solution.py:202
  1114.8 3700.4 %reduce-scatter.20.cloned.1.call-start = ((), (), s32[]{:S(2)}) async-start(), calls=%async_computation.24 | async-start | bytes 47579136 | tf_op jit(solution)/shard_map/reduce_scatter | solution.py:203
  1135.5 1.3 copy-start.5
  1136.8 13.0 copy-start.15
  1136.8 13.0 copy-start.17
  1149.8 6.5 copy-start.21
  (10 other events, 10.1 us)
Sparse Core Ops, SparseCore 0:
  11.0 56.6 all-gather.7
  70.6 76.4 all-gather.11
  150.5 58.8 all-gather.9
  212.1 76.4 all-gather.13
  291.3 143.2 all-gather.17
  437.3 142.7 all-gather.19
  583.0 142.7 all-gather.15
  894.4 141.8 reduce-scatter.7
  1039.8 135.9 reduce-scatter.11
  1178.5 354.3 reduce-scatter.13
  1535.9 358.9 reduce-scatter.9
  1897.7 970.0 reduce-scatter.15
  2870.8 970.7 reduce-scatter.17
  3844.4 970.7 reduce-scatter.19
where the time goes:
time: 4830 us; the launch traced here: 4820 us
  waiting for transfers between devices  4310 us (89%)
  matrix products  303 us (6%)
  blocking collectives  94.1 us (2%)
    reduce_scatter x1, waiting for transfers between devices, on_device(): lax.psum_scatter(grad_up_term, ('row', 'au'), scatter_dimension=0, tiled=...  974 us
    reduce_scatter x1, waiting for transfers between devices, on_device(): lax.psum_scatter(grad_down_term, ('row', 'au'), scatter_dimension=0, tile...  974 us
    reduce_scatter x1, waiting for transfers between devices, on_device(): lax.psum_scatter(grad_gate_term, ('row', 'au'), scatter_dimension=0, tile...  973 us
    reduce_scatter x1, waiting for transfers between devices, on_device(): lax.psum_scatter(grad_query_term, ('row', 'au'), scatter_dimension=0, til...  362 us
    reduce_scatter x1, waiting for transfers between devices, on_device(): lax.psum_scatter(grad_out_term, ('row', 'au'), scatter_dimension=0, tiled...  334 us
    reduce_scatter x1, waiting for transfers between devices, on_device(): lax.psum_scatter(grad_keyval_term, ('row', 'au'), scatter_dimension=1, ti...  142 us
    all_gather x1, waiting for transfers between devices, on_device(): lax.all_gather(w_down, ('row', 'au'), axis=0, tiled=True)  134 us
    all_gather x1, waiting for transfers between devices, on_device(): lax.all_gather(w_gate, ('row', 'au'), axis=0, tiled=True)  132 us
  transfers between devices with their start and end apart: 17, of which 15 were waited for; matrix products, arithmetic and copies ran while one was open for 5% of the time, Pallas kernels for 0%

commit v1 on v0

v1 whole, which is shorter than its diff:
```python
import math

import jax
import jax.numpy as jnp
from jax import lax
from jax.sharding import PartitionSpec as P

HQ = 16
HEAD_WIDTH = 128


norm_eps = 1e-05
theta_base = 10000.0


def rotate(values, cosine, sine):
    half = values.shape[-1] // 2
    first = values[..., :half]
    second = values[..., half:]
    return jnp.concatenate(
        [first * cosine - second * sine, second * cosine + first * sine], axis=-1
    )


def rotate_back(grads, cosine, sine):
    half = grads.shape[-1] // 2
    first = grads[..., :half]
    second = grads[..., half:]
    return jnp.concatenate(
        [first * cosine + second * sine, second * cosine - first * sine], axis=-1
    )


def document_info(places, lengths_row):
    starts = jnp.cumsum(lengths_row) - lengths_row
    inside = places[:, None] >= starts[None, :]
    documents = jnp.sum(inside.astype(jnp.int32), axis=1) - 1
    begins = jnp.max(jnp.where(inside, starts[None, :], 0), axis=1)
    return (documents, places - begins)


def angle_table(positions):
    half = HEAD_WIDTH // 2
    inverse_freq = jnp.exp(
        -math.log(theta_base) * (2.0 * jnp.arange(half, dtype=jnp.float32) / HEAD_WIDTH)
    )
    angles = positions.astype(jnp.float32)[..., None] * inverse_freq
    return (jnp.cos(angles), jnp.sin(angles))


def dot32(left, right, dims):
    return lax.dot_general(left, right, (dims, ((), ())), preferred_element_type=jnp.float32)


def spread(values, axis):
    copies = jnp.broadcast_to(values[None], (lax.axis_size(axis),) + values.shape)
    return lax.all_to_all(copies, axis, 0, 0)


def swap(blocks, axis):
    return lax.all_to_all(blocks, axis, 0, 0)


def on_device(
    tokens,
    permutation,
    lengths,
    w_query,
    w_keyval,
    w_out,
    w_gate,
    w_up,
    w_down,
    attn_gain,
    mlp_gain,
    out_grad,
    kv_partner,
):
    low = jnp.bfloat16
    wide = jnp.float32
    batches, local_rows, width = tokens.shape
    across = lax.axis_size("au")
    rows = lax.axis_size("row")
    slot_count = permutation.shape[1]
    q_width = w_query.shape[1]
    kv_width = w_keyval.shape[1]
    own_width = w_query.shape[0]
    ff = w_gate.shape[1]
    ff_here = ff // rows
    q_here = q_width // across
    kv_here = kv_width // across
    group_tokens = across * batches * local_rows
    row_index = lax.axis_index("row")
    au_index = lax.axis_index("au")
    group_first = row_index * across * local_rows
    first_slot = group_first + au_index * local_rows
    score_scale = HEAD_WIDTH ** (-0.5)
    key_rows = min(512, slot_count)
    key_blocks = slot_count // key_rows

    gain_one = attn_gain.astype(wide)[:, None]
    gain_two = mlp_gain.astype(wide)[:, None]
    query_scaled = (w_query.astype(wide) * gain_one).astype(low)
    keyval_scaled = (w_keyval.astype(wide) * gain_one).astype(low)
    gate_scaled = (w_gate.astype(wide) * gain_two).astype(low)
    up_scaled = (w_up.astype(wide) * gain_two).astype(low)

    slot_docs = []
    group_positions = []
    for batch_index in range(batches):
        documents, positions = document_info(permutation[batch_index], lengths[batch_index])
        slot_docs.append(documents)
        group_positions.append(
            lax.dynamic_slice_in_dim(positions, group_first, across * local_rows)
        )
    slot_docs = jnp.stack(slot_docs)
    group_cosine, group_sine = angle_table(jnp.stack(group_positions))
    cosine = lax.dynamic_slice_in_dim(group_cosine, au_index * local_rows, local_rows, 1)
    sine = lax.dynamic_slice_in_dim(group_sine, au_index * local_rows, local_rows, 1)
    group_cosine = group_cosine.reshape(batches, across, local_rows, -1).transpose(1, 0, 2, 3)
    group_sine = group_sine.reshape(batches, across, local_rows, -1).transpose(1, 0, 2, 3)
    query_docs = lax.dynamic_slice_in_dim(slot_docs, first_slot, local_rows, 1)
    query_places = lax.dynamic_slice_in_dim(permutation, first_slot, local_rows, 1)

    def visibility(offset, count):
        key_docs = lax.dynamic_slice_in_dim(slot_docs, offset, count, 1)
        key_places = lax.dynamic_slice_in_dim(permutation, offset, count, 1)
        return (query_docs[:, :, None] == key_docs[:, None, :]) & (
            key_places[:, None, :] <= query_places[:, :, None]
        )

    column_blocks = query_scaled.reshape(own_width, across, q_here).transpose(1, 0, 2)
    keyval_blocks = jnp.broadcast_to(keyval_scaled[None], (across, own_width, kv_width))
    column_blocks = swap(jnp.concatenate([column_blocks, keyval_blocks], axis=-1), "au")
    columns = lax.all_gather(column_blocks, "row", axis=0).reshape(width, q_here + kv_width)

    inputs_wide = tokens.astype(wide)
    inverse_one = lax.rsqrt(jnp.mean(inputs_wide * inputs_wide, axis=-1, keepdims=True) + norm_eps)
    unit_one = inputs_wide * inverse_one
    unit_group = spread(unit_one.astype(low), "au")

    projected = dot32(unit_group, columns, ((3,), (0,)))
    query_group = projected[..., :q_here].reshape(
        across, batches, local_rows, q_here // HEAD_WIDTH, HEAD_WIDTH
    )
    query_group = rotate(query_group, group_cosine[:, :, :, None], group_sine[:, :, :, None])
    query = swap(query_group.astype(low), "au")
    query = query.transpose(1, 2, 0, 3, 4).reshape(batches, local_rows, HQ, HEAD_WIDTH)
    key_group = rotate(
        projected[..., q_here : q_here + HEAD_WIDTH], group_cosine, group_sine
    )
    keyval = jnp.concatenate([key_group, projected[..., q_here + HEAD_WIDTH :]], axis=-1)
    keyval = keyval.astype(low).transpose(1, 0, 2, 3).reshape(batches, -1, kv_width)
    keyval_all = lax.all_gather(keyval, "row", axis=1, tiled=True)

    out_full = lax.all_gather(w_out, ("row", "au"), axis=0, tiled=True)

    ff_blocks = jnp.concatenate(
        [gate_scaled.reshape(own_width, rows, ff_here), up_scaled.reshape(own_width, rows, ff_here)],
        axis=-1,
    ).transpose(1, 0, 2)
    ff_blocks = swap(ff_blocks, "row")
    ff_full = lax.all_gather(ff_blocks, "au", axis=1).reshape(width, 2 * ff_here)
    down_full = lax.all_gather(w_down, "au", axis=0, tiled=True)
    out_grad_rows = lax.all_gather(out_grad, "row", axis=0).reshape(-1, width)

    start_state = (
        jnp.zeros((batches, local_rows, HQ, HEAD_WIDTH), jnp.float32),
        jnp.full((batches, local_rows, HQ), -1e30, jnp.float32),
        jnp.zeros((batches, local_rows, HQ), jnp.float32),
    )

    def absorb(running, block_index):
        weighted, highest, denominator = running
        offset = block_index * key_rows
        incoming_values = lax.dynamic_slice_in_dim(keyval_all, offset, key_rows, 1)
        visible = visibility(offset, key_rows)[:, :, None, :]
        scores = (
            jnp.einsum(
                "azol,atl->azot",
                query,
                incoming_values[..., :HEAD_WIDTH],
                preferred_element_type=jnp.float32,
            )
            * score_scale
        )
        scores = jnp.where(visible, scores, -1e30)
        new_high = jnp.maximum(highest, jnp.max(scores, axis=-1))
        rescale = jnp.exp(highest - new_high)
        weights = jnp.where(visible, jnp.exp(scores - new_high[..., None]), 0.0)
        denominator = denominator * rescale + jnp.sum(weights, axis=-1)
        weighted = weighted * rescale[..., None] + jnp.einsum(
            "cisz,czn->cisn",
            weights.astype(jnp.bfloat16),
            incoming_values[..., HEAD_WIDTH:],
            preferred_element_type=jnp.float32,
        )
        return ((weighted, new_high, denominator), None)

    (weighted, highest, denominator), _ = lax.scan(
        absorb, start_state, jnp.arange(key_blocks, dtype=jnp.int32)
    )
    attended_wide = weighted / denominator[..., None]
    log_mass = highest + jnp.log(denominator)
    attended = attended_wide.astype(low).reshape(batches, local_rows, q_width)
    attended_group = spread(attended, "au")
    hidden = inputs_wide + dot32(attended, out_full, ((2,), (0,)))

    inverse_two = lax.rsqrt(jnp.mean(hidden * hidden, axis=-1, keepdims=True) + norm_eps)
    unit_two = hidden * inverse_two
    unit_rows = lax.all_gather(unit_two.astype(low), "row", axis=0).reshape(-1, width)
    both = dot32(unit_rows, ff_full, ((1,), (0,)))
    gate = both[:, :ff_here]
    up_part = both[:, ff_here:]
    sigmoid_gate = jax.nn.sigmoid(gate)
    inner = (gate * sigmoid_gate * up_part).astype(low)
    grad_inner = dot32(out_grad_rows, down_full, ((1,), (1,)))
    grad_gate = grad_inner * up_part * sigmoid_gate * (1.0 + gate * (1.0 - sigmoid_gate))
    grad_up = grad_inner * gate * sigmoid_gate
    grad_both = jnp.concatenate([grad_gate.astype(low), grad_up.astype(low)], axis=1)
    scaled_two_part = dot32(grad_both, ff_full, ((1,), (1,)))
    scaled_two = lax.psum_scatter(
        scaled_two_part.astype(low).reshape(rows, batches, local_rows, width), "row"
    ).astype(wide)
    result_part = dot32(inner, down_full, ((1,), (0,)))
    result = hidden + lax.psum_scatter(
        result_part.astype(low).reshape(rows, batches, local_rows, width), "row"
    ).astype(wide)

    grad_hidden = out_grad.astype(wide) + inverse_two * (
        scaled_two - unit_two * jnp.mean(scaled_two * unit_two, axis=-1, keepdims=True)
    )
    grad_branch = grad_hidden.astype(low)
    grad_attended = (
        dot32(grad_branch, out_full, ((2,), (1,)))
        .astype(low)
        .reshape(batches, local_rows, HQ, HEAD_WIDTH)
    )
    branch_columns = swap(
        grad_branch.reshape(batches, local_rows, across, -1).transpose(2, 0, 1, 3), "au"
    )

    both_term = dot32(unit_rows, grad_both, ((0,), (0,))).astype(low)
    both_term = both_term.reshape(rows, across, own_width, 2 * ff_here).transpose(1, 0, 2, 3)
    both_term = lax.psum_scatter(
        both_term.reshape(-1, 2 * ff_here), "au", scatter_dimension=0, tiled=True
    )
    both_term = swap(both_term.reshape(rows, own_width, 2 * ff_here), "row").astype(wide)
    gate_term = both_term[..., :ff_here].transpose(1, 0, 2).reshape(own_width, ff)
    up_term = both_term[..., ff_here:].transpose(1, 0, 2).reshape(own_width, ff)
    down_term = dot32(inner, out_grad_rows, ((0,), (0,))).astype(low)
    shard_down = lax.psum_scatter(
        down_term, "au", scatter_dimension=0, tiled=True
    ).astype(wide)
    shard_gain_two = jnp.sum(
        gate_term * w_gate.astype(wide) + up_term * w_up.astype(wide), axis=1
    )
    shard_gate = gate_term * gain_two
    shard_up = up_term * gain_two

    settle = jnp.sum(grad_attended.astype(jnp.float32) * attended_wide, axis=-1)

    def key_block(carried, block_index):
        grad_query_acc, grad_keyval_acc = carried
        first_row = block_index * key_rows
        incoming_values = lax.dynamic_slice_in_dim(keyval_all, first_row, key_rows, 1)
        visible = visibility(first_row, key_rows)[:, :, None, :]
        scores = (
            jnp.einsum(
                "azol,atl->azot",
                query,
                incoming_values[..., :HEAD_WIDTH],
                preferred_element_type=jnp.float32,
            )
            * score_scale
        )
        weights = jnp.where(visible, jnp.exp(scores - log_mass[..., None]), 0.0)
        grad_value = jnp.einsum(
            "fepu,fepc->fuc",
            weights.astype(jnp.bfloat16),
            grad_attended,
            preferred_element_type=jnp.float32,
        )
        grad_weights = jnp.einsum(
            "azol,atl->azot",
            grad_attended,
            incoming_values[..., HEAD_WIDTH:],
            preferred_element_type=jnp.float32,
        )
        score_gradient = (weights * (grad_weights - settle[..., None])).astype(jnp.bfloat16)
        grad_query_acc = (
            grad_query_acc
            + jnp.einsum(
                "cisz,czn->cisn",
                score_gradient,
                incoming_values[..., :HEAD_WIDTH],
                preferred_element_type=jnp.float32,
            )
            * score_scale
        )
        grad_key = (
            jnp.einsum(
                "fepu,fepc->fuc",
                score_gradient,
                query,
                preferred_element_type=jnp.float32,
            )
            * score_scale
        )
        grad_keyval_acc = lax.dynamic_update_slice_in_dim(
            grad_keyval_acc, jnp.concatenate([grad_key, grad_value], axis=-1), first_row, 1
        )
        return ((grad_query_acc, grad_keyval_acc), None)

    start_grads = (
        jnp.zeros((batches, local_rows, HQ, HEAD_WIDTH), jnp.float32),
        jnp.zeros((batches, slot_count, 2 * HEAD_WIDTH), jnp.float32),
    )
    (grad_query_heads, grad_keyval_term), _ = lax.scan(
        key_block, start_grads, jnp.arange(key_blocks, dtype=jnp.int32)
    )
    keyval_blocks = grad_keyval_term.astype(low).reshape(
        batches, rows, across, local_rows, kv_width
    )
    keyval_blocks = swap(keyval_blocks.transpose(2, 1, 0, 3, 4), "au")
    keyval_blocks = jnp.sum(keyval_blocks.astype(wide), axis=0).astype(low)
    grad_keyval_local = jnp.sum(swap(keyval_blocks, "row").astype(wide), axis=0)
    grad_keyval_local = (grad_keyval_local + kv_partner.astype(wide)).astype(low)
    grad_key_pre = rotate_back(grad_keyval_local[..., :HEAD_WIDTH].astype(wide), cosine, sine)
    grad_keyval_pre = jnp.concatenate(
        [grad_key_pre, grad_keyval_local[..., HEAD_WIDTH:].astype(wide)], axis=-1
    ).astype(low)
    grad_query_pre = rotate_back(
        grad_query_heads.astype(low).astype(wide), cosine[:, :, None], sine[:, :, None]
    )
    grad_query_pre = grad_query_pre.astype(low).reshape(batches, local_rows, q_width)

    def column_split(values):
        blocks = values.reshape(batches, local_rows, across, -1).transpose(2, 0, 1, 3)
        return swap(blocks, "au")

    def row_owner(term):
        blocks = term.astype(low).reshape(rows, across, own_width, -1)
        part = lax.psum_scatter(blocks, "row")
        return swap(part, "au").transpose(1, 0, 2).reshape(own_width, -1).astype(wide)

    group_dims = ((0, 1, 2), (0, 1, 2))
    shard_out = row_owner(dot32(attended_group, branch_columns, group_dims))
    query_term = row_owner(dot32(unit_group, column_split(grad_query_pre), group_dims))
    keyval_term = row_owner(dot32(unit_group, column_split(grad_keyval_pre), group_dims))
    shard_gain_one = jnp.sum(query_term * w_query.astype(wide), axis=1) + jnp.sum(
        keyval_term * w_keyval.astype(wide), axis=1
    )
    shard_query = query_term * gain_one
    shard_keyval = keyval_term * gain_one

    query_full = lax.all_gather(query_scaled, ("row", "au"), axis=0, tiled=True)
    keyval_full = columns[:, q_here:]
    scaled_one = dot32(grad_query_pre, query_full, ((2,), (1,))) + dot32(
        grad_keyval_pre, keyval_full, ((2,), (1,))
    )
    grad_inputs = grad_hidden + inverse_one * (
        scaled_one - unit_one * jnp.mean(scaled_one * unit_one, axis=-1, keepdims=True)
    )
    return (
        result.astype(low),
        grad_inputs.astype(low),
        shard_query,
        shard_keyval,
        shard_out,
        shard_gate,
        shard_up,
        shard_down,
        shard_gain_one,
        shard_gain_two,
    )


def solution(mesh):
    return jax.shard_map(
        on_device,
        mesh=mesh,
        in_specs=(
            P(None, ("row", "au"), None),
            P(),
            P(),
            P(("row", "au"), None),
            P(("row", "au"), None),
            P(("row", "au"), None),
            P(("row", "au"), None),
            P(("row", "au"), None),
            P(("row", "au"), None),
            P(("row", "au")),
            P(("row", "au")),
            P(None, ("row", "au"), None),
            P(None, ("row", "au"), None),
        ),
        out_specs=(
            P(None, ("row", "au"), None),
            P(None, ("row", "au"), None),
            P(("row", "au"), None),
            P(("row", "au"), None),
            P(("row", "au"), None),
            P(("row", "au"), None),
            P(("row", "au"), None),
            P(("row", "au"), None),
            P(("row", "au")),
            P(("row", "au")),
        ),
        check_vma=False,
    )
```

time: 4830 us -> 932 us (0.19)
  waiting for transfers between devices: 4310 us -> 405 us
  matrix products: 303 us -> 217 us
    reduce_scatter x7, waiting for transfers between devices: 3760 us -> 47.1 us  [the longest x1 24.8 us: on_device(): lax.psum_scatter(scaled_two_part.astype(low).reshape(rows, batches, local...]
    all_gather x7 -> x8, waiting for transfers between devices: 520 us -> 191 us  [the longest x1 57.7 us: on_device(): out_grad_rows = lax.all_gather(out_grad, 'row', axis=0).reshape(-1, width)]
    all_to_all x3 -> x10, waiting for transfers between devices: 30 us -> 165 us  [the longest x8 108 us: swap(): return lax.all_to_all(blocks, axis, 0, 0)]
    all_to_all x1 -> x4, blocking collectives: 12.5 us -> 103 us  [swap(): return lax.all_to_all(blocks, axis, 0, 0)]
    dot_general x43 -> x39, matrix products: 265 us -> 176 us  [the longest x14 101 us: dot32(): lax.dot_general(left, right, (dims, ((), ())), preferred_element_type=jnp...]
    unnamed x2 -> x0, blocking collectives: 81.6 us -> none
  transfers between devices with their start and end apart: 17 -> 25, of which waited for: 15 -> 17; matrix products, arithmetic and copies ran while one was open for 5% -> 34% of each run, Pallas kernels for 0% -> 0%
where the time goes in v1:
time: 932 us; the launch traced here: 921 us
  waiting for transfers between devices  405 us (43%)
  matrix products  217 us (23%)
  blocking collectives  103 us (11%)
  local copies, waits for them, and re-layouts  75 us (8%)
  other arithmetic  58 us (6%)
  starting transfers between devices  40.3 us (4%)
  between operations  15.5 us (2%)
    all_to_all x8, waiting for transfers between devices, swap(): return lax.all_to_all(blocks, axis, 0, 0)  108 us
    all_to_all x4, blocking collectives, swap(): return lax.all_to_all(blocks, axis, 0, 0)  103 us
    dot_general x14, matrix products, dot32(): lax.dot_general(left, right, (dims, ((), ())), preferred_element_type=jnp...  101 us
    all_gather x1, waiting for transfers between devices, on_device(): out_grad_rows = lax.all_gather(out_grad, 'row', axis=0).reshape(-1, width)  57.7 us
    all_to_all x2, waiting for transfers between devices, spread(): return lax.all_to_all(copies, axis, 0, 0)  56.5 us
    all_gather x1, waiting for transfers between devices, on_device(): lax.all_gather(unit_two.astype(low), 'row', axis=0).reshape(-1, width)  52.3 us
    all_gather x1, waiting for transfers between devices, on_device(): lax.all_gather(ff_blocks, 'au', axis=1).reshape(width, 2 * ff_here)  49.6 us
    all_to_all x8, starting transfers between devices, swap(): return lax.all_to_all(blocks, axis, 0, 0)  29.9 us
  transfers between devices with their start and end apart: 25, of which 17 were waited for; matrix products, arithmetic and copies ran while one was open for 34% of the time, Pallas kernels for 0%

profile of v1, /device:TPU:0, one launch (start us, length us, event | category | flops | bytes accessed | tf_op | source)
XLA Modules:
  0.0 921.2 jit_solution(18101240943898931283)
XLA Ops:
  10.0 12.2 %all_to_all.70 = bf16[4,64,768]{2,1,0:T(8,128)(2,1)} all-to-all(bf16[4,64,768]{2,1,0:T(8,128)(2,1)S(1)} %pad_maximum_fusion.5), channel_id=1, replica_groups=mesh['au'=4,'row'=8] {'au'}, dimensions={0} | all-to-all | bytes 786432 | tf_op jit(solution)/shard_map/all_to_all | solution.py:61
  29.9 28.1 %all-to-all-done = bf16[4,2,80,2048]{3,2,1,0:T(8,128)(2,1)S(1)} async-done(((bf16[4,2,80,2048]{3,2,1,0:T(8,128)(2,1)}), bf16[4,2,80,2048]{3,2,1,0:T(8,128)(2,1)S(1)}, u32[]{:S(2)}, u32[]{:S(2)}) %all-to-all-start) | async-done | bytes 2621472 | tf_op jit(solution)/shard_map/all_to_all | solution.py:57
  83.7 47.6 %all-to-all-done.3 = bf16[8,64,1408]{2,1,0:T(8,128)(2,1)S(1)} async-done(((bf16[8,64,1408]{2,1,0:T(8,128)(2,1)}), bf16[8,64,1408]{2,1,0:T(8,128)(2,1)S(1)}, u32[]{:S(2)}, u32[]{:S(2)}) %all-to-all-start.3) | async-done | bytes 1441824 | tf_op jit(solution)/shard_map/all_to_all | solution.py:61
  137.3 9.2 all-to-all-done.2
  146.6 67.9 %while.28 = (s32[]{:T(128)}, f32[2,80,16,128]{3,2,1,0:T(8,128)}, f32[2,80,16]{1,2,0:T(8,128)S(1)}, f32[2,80,16]{1,2,0:T(8,128)S(1)}, s32[2,80]{1,0:T(2,128)S(1)}...) while((s32[]{:T(128)}, f32[2,80,16,128]{3,2,1,0:T(8,128)}, ...), condition=%wide.region_10.11_spmd.clone, body=%wide.region_7.10_spmd.clone.sunk | while | flops 684126720 | bytes 19975672 | solution.py:200
  148.0 4.2 fusion.132
  161.0 4.2 fusion.132
  188.6 4.2 fusion.132
  196.6 4.3 fusion.135
  216.7 6.0 multiply_reduce_fusion.1
  225.6 49.6 %all-gather.25.cloned.1.call-done = bf16[8,256,1408]{2,0,1:T(8,128)(2,1)} async-done(((bf16[8,64,1408]{2,0,1:T(8,128)(2,1)}), bf16[8,256,1408]{2,0,1:T(8,128)(2,1)}) %all-gather.25.cloned.1.call-update) | async-done | bytes 5767184 | tf_op jit(solution)/shard_map/all_gather | solution.py:163
  275.2 5.8 copy.148
  281.1 52.3 %all-gather.23.cloned.1.call-done = bf16[16,80,2048]{2,1,0:T(8,128)(2,1)} async-done(((bf16[2,80,2048]{2,1,0:T(8,128)(2,1)}), bf16[16,80,2048]{2,1,0:T(8,128)(2,1)}) %all-gather.23.cloned.1.call-update) | async-done | bytes 5242896 | tf_op jit(solution)/shard_map/all_gather | solution.py:211
  333.4 13.7 %fusion.82 = f32[1280,1408]{1,0:T(8,128)} fusion(bf16[1280,2048]{1,0:T(8,128)(2,1)} %bitcast.297, bf16[2048,1408]{1,0:T(8,128)(2,1)} %bitcast.268), kind=kOutput, calls=%fused_computation.184 | convolution fusion | flops 7381975040 | bytes 18219008 | tf_op jit(solution)/shard_map/dot_general | solution.py:52
  347.0 28.7 %all-gather.17.cloned.1.call-done = bf16[704,2048]{1,0:T(8,128)(2,1)} async-done(((bf16[176,2048]{1,0:T(8,128)(2,1)}), bf16[704,2048]{1,0:T(8,128)(2,1)}) %all-gather.17.cloned.1.call-update) | async-done | bytes 2883600 | tf_op jit(solution)/shard_map/all_gather | solution.py:164
  375.7 57.7 %all-gather.27.cloned.1.call-done = bf16[16,80,2048]{2,1,0:T(8,128)(2,1)} async-done(((bf16[2,80,2048]{2,1,0:T(8,128)(2,1)}), bf16[16,80,2048]{2,1,0:T(8,128)(2,1)}) %all-gather.27.cloned.1.call-update) | async-done | bytes 5242896 | tf_op jit(solution)/shard_map/all_gather | solution.py:165
  433.4 12.6 %multiply_convert_fusion.1 = (bf16[1280,704]{1,0:T(8,128)(2,1)S(1)}, bf16[1280,704]{1,0:T(8,128)(2,1)S(1)}, bf16[1280,704]{1,0:T(8,128)(2,1)}) fusion(f32[1280,1408]{1,0:T(8,128)} %fusion.82, bf16[1280,2048]{1,0:T(8,128)(2,1)} %bitcast.295, bf16[704,2048]{1,0:T(8,128)(2,1)} %all-gather.17.cloned.1.call-done), kind=kOutput, calls=%fused_computation.59 | convolution fusion | flops 3705405440 | bytes 20742144 | tf_op jit(solution)/shard_map/dot_general | solution.py:52
  446.0 10.2 %convolution_convert_fusion.2 = bf16[1280,2048]{1,0:T(8,128)(2,1)} fusion(bf16[2048,1408]{1,0:T(8,128)(2,1)S(1)} %bitcast.269, bf16[1280,704]{1,0:T(8,128)(2,1)S(1)} %get-tuple-element.366, bf16[1280,704]{1,0:T(8,128)(2,1)S(1)} %get-tuple-element.365), kind=kOutput, calls=%fused_computation.55 | convolution fusion | flops 7391805440 | bytes 14614528 | tf_op jit(solution)/shard_map/dot_general | solution.py:52
  456.8 11.8 %convolution_convert_fusion = bf16[2048,1408]{1,0:T(8,128)(2,1)S(1)} fusion(bf16[1280,2048]{1,0:T(8,128)(2,1)} %bitcast.298, bf16[1280,704]{1,0:T(8,128)(2,1)} %copy-done.50, bf16[1280,704]{1,0:T(8,128)(2,1)} %copy-done.49), kind=kOutput, calls=%fused_computation.53 | convolution fusion | flops 7392067584 | bytes 14614528 | tf_op jit(solution)/shard_map/dot_general | solution.py:52
  471.6 8.6 convolution_convert_fusion.3
  481.2 9.0 convolution_convert_fusion.1
  490.3 24.8 %reduce-scatter.10.cloned.1.call-done = bf16[1,2,80,2048]{3,2,1,0:T(8,128)(2,1)} async-done(((bf16[8,2,80,2048]{3,2,1,0:T(8,128)(2,1)}), bf16[1,2,80,2048]{3,2,1,0:T(8,128)(2,1)}) %reduce-scatter.10.cloned.1.call-update) | async-done | bytes 655376 | tf_op jit(solution)/shard_map/reduce_scatter | solution.py:222
  518.0 6.6 fusion.44
  528.7 108.5 %while.29 = (s32[]{:T(128)}, f32[2,80,16,128]{3,2,1,0:T(8,128)}, bf16[2,2560,256]{2,1,0:T(8,128)(2,1)}, s32[2,80]{1,0:T(2,128)S(1)}, s32[5]{0:T(128)S(1)}, /*ind...) while((s32[]{:T(128)}, f32[2,80,16,128]{3,2,1,0:T(8,128)}, ...), condition=%wide.region_17.18_spmd.clone, body=%wide.region_16.17_spmd.clone.sunk | while | flops 1693368320 | bytes 57187908 | solution.py:319
  530.3 4.3 fusion.143
  534.6 4.5 fusion.144
  551.6 4.2 fusion.143
  555.8 4.6 fusion.144
  573.4 4.2 fusion.143
  577.6 4.6 fusion.144
  595.1 4.2 fusion.143
  599.3 4.7 fusion.144
  617.0 4.2 fusion.143
  621.2 4.6 fusion.144
  639.3 40.2 %all_to_all.71 = bf16[4,8,2,80,256]{4,3,1,2,0:T(8,128)(2,1)S(1)} all-to-all(bf16[4,8,2,80,256]{4,3,1,2,0:T(8,128)(2,1)S(1)} %copy.154), channel_id=1, replica_groups=mesh['au'=4,'row'=8] {'au'}, dimensions={0} | all-to-all | bytes 5242880 | tf_op jit(solution)/shard_map/all_to_all | solution.py:61
  682.1 39.9 %all_to_all.72 = bf16[8,2,80,256]{3,2,1,0:T(8,128)(2,1)S(1)} all-to-all(bf16[8,2,80,256]{3,2,1,0:T(8,128)(2,1)S(1)} %copy.156), channel_id=1, replica_groups=mesh['au'=4,'row'=8] {'row'}, dimensions={0} | all-to-all | bytes 1310720 | tf_op jit(solution)/shard_map/all_to_all | solution.py:61
  723.9 4.7 all-to-all-start.10
  730.9 28.4 %all-to-all-done.10 = bf16[4,2,80,2048]{3,2,1,0:T(8,128)(2,1)} async-done(((bf16[4,2,80,2048]{3,2,1,0:T(8,128)(2,1)}), bf16[4,2,80,2048]{3,2,1,0:T(8,128)(2,1)}, u32[]{:S(2)}, u32[]{:S(2)}) %all-to-all-start.10) | async-done | bytes 2621472 | tf_op jit(solution)/shard_map/all_to_all | solution.py:57
  773.6 6.4 all-to-all-done.11
  780.0 5.1 bitcast_convert_fusion
  789.8 10.6 %all_to_all.73 = bf16[4,2,80,512]{3,2,1,0:T(8,128)(2,1)S(1)} all-to-all(bf16[4,2,80,512]{3,2,1,0:T(8,128)(2,1)S(1)} %bitcast.276), channel_id=1, replica_groups=mesh['au'=4,'row'=8] {'au'}, dimensions={0} | all-to-all | bytes 1310720 | tf_op jit(solution)/shard_map/all_to_all | solution.py:61
  803.7 4.3 all-to-all-start.13
  810.7 6.4 fusion.35
  823.2 31.5 %all-to-all-done.13 = bf16[8,64,1408]{2,1,0:T(8,128)(2,1)} async-done(((bf16[8,64,1408]{2,1,0:T(8,128)(2,1)}), bf16[8,64,1408]{2,1,0:T(8,128)(2,1)}, u32[]{:S(2)}, u32[]{:S(2)}) %all-to-all-start.13) | async-done | bytes 1441824 | tf_op jit(solution)/shard_map/all_to_all | solution.py:61
  867.1 4.4 fusion.53
  876.7 4.6 all-to-all-done.12
  881.3 22.2 %reduce-scatter.12.cloned.1.call-done = bf16[1,4,64,512]{3,2,1,0:T(8,128)(2,1)} async-done(((bf16[8,4,64,512]{3,2,1,0:T(8,128)(2,1)}), bf16[1,4,64,512]{3,2,1,0:T(8,128)(2,1)}) %reduce-scatter.12.cloned.1.call-update) | async-done | bytes 262160 | tf_op jit(solution)/shard_map/reduce_scatter | solution.py:344
  908.1 4.5 all-to-all-done.7
  (372 shorter events, 230.0 us)
Async XLA Ops:
  7.2 15.0 %copy-start.7 = (bf16[2,80,2048]{2,1,0:T(8,128)(2,1)S(1)}, bf16[2,80,2048]{2,1,0:T(8,128)(2,1)}, u32[]{:S(2)}) copy-start(bf16[2,80,2048]{2,1,0:T(8,128)(2,1)} %param.17) | copy-start | bytes 1966084
  7.2 53.2 %all-gather.21.cloned.1.call-start = ((), (), s32[]{:S(2)}) async-start(), calls=%async_computation.32 | async-start | bytes 3538944 | tf_op jit(solution)/shard_map/all_gather | solution.py:135
  7.9 17.1 %copy-start.41 = (f32[64]{0:T(128)}, f32[64]{0:T(128)S(1)}, u32[]{:S(2)}) copy-start(f32[64]{0:T(128)S(1)} %convert_element_type.215) | copy-start | bytes 772
  9.0 16.0 %copy-start.22 = (bf16[64,2048]{1,0:T(8,128)(2,1)}, bf16[64,2048]{1,0:T(8,128)(2,1)S(1)}, u32[]{:S(2)}) copy-start(bf16[64,2048]{1,0:T(8,128)(2,1)S(1)} %fusion.65) | copy-start | bytes 786436
  25.0 33.0 %all-to-all-start = ((bf16[4,2,80,2048]{3,2,1,0:T(8,128)(2,1)}), bf16[4,2,80,2048]{3,2,1,0:T(8,128)(2,1)S(1)}, u32[]{:S(2)}, u32[]{:S(2)}) async-start(bf16[4,2,80,2048]{3,2,1,0:T(8,128)(2,1)} %broadcast_in_dim.61), calls=%async_computation | async-start | bytes 5242880 | tf_op jit(solution)/shard_map/all_to_all | solution.py:57
  28.8 117.7 %all-gather.13.cloned.1.call-start = ((), (), s32[]{:S(2)}) async-start(), calls=%async_computation.21 | async-start | bytes 2949120 | tf_op jit(solution)/shard_map/all_gather | solution.py:154
  29.7 34.8 %copy-start.35 = (s32[320]{0:T(512)}, s32[320]{0:T(512)S(1)}, u32[]{:S(2)}) copy-start(s32[320]{0:T(512)S(1)} %get-tuple-element.403) | copy-start | bytes 3844
  29.7 34.8 %copy-start.37 = (s32[320]{0:T(512)}, s32[320]{0:T(512)S(1)}, u32[]{:S(2)}) copy-start(s32[320]{0:T(512)S(1)} %get-tuple-element.404) | copy-start | bytes 3844
  29.9 34.7 %copy-start.44 = (f32[64]{0:T(128)}, f32[64]{0:T(128)S(1)}, u32[]{:S(2)}) copy-start(f32[64]{0:T(128)S(1)} %multiply_exponential_fusion) | copy-start | bytes 772
  58.0 6.5 copy-start.4
  68.9 147.8 %all-gather.15.cloned.1.call-start = ((), (), s32[]{:S(2)}) async-start(), calls=%async_computation.22 | async-start | bytes 8650752 | tf_op jit(solution)/shard_map/all_gather | solution.py:156
  73.1 58.2 %all-to-all-start.3 = ((bf16[8,64,1408]{2,1,0:T(8,128)(2,1)}), bf16[8,64,1408]{2,1,0:T(8,128)(2,1)S(1)}, u32[]{:S(2)}, u32[]{:S(2)}) async-start(bf16[8,64,1408]{2,1,0:T(8,128)(2,1)} %copy.146), calls=%async_computation.3 | async-start | bytes 2883584 | tf_op jit(solution)/shard_map/all_to_all | solution.py:61
  131.2 15.2 %all-to-all-start.2 = ((bf16[4,2,80,4,128]{4,3,2,1,0:T(4,128)(2,1)}), bf16[4,2,80,4,128]{4,3,2,1,0:T(4,128)(2,1)S(1)}, u32[]{:S(2)}, u32[]{:S(2)}) async-start(bf16[4,2,80,4,128]{4,3,2,1,0:T(4,128)(2,1)} %pad_maximum_fusion.4), calls=%async_computation.2 | async-start | bytes 1310720 | tf_op jit(solution)/shard_map/all_to_all | solution.py:61
  134.9 140.3 %all-gather.25.cloned.1.call-start = ((), (), s32[]{:S(2)}) async-start(), calls=%async_computation.34 | async-start | bytes 7208960 | tf_op jit(solution)/shard_map/all_gather | solution.py:163
  137.0 196.4 %all-gather.23.cloned.1.call-start = ((), (), s32[]{:S(2)}) async-start(), calls=%async_computation.33 | async-start | bytes 5898240 | tf_op jit(solution)/shard_map/all_gather | solution.py:211
  222.8 293.8 %copy-start.2 = (f32[2,80,2048]{2,1,0:T(8,128)}, f32[2,80,2048]{2,1,0:T(8,128)S(1)}, u32[]{:S(2)}) copy-start(f32[2,80,2048]{2,1,0:T(8,128)S(1)} %get-tuple-element.398) | copy-start | bytes 3932164
  224.0 151.7 %all-gather.17.cloned.1.call-start = ((), (), s32[]{:S(2)}) async-start(), calls=%async_computation.23 | async-start | bytes 3604480 | tf_op jit(solution)/shard_map/all_gather | solution.py:164
  224.6 208.9 %all-gather.27.cloned.1.call-start = ((), (), s32[]{:S(2)}) async-start(), calls=%async_computation.35 | async-start | bytes 5898240 | tf_op jit(solution)/shard_map/all_gather | solution.py:165
  225.3 289.8 %reduce-scatter.10.cloned.1.call-start = ((), (), s32[]{:S(2)}) async-start(), calls=%async_computation.25 | async-start | bytes 5898240 | tf_op jit(solution)/shard_map/reduce_scatter | solution.py:222
  433.4 12.6 %copy-start.17 = (bf16[8,256,1408]{2,1,0:T(8,128)(2,1)S(1)}, bf16[8,256,1408]{2,1,0:T(8,128)(2,1)}, u32[]{:S(2)}) copy-start(bf16[8,256,1408]{2,1,0:T(8,128)(2,1)} %copy.148) | copy-start | bytes 17301508
  446.0 10.2 %copy-start.49 = (bf16[1280,704]{1,0:T(8,128)(2,1)}, bf16[1280,704]{1,0:T(8,128)(2,1)S(1)}, u32[]{:S(2)}) copy-start(bf16[1280,704]{1,0:T(8,128)(2,1)S(1)} %get-tuple-element.365) | copy-start | bytes 5406724
  446.0 10.2 %copy-start.50 = (bf16[1280,704]{1,0:T(8,128)(2,1)}, bf16[1280,704]{1,0:T(8,128)(2,1)S(1)}, u32[]{:S(2)}) copy-start(bf16[1280,704]{1,0:T(8,128)(2,1)S(1)} %get-tuple-element.366) | copy-start | bytes 5406724
  456.3 347.4 %reduce-scatter.18.cloned.1.call-start = ((), (), s32[]{:S(2)}) async-start(), calls=%async_computation.30 | async-start | bytes 7208960 | tf_op jit(solution)/shard_map/reduce_scatter | solution.py:245
  471.6 336.4 %reduce-scatter.20.cloned.1.call-start = ((), (), s32[]{:S(2)}) async-start(), calls=%async_computation.31 | async-start | bytes 3604480 | tf_op jit(solution)/shard_map/reduce_scatter | solution.py:252
  480.3 330.4 %all-gather.19.cloned.1.call-start = ((), (), s32[]{:S(2)}) async-start(), calls=%async_computation.26 | async-start | bytes 8650752 | tf_op jit(solution)/shard_map/all_gather | solution.py:357
  481.0 339.1 %reduce-scatter.8.cloned.1.call-start = ((), (), s32[]{:S(2)}) async-start(), calls=%async_computation.24 | async-start | bytes 5898240 | tf_op jit(solution)/shard_map/reduce_scatter | solution.py:226
  490.3 26.2 %copy-start.14 = (bf16[2,80,2048]{2,1,0:T(8,128)(2,1)S(1)}, bf16[2,80,2048]{2,1,0:T(8,128)(2,1)}, u32[]{:S(2)}) copy-start(bf16[2,80,2048]{2,1,0:T(8,128)(2,1)} %param.28) | copy-start | bytes 1966084
  518.0 6.6 copy-start.10
  679.5 42.4 %copy-start.13 = (bf16[2,80,2048]{2,1,0:T(8,128)(2,1)S(1)}, bf16[2,80,2048]{2,1,0:T(8,128)(2,1)}, u32[]{:S(2)}) copy-start(bf16[2,80,2048]{2,1,0:T(8,128)(2,1)} %copy-done.12) | copy-start | bytes 1966084
  723.9 35.4 %all-to-all-start.10 = ((bf16[4,2,80,2048]{3,2,1,0:T(8,128)(2,1)}), bf16[4,2,80,2048]{3,2,1,0:T(8,128)(2,1)}, u32[]{:S(2)}, u32[]{:S(2)}) async-start(bf16[4,2,80,2048]{3,2,1,0:T(8,128)(2,1)} %broadcast_in_dim.72), calls=%async_computation.14 | async-start | bytes 5242880 | tf_op jit(solution)/shard_map/all_to_all | solution.py:57
  728.6 34.0 %copy-start.11 = (bf16[2,80,2048]{2,1,0:T(8,128)(2,1)S(1)}, bf16[2,80,2048]{2,1,0:T(8,128)(2,1)}, u32[]{:S(2)}) copy-start(bf16[2,80,2048]{2,1,0:T(8,128)(2,1)} %copy-done.10) | copy-start | bytes 1966084
  728.9 42.9 %copy-start.5 = (bf16[4,2,80,2048]{3,2,1,0:T(8,128)(2,1)S(1)}, bf16[4,2,80,2048]{3,2,1,0:T(8,128)(2,1)}, u32[]{:S(2)}) copy-start(bf16[4,2,80,2048]{3,2,1,0:T(8,128)(2,1)} %copy-done.4) | copy-start | bytes 7864324
  759.3 8.3 all-to-all-start.8
  767.6 12.4 %all-to-all-start.11 = ((bf16[4,2,80,512]{3,2,1,0:T(8,128)(2,1)}), bf16[4,2,80,512]{3,2,1,0:T(8,128)(2,1)}, u32[]{:S(2)}, u32[]{:S(2)}) async-start(bf16[4,2,80,512]{3,2,1,0:T(8,128)(2,1)} %bitcast.274), calls=%async_computation.15 | async-start | bytes 1310720 | tf_op jit(solution)/shard_map/all_to_all | solution.py:61
  771.8 90.3 %reduce-scatter.14.cloned.1.call-start = ((), (), s32[]{:S(2)}) async-start(), calls=%async_computation.28 | async-start | bytes 589824 | tf_op jit(solution)/shard_map/reduce_scatter | solution.py:344
  773.5 98.5 %reduce-scatter.16.cloned.1.call-start = ((), (), s32[]{:S(2)}) async-start(), calls=%async_computation.29 | async-start | bytes 2359296 | tf_op jit(solution)/shard_map/reduce_scatter | solution.py:344
  785.1 118.4 %reduce-scatter.12.cloned.1.call-start = ((), (), s32[]{:S(2)}) async-start(), calls=%async_computation.27 | async-start | bytes 2359296 | tf_op jit(solution)/shard_map/reduce_scatter | solution.py:344
  787.1 13.3 %copy-start.6 = (bf16[4,2,80,2048]{3,2,1,0:T(8,128)(2,1)S(1)}, bf16[4,2,80,2048]{3,2,1,0:T(8,128)(2,1)}, u32[]{:S(2)}) copy-start(bf16[4,2,80,2048]{3,2,1,0:T(8,128)(2,1)} %copy-done.4) | copy-start | bytes 7864324
  803.7 51.1 %all-to-all-start.13 = ((bf16[8,64,1408]{2,1,0:T(8,128)(2,1)}), bf16[8,64,1408]{2,1,0:T(8,128)(2,1)}, u32[]{:S(2)}, u32[]{:S(2)}) async-start(bf16[8,64,1408]{2,1,0:T(8,128)(2,1)} %bitcast.282), calls=%async_computation.19 | async-start | bytes 2883584 | tf_op jit(solution)/shard_map/all_to_all | solution.py:61
  810.6 6.4 copy-start.9
  859.5 7.6 copy-start.47
  860.4 6.7 copy-start.18
  863.8 8.0 all-to-all-start.9
  867.1 8.8 copy-start.33
  867.1 8.8 copy-start.42
  871.9 40.8 %copy-start.26 = (bf16[64,2048]{1,0:T(8,128)(2,1)S(1)}, bf16[64,2048]{1,0:T(8,128)(2,1)}, u32[]{:S(2)}) copy-start(bf16[64,2048]{1,0:T(8,128)(2,1)} %param.20) | copy-start | bytes 786436
  872.0 9.2 %all-to-all-start.12 = ((bf16[4,64,512]{2,1,0:T(8,128)(2,1)}), bf16[4,64,512]{2,1,0:T(8,128)(2,1)S(1)}, u32[]{:S(2)}, u32[]{:S(2)}) async-start(bf16[4,64,512]{2,1,0:T(8,128)(2,1)} %bitcast.291), calls=%async_computation.17 | async-start | bytes 524288 | tf_op jit(solution)/shard_map/all_to_all | solution.py:61
  903.5 9.1 all-to-all-start.7
  (36 other events, 116.0 us)
Sparse Core Ops, SparseCore 0:
  22.3 38.0 all-gather.20
  69.1 58.1 all-gather.12
  130.2 78.2 all-gather.14
  210.8 64.4 all-gather.24
  277.3 56.0 all-gather.22
  335.1 40.5 all-gather.16
  377.3 56.0 all-gather.26
  456.4 58.6 reduce-scatter.9
  518.1 64.1 reduce-scatter.17
  585.2 41.7 reduce-scatter.19
  629.9 97.0 all-gather.18
  729.1 58.8 reduce-scatter.7
  790.9 30.0 reduce-scatter.13
  823.2 42.3 reduce-scatter.15
  867.8 35.5 reduce-scatter.11

commit v2 on v1

v2 whole, which is shorter than its diff:
```python
import functools
import math

import jax
import jax.numpy as jnp
from jax import lax
from jax.experimental import pallas as pl
from jax.experimental.pallas import tpu as pltpu
from jax.sharding import PartitionSpec as P

HQ = 16
HEAD_WIDTH = 128
LOG2E = math.log2(math.e)


norm_eps = 1e-05
theta_base = 10000.0


def rotate(values, cosine, sine):
    half = values.shape[-1] // 2
    first = values[..., :half]
    second = values[..., half:]
    return jnp.concatenate(
        [first * cosine - second * sine, second * cosine + first * sine], axis=-1
    )


def rotate_back(grads, cosine, sine):
    half = grads.shape[-1] // 2
    first = grads[..., :half]
    second = grads[..., half:]
    return jnp.concatenate(
        [first * cosine + second * sine, second * cosine - first * sine], axis=-1
    )


def document_info(places, lengths_row):
    starts = jnp.cumsum(lengths_row) - lengths_row
    inside = places[:, None] >= starts[None, :]
    documents = jnp.sum(inside.astype(jnp.int32), axis=1) - 1
    begins = jnp.max(jnp.where(inside, starts[None, :], 0), axis=1)
    return (documents, places - begins)


def angle_table(positions):
    half = HEAD_WIDTH // 2
    inverse_freq = jnp.exp(
        -math.log(theta_base) * (2.0 * jnp.arange(half, dtype=jnp.float32) / HEAD_WIDTH)
    )
    angles = positions.astype(jnp.float32)[..., None] * inverse_freq
    return (jnp.cos(angles), jnp.sin(angles))


low = jnp.bfloat16
wide = jnp.float32


def dot32(left, right, dims):
    return lax.dot_general(left, right, (dims, ((), ())), preferred_element_type=jnp.float32)


NN = ((1,), (0,))
NT = ((1,), (1,))
TN = ((0,), (0,))


def head_columns(ref, heads):
    return jnp.concatenate(
        [ref[:, h * HEAD_WIDTH : (h + 1) * HEAD_WIDTH] for h in range(heads)], axis=0
    )


def visible_bias(places, place, start):
    return jnp.where((places <= place) & (places >= start), 0.0, -1e30)


def attend_kernel(heads, q_ref, kv_ref, own_ref, keys_ref, att_ref, wide_ref, mass_ref, bias_ref):
    count = q_ref.shape[0]
    scale = HEAD_WIDTH**-0.5 * LOG2E

    @pl.when(pl.program_id(1) == 0)
    def _():
        bias_ref[...] = visible_bias(keys_ref[...], own_ref[:, 0:1], own_ref[:, 1:2])

    query = head_columns(q_ref, heads)
    keyval = kv_ref[...]
    scores = dot32(query, keyval[:, :HEAD_WIDTH], NT)
    bias = bias_ref[...]
    for h in range(heads):
        part = scores[h * count : (h + 1) * count] * scale + bias
        highest = jnp.max(part, axis=1, keepdims=True)
        weights = jnp.exp2(part - highest)
        mass = jnp.sum(weights, axis=1, keepdims=True)
        attended = dot32(weights.astype(low), keyval[:, HEAD_WIDTH:], NN) / mass
        columns = slice(h * HEAD_WIDTH, (h + 1) * HEAD_WIDTH)
        att_ref[:, columns] = attended.astype(low)
        wide_ref[:, columns] = attended
        mass_ref[:, columns] = jnp.broadcast_to(highest + jnp.log2(mass), (count, HEAD_WIDTH))


def heads_per_step(slots):
    return max(1, min(4, 4 * 2560 // slots))


def attend(query, keyval, own, keys):
    batches, count, width = query.shape
    slots, kv_width = keyval.shape[1:]
    heads = heads_per_step(slots)
    spec = pl.BlockSpec((None, count, heads * HEAD_WIDTH), lambda b, g: (b, 0, g))
    return pl.pallas_call(
        functools.partial(attend_kernel, heads),
        grid=(batches, HQ // heads),
        in_specs=[
            spec,
            pl.BlockSpec((None, slots, kv_width), lambda b, g: (b, 0, 0)),
            pl.BlockSpec((None, count, 2), lambda b, g: (b, 0, 0)),
            pl.BlockSpec((None, 1, slots), lambda b, g: (b, 0, 0)),
        ],
        out_specs=[spec, spec, spec],
        out_shape=[
            jax.ShapeDtypeStruct(query.shape, low),
            jax.ShapeDtypeStruct(query.shape, wide),
            jax.ShapeDtypeStruct(query.shape, wide),
        ],
        scratch_shapes=[pltpu.VMEM((count, slots), wide)],
        cost_estimate=pl.CostEstimate(
            flops=4 * batches * count * width * slots,
            transcendentals=batches * HQ * count * slots,
            bytes_accessed=16 * batches * count * width,
        ),
        compiler_params=pltpu.CompilerParams(vmem_limit_bytes=48 << 20),
    )(query, keyval, own, keys)


def attend_back_kernel(
    heads,
    chunk,
    q_ref,
    g_ref,
    wide_ref,
    mass_ref,
    kv_ref,
    own_ref,
    keys_ref,
    gq_ref,
    gkv_ref,
    bias_ref,
):
    count = q_ref.shape[0]
    slots = keys_ref.shape[0]
    rate = HEAD_WIDTH**-0.5
    scale = rate * LOG2E

    @pl.when(pl.program_id(1) == 0)
    def _():
        bias_ref[...] = visible_bias(keys_ref[...], own_ref[0:1], own_ref[1:2])
        gkv_ref[...] = jnp.zeros_like(gkv_ref)

    query = head_columns(q_ref, heads)
    grads = head_columns(g_ref, heads)
    mass = head_columns(mass_ref, heads)
    settle = jnp.sum(grads.astype(wide) * head_columns(wide_ref, heads), axis=1, keepdims=True)
    lane = lax.broadcasted_iota(jnp.int32, mass.shape, 1)
    stats = jnp.where(lane == 0, mass, settle).T
    mass_row = stats[0:1]
    settle_row = stats[1:2]
    keyval = kv_ref[...]
    grad_query = jnp.zeros((heads * count, HEAD_WIDTH), wide)
    for c in range(slots // chunk):
        span = slice(c * chunk, (c + 1) * chunk)
        key = keyval[span, :HEAD_WIDTH]
        value = keyval[span, HEAD_WIDTH:]
        weights = jnp.exp2(dot32(key, query, NT) * scale + bias_ref[span, :] - mass_row)
        slope = (weights * (dot32(value, grads, NT) - settle_row)).astype(low)
        gkv_ref[span, HEAD_WIDTH:] += dot32(weights.astype(low), grads, NN)
        gkv_ref[span, :HEAD_WIDTH] += dot32(slope, query, NN) * rate
        grad_query = grad_query + dot32(slope, key, TN)
    for h in range(heads):
        gq_ref[:, h * HEAD_WIDTH : (h + 1) * HEAD_WIDTH] = (
            grad_query[h * count : (h + 1) * count] * rate
        ).astype(low)


def attend_back(query, grads, att_wide, mass, keyval, own, keys):
    batches, count, width = query.shape
    slots, kv_width = keyval.shape[1:]
    heads = heads_per_step(slots)
    own = jnp.tile(own, (1, 1, heads))
    spec = pl.BlockSpec((None, count, heads * HEAD_WIDTH), lambda b, g: (b, 0, g))
    kv_spec = pl.BlockSpec((None, slots, kv_width), lambda b, g: (b, 0, 0))
    return pl.pallas_call(
        functools.partial(attend_back_kernel, heads, min(512, slots)),
        grid=(batches, HQ // heads),
        in_specs=[
            spec,
            spec,
            spec,
            spec,
            kv_spec,
            pl.BlockSpec((None, 2, heads * count), lambda b, g: (b, 0, 0)),
            pl.BlockSpec((None, slots, 1), lambda b, g: (b, 0, 0)),
        ],
        out_specs=[spec, kv_spec],
        out_shape=[
            jax.ShapeDtypeStruct(query.shape, low),
            jax.ShapeDtypeStruct(keyval.shape, wide),
        ],
        scratch_shapes=[pltpu.VMEM((slots, heads * count), wide)],
        cost_estimate=pl.CostEstimate(
            flops=10 * batches * count * width * slots,
            transcendentals=batches * HQ * count * slots,
            bytes_accessed=16 * batches * count * width,
        ),
        compiler_params=pltpu.CompilerParams(vmem_limit_bytes=48 << 20),
    )(query, grads, att_wide, mass, keyval, own, keys)


def together(*values):
    return lax.optimization_barrier(values)


def exchange(values, axis, offset):
    members = lax.axis_size(axis)
    return lax.ppermute(values, axis, [(i, i ^ offset) for i in range(members)])


def by_index(parts, place):
    bit = 1
    while bit < len(parts):
        flip = (place & bit) != 0
        parts = [jnp.where(flip, parts[i ^ bit], parts[i]) for i in range(len(parts))]
        bit *= 2
    return parts


def trade_au(parts):
    return [parts[0]] + [exchange(parts[k], "au", k) for k in range(1, len(parts))]


def gather_au(values):
    return trade_au([values] * lax.axis_size("au"))


def core_rows(values):
    core = lax.axis_index("row") % 2
    blocks = values.reshape((values.shape[0] // 2, 2) + values.shape[1:])
    return (
        lax.dynamic_index_in_dim(blocks, core, 1, False),
        lax.dynamic_index_in_dim(blocks, 1 - core, 1, False),
    )


def join_cores(here):
    other = exchange(here, "row", 1)
    first = lax.axis_index("row") % 2 == 0
    pairs = jnp.stack([jnp.where(first, here, other), jnp.where(first, other, here)], axis=1)
    return pairs.reshape((-1,) + here.shape[1:])


def join_rows(parts):
    return join_cores(jnp.stack(by_index(parts, lax.axis_index("row") // 2)))


def reduce_cores(blocks):
    mine, others = core_rows(blocks)
    return mine.astype(wide) + exchange(others.astype(low), "row", 1).astype(wide)


def reduce_chips(here):
    chip = lax.axis_index("row") // 2
    total = lax.dynamic_index_in_dim(here, chip, 0, False)
    here = here.astype(low)
    for k in range(1, here.shape[0]):
        part = lax.dynamic_index_in_dim(here, chip ^ k, 0, False)
        total = total + exchange(part, "row", 2 * k).astype(wide)
    return total


def on_device(
    tokens,
    permutation,
    lengths,
    w_query,
    w_keyval,
    w_out,
    w_gate,
    w_up,
    w_down,
    attn_gain,
    mlp_gain,
    out_grad,
    kv_partner,
):
    batches, local_rows, width = tokens.shape
    across = lax.axis_size("au")
    rows = lax.axis_size("row")
    slot_count = permutation.shape[1]
    q_width = w_query.shape[1]
    kv_width = w_keyval.shape[1]
    own_width = w_query.shape[0]
    ff = w_gate.shape[1]
    ff_here = ff // rows
    ff_own = w_down.shape[0]
    q_here = q_width // across
    row_index = lax.axis_index("row")
    au_index = lax.axis_index("au")
    group_rows = across * local_rows

    gain_one = attn_gain.astype(wide)[:, None]
    gain_two = mlp_gain.astype(wide)[:, None]
    query_scaled = (w_query.astype(wide) * gain_one).astype(low)
    keyval_scaled = (w_keyval.astype(wide) * gain_one).astype(low)
    gate_scaled = (w_gate.astype(wide) * gain_two).astype(low)
    up_scaled = (w_up.astype(wide) * gain_two).astype(low)

    inputs_wide = tokens.astype(wide)
    inverse_one = lax.rsqrt(jnp.mean(inputs_wide * inputs_wide, axis=-1, keepdims=True) + norm_eps)
    unit_one = inputs_wide * inverse_one
    unit_group = jnp.stack(gather_au(unit_one.astype(low)))

    out_rows = lax.all_gather(w_out, "row", axis=0)

    column_blocks = query_scaled.reshape(own_width, across, q_here).transpose(1, 0, 2)
    keyval_blocks = jnp.broadcast_to(keyval_scaled[None], (across, own_width, kv_width))
    column_blocks = lax.all_to_all(
        jnp.concatenate([column_blocks, keyval_blocks], axis=-1), "au", 0, 0
    )
    far_offsets = list(range(2, rows, 2))
    grad_parts = [out_grad] + [exchange(out_grad, "row", k) for k in far_offsets[:-1]]
    column_blocks, unit_group, *grad_parts = together(column_blocks, unit_group, *grad_parts)
    column_rows = lax.all_gather(column_blocks, "row", axis=0)
    columns = column_rows.reshape(width, q_here + kv_width)

    au_order = jnp.arange(across, dtype=jnp.int32) ^ au_index
    places = jnp.take(permutation.reshape(batches, rows, across, local_rows), au_order, axis=2)
    key_places = places.reshape(batches, slot_count)
    group_places = lax.dynamic_index_in_dim(places, row_index, 1, False)
    group_positions = jnp.stack(
        [
            document_info(group_places[b].reshape(-1), lengths[b])[1].reshape(across, local_rows)
            for b in range(batches)
        ],
        axis=1,
    )
    group_cosine, group_sine = angle_table(group_positions)
    own = jnp.stack([group_places[:, 0], group_places[:, 0] - group_positions[0]], axis=1)
    cosine = group_cosine[0]
    sine = group_sine[0]

    ff_blocks = jnp.concatenate(
        [gate_scaled.reshape(own_width, rows, ff_here), up_scaled.reshape(own_width, rows, ff_here)],
        axis=-1,
    ).transpose(1, 0, 2)
    columns, ff_blocks = together(columns, ff_blocks)
    projected = dot32(unit_group, columns, ((3,), (0,)))
    key_group = rotate(projected[..., q_here : q_here + HEAD_WIDTH], group_cosine, group_sine)
    keyval = jnp.concatenate([key_group, projected[..., q_here + HEAD_WIDTH :]], axis=-1)
    keyval = keyval.astype(low).transpose(1, 0, 2, 3).reshape(batches, group_rows, kv_width)
    query_group, keyval = together(projected[..., :q_here], keyval)
    keyval_gate = query_group
    keyval_all = lax.all_gather(keyval, "row", axis=1, tiled=True)
    ff_rows = lax.all_to_all(ff_blocks, "row", 0, 0)
    *out_parts, keyval_gate = together(*gather_au(core_rows(out_rows)[0]), keyval_gate)
    out_half = jnp.stack(by_index(out_parts, au_index), axis=1)
    out_full = join_cores(out_half).reshape(q_width, width)

    query_group = keyval_gate.reshape(
        across, batches, local_rows, q_here // HEAD_WIDTH, HEAD_WIDTH
    )
    query_group = rotate(query_group, group_cosine[:, :, :, None], group_sine[:, :, :, None])
    query_group = query_group.astype(low).reshape(across, batches, local_rows, q_here)
    query = jnp.concatenate(by_index(trade_au(list(query_group)), au_index), axis=-1)

    ff_parts = gather_au(ff_rows)
    grad_parts.append(exchange(grad_parts[0], "row", far_offsets[-1]))
    query, out_full, ff_rows, *grad_parts = together(query, out_full, ff_rows, *grad_parts)
    grad_rows = join_rows(grad_parts).reshape(-1, width)
    attended, att_wide, log_mass = attend(
        query, keyval_all, own.transpose(0, 2, 1), key_places[:, None, :]
    )
    ff_parts[0] = ff_rows
    attended, ff_parts[1], ff_parts[2] = together(attended, ff_parts[1], ff_parts[2])
    attended_kept, *ff_parts = together(attended, *ff_parts)
    ff_full = jnp.zeros((rows, across, own_width, 2 * ff_here), low)
    for k, part in enumerate(ff_parts):
        ff_full = lax.dynamic_update_index_in_dim(ff_full, part, au_index ^ k, 1)
    ff_full = ff_full.reshape(width, 2 * ff_here)
    down_full = jnp.zeros((across, ff_own, width), low)
    for k, part in enumerate(gather_au(w_down)):
        down_full = lax.dynamic_update_index_in_dim(down_full, part, au_index ^ k, 0)
    down_full = down_full.reshape(-1, width)

    hidden = inputs_wide + dot32(attended, out_full, ((2,), (0,)))
    inverse_two = lax.rsqrt(jnp.mean(hidden * hidden, axis=-1, keepdims=True) + norm_eps)
    unit_two = hidden * inverse_two
    unit_rows = lax.all_gather(unit_two.astype(low), "row", axis=0).reshape(-1, width)

    both = dot32(unit_rows, ff_full, NN)
    gate = both[:, :ff_here]
    up_part = both[:, ff_here:]
    sigmoid_gate = jax.nn.sigmoid(gate)
    inner = (gate * sigmoid_gate * up_part).astype(low)
    grad_inner = dot32(grad_rows, down_full, NT)
    grad_gate = grad_inner * up_part * sigmoid_gate * (1.0 + gate * (1.0 - sigmoid_gate))
    grad_up = grad_inner * gate * sigmoid_gate
    grad_both = jnp.concatenate([grad_gate.astype(low), grad_up.astype(low)], axis=1)
    scaled_two = dot32(grad_both, ff_full, NT).astype(low)
    attended_kept, query_columns, unit_rows = together(
        attended_kept, core_rows(column_rows[..., :q_here])[0], unit_rows
    )
    attended_group = jnp.stack(gather_au(attended_kept))
    scaled_two, attended_group = together(scaled_two, attended_group)
    scaled_two = lax.psum_scatter(
        scaled_two.reshape(rows, batches, local_rows, width), "row"
    ).astype(wide)

    both_term = dot32(unit_rows, grad_both, TN).astype(low)
    both_term = both_term.reshape(rows, across, own_width, 2 * ff_here)
    both_parts = [
        lax.dynamic_index_in_dim(both_term, au_index ^ k, 1, False) for k in range(across)
    ]
    both_parts = trade_au(both_parts)
    down_term = dot32(inner, grad_rows, TN).astype(low).reshape(across, ff_own, width)
    down_parts = [
        lax.dynamic_index_in_dim(down_term, au_index ^ k, 0, False) for k in range(across)
    ]
    down_parts = trade_au(down_parts)
    result_part = dot32(inner, down_full, NN).astype(low)
    result_part = result_part.reshape(rows, batches, local_rows, width)
    scaled_two, result_part, down_parts[0], query_columns, *both_parts = together(
        scaled_two, result_part, down_parts[0], query_columns, *both_parts
    )
    query_half = gather_au(query_columns)
    both_term = sum(part.astype(wide) for part in both_parts).astype(low)
    both_term = lax.all_to_all(both_term, "row", 0, 0)
    result_part = lax.psum_scatter(result_part, "row")

    grad_hidden = out_grad.astype(wide) + inverse_two * (
        scaled_two - unit_two * jnp.mean(scaled_two * unit_two, axis=-1, keepdims=True)
    )
    grad_branch = grad_hidden.astype(low)
    grad_att = dot32(grad_branch, out_full, ((2,), (1,))).astype(low)
    query_full = [join_cores(part).reshape(width, q_here) for part in query_half]

    def column_trade(values):
        size = values.shape[-1] // across
        parts = [values[..., i * size : (i + 1) * size] for i in range(across)]
        return jnp.stack(trade_au(by_index(parts, au_index)))

    def owner_columns(part, sizes):
        parts = by_index(trade_au(by_index(list(part), au_index)), au_index)
        ends = [sum(sizes[: i + 1]) for i in range(len(sizes))]
        return [
            jnp.concatenate([p[:, e - n : e] for p in parts], axis=-1).astype(wide)
            for n, e in zip(sizes, ends)
        ]

    group_dims = ((0, 1, 2), (0, 1, 2))
    branch_columns = column_trade(grad_branch)
    out_term = dot32(attended_group, branch_columns, group_dims).astype(low)
    out_term = reduce_chips(reduce_cores(out_term.reshape(rows, across, own_width, -1)))

    grad_query_heads, grad_keyval_term = attend_back(
        query, grad_att, att_wide, log_mass, keyval_all, own, key_places[:, :, None]
    )
    result_part, grad_query_heads, grad_keyval_term = together(
        result_part, grad_query_heads, grad_keyval_term
    )
    result = hidden + result_part.astype(wide)
    blocks = grad_keyval_term.reshape(batches, rows, across, local_rows, kv_width)
    here = reduce_cores(blocks.transpose(1, 0, 2, 3, 4))
    parts = [here[:, :, k] for k in range(across)]
    parts = trade_au([parts[0]] + [part.astype(low) for part in parts[1:]])
    grad_keyval_local = reduce_chips(sum(part.astype(wide) for part in parts))
    grad_keyval_local, out_term = together(grad_keyval_local, out_term)
    grad_keyval_local = (grad_keyval_local + kv_partner.astype(wide)).astype(low)
    grad_key_pre = rotate_back(grad_keyval_local[..., :HEAD_WIDTH].astype(wide), cosine, sine)
    grad_keyval_pre = jnp.concatenate(
        [grad_key_pre, grad_keyval_local[..., HEAD_WIDTH:].astype(wide)], axis=-1
    ).astype(low)
    grad_query_pre = rotate_back(
        grad_query_heads.reshape(batches, local_rows, HQ, HEAD_WIDTH).astype(wide),
        cosine[:, :, None],
        sine[:, :, None],
    )
    grad_query_pre = grad_query_pre.astype(low).reshape(batches, local_rows, q_width)

    query_term = dot32(unit_group, column_trade(grad_query_pre), group_dims).astype(low)
    query_term = lax.psum_scatter(query_term.reshape(rows, across, own_width, -1), "row")
    keyval_term = dot32(unit_group, column_trade(grad_keyval_pre), group_dims)
    keyval_term = reduce_chips(reduce_cores(keyval_term.reshape(rows, across, own_width, -1)))
    query_term, both_term = together(query_term, both_term)
    both_term = both_term.astype(wide)
    shard_out, query_term, keyval_term = owner_columns(
        jnp.concatenate([out_term.astype(low), query_term, keyval_term.astype(low)], axis=-1),
        [q_here, q_here, kv_width // across],
    )

    gate_term = both_term[..., :ff_here].transpose(1, 0, 2).reshape(own_width, ff)
    up_term = both_term[..., ff_here:].transpose(1, 0, 2).reshape(own_width, ff)
    shard_gain_two = jnp.sum(
        gate_term * w_gate.astype(wide) + up_term * w_up.astype(wide), axis=1
    )
    shard_gate = gate_term * gain_two
    shard_up = up_term * gain_two
    shard_down = sum(part.astype(wide) for part in down_parts)
    shard_gain_one = jnp.sum(query_term * w_query.astype(wide), axis=1) + jnp.sum(
        keyval_term * w_keyval.astype(wide), axis=1
    )
    shard_query = query_term * gain_one
    shard_keyval = keyval_term * gain_one

    scaled_one = dot32(grad_keyval_pre, columns[:, q_here:], ((2,), (1,)))
    grad_query_parts = by_index(
        [grad_query_pre[..., i * q_here : (i + 1) * q_here] for i in range(across)], au_index
    )
    for part, weight in zip(grad_query_parts, query_full):
        scaled_one = scaled_one + dot32(part, weight, ((2,), (1,)))
    grad_inputs = grad_hidden + inverse_one * (
        scaled_one - unit_one * jnp.mean(scaled_one * unit_one, axis=-1, keepdims=True)
    )
    return (
        result.astype(low),
        grad_inputs.astype(low),
        shard_query,
        shard_keyval,
        shard_out,
        shard_gate,
        shard_up,
        shard_down,
        shard_gain_one,
        shard_gain_two,
    )


def solution(mesh):
    return jax.shard_map(
        on_device,
        mesh=mesh,
        in_specs=(
            P(None, ("row", "au"), None),
            P(),
            P(),
            P(("row", "au"), None),
            P(("row", "au"), None),
            P(("row", "au"), None),
            P(("row", "au"), None),
            P(("row", "au"), None),
            P(("row", "au"), None),
            P(("row", "au")),
            P(("row", "au")),
            P(None, ("row", "au"), None),
            P(None, ("row", "au"), None),
        ),
        out_specs=(
            P(None, ("row", "au"), None),
            P(None, ("row", "au"), None),
            P(("row", "au"), None),
            P(("row", "au"), None),
            P(("row", "au"), None),
            P(("row", "au"), None),
            P(("row", "au"), None),
            P(("row", "au"), None),
            P(("row", "au")),
            P(("row", "au")),
        ),
        check_vma=False,
    )
```

time: 932 us -> 665 us (0.71)
  waiting for transfers between devices: 405 us -> 269 us
  matrix products: 217 us -> 84 us
  blocking collectives: 103 us -> 0 us
  starting transfers between devices: 40.3 us -> 87.5 us
  Pallas kernels: 0 us -> 42.8 us
  other arithmetic: 58 us -> 88 us
    ppermute x0 -> x63, waiting for transfers between devices: none -> 167 us  [exchange(): return lax.ppermute(values, axis, [(i, i ^ offset) for i in range(members)])]
    all_gather x6 -> x2, waiting for transfers between devices: 138 us -> 20.3 us  [the longest x1 20.3 us: on_device(): column_rows = lax.all_gather(column_blocks, 'row', axis=0)]
    dot_general x35 -> x0, matrix products: 116 us -> none  [the longest x5 23 us: key_block(): jnp.einsum('azol,atl->azot', grad_attended, incoming_values[..., HEAD_WID...]
    all_to_all x10 -> x3, waiting for transfers between devices: 165 us -> 54.9 us  [the longest x1 53.7 us: on_device(): ff_rows = lax.all_to_all(ff_blocks, 'row', 0, 0)]
    all_to_all x4 -> x0, blocking collectives: 103 us -> none  [swap(): return lax.all_to_all(blocks, axis, 0, 0)]
    ppermute x0 -> x63, starting transfers between devices: none -> 73.9 us  [exchange(): return lax.ppermute(values, axis, [(i, i ^ offset) for i in range(members)])]
    all_gather x1, waiting for transfers between devices: 52.3 us -> 0.01 us  [on_device(): lax.all_gather(unit_two.astype(low), 'row', axis=0).reshape(-1, width)]
    pallas_call x0 -> x2, Pallas kernels: none -> 42.8 us  [the longest x1 27.6 us: attend_back(): pl.pallas_call(functools.partial(attend_back_kernel, heads, min(512, slot...]
  transfers between devices with their start and end apart: 25 -> 73, of which waited for: 17 -> 30; matrix products, arithmetic and copies ran while one was open for 34% -> 33% of each run, Pallas kernels for 0% -> 7%
where the time goes in v2:
time: 665 us; the launch traced here: 656 us
  waiting for transfers between devices  269 us (40%)
  other arithmetic  88 us (13%)
  starting transfers between devices  87.5 us (13%)
  matrix products  84 us (13%)
  local copies, waits for them, and re-layouts  69.6 us (10%)
  Pallas kernels  42.8 us (6%)
  between operations  15.7 us (2%)
    ppermute x63, waiting for transfers between devices, exchange(): return lax.ppermute(values, axis, [(i, i ^ offset) for i in range(members)])  167 us
    dot_general x17, matrix products, dot32(): lax.dot_general(left, right, (dims, ((), ())), preferred_element_type=jnp...  84 us
    ppermute x63, starting transfers between devices, exchange(): return lax.ppermute(values, axis, [(i, i ^ offset) for i in range(members)])  73.9 us
    all_to_all x1, waiting for transfers between devices, on_device(): ff_rows = lax.all_to_all(ff_blocks, 'row', 0, 0)  53.7 us
    pallas_call x1, Pallas kernels, attend_back(): pl.pallas_call(functools.partial(attend_back_kernel, heads, min(512, slot...  27.6 us
    reduce_scatter x1, waiting for transfers between devices, on_device(): lax.psum_scatter(scaled_two.reshape(rows, batches, local_rows, width), 'r...  25.5 us
    another operation x12, other arithmetic, join_cores(): jnp.stack([jnp.where(first, here, other), jnp.where(first, other, here)],...  22.6 us
    all_gather x1, waiting for transfers between devices, on_device(): column_rows = lax.all_gather(column_blocks, 'row', axis=0)  20.3 us
  transfers between devices with their start and end apart: 73, of which 30 were waited for; matrix products, arithmetic and copies ran while one was open for 33% of the time, Pallas kernels for 7%

profile of v2, /device:TPU:0, one launch (start us, length us, event | category | flops | bytes accessed | tf_op | source)
XLA Modules:
  0.0 656.5 jit_solution(9020315101603103310)
XLA Ops:
  11.4 3.9 collective-permute-start.5
  22.0 4.1 all-to-all-start
  26.4 4.7 collective-permute-done.5
  31.1 14.2 %collective-permute-done.4 = bf16[2,80,2048]{2,1,0:T(8,128)(2,1)} collective-permute-done((bf16[2,80,2048]{2,1,0:T(8,128)(2,1)}, bf16[2,80,2048]{2,1,0:T(8,128)(2,1)}, u32[]{:S(2)}, u32[]{:S(2)}) %collective-permute-start.4) | collective-permute-done | bytes 655392 | tf_op jit(solution)/shard_map/ppermute | solution.py:225
  48.9 13.7 %collective-permute-done.6 = bf16[2,80,2048]{2,1,0:T(8,128)(2,1)} collective-permute-done((bf16[2,80,2048]{2,1,0:T(8,128)(2,1)S(1)}, bf16[2,80,2048]{2,1,0:T(8,128)(2,1)}, u32[]{:S(2)}, u32[]{:S(2)}) %collective-permute-start.6) | collective-permute-done | bytes 655392 | tf_op jit(solution)/shard_map/ppermute | solution.py:225
  74.8 2.9 maximum_bitcast_fusion
  83.5 20.3 %all-gather.12.cloned.1.call-done = bf16[32,64,768]{2,1,0:T(8,128)(2,1)} async-done(((bf16[4,64,768]{2,1,0:T(8,128)(2,1)}), bf16[32,64,768]{2,1,0:T(8,128)(2,1)}) %all-gather.12.cloned.1.call-update) | async-done | bytes 3145744 | tf_op jit(solution)/shard_map/all_gather | solution.py:332
  103.8 4.1 fusion.4
  112.2 12.5 %collective-permute-done.1 = bf16[4,64,2048]{2,1,0:T(8,128)(2,1)} collective-permute-done((bf16[4,64,2048]{2,1,0:T(8,128)(2,1)}, bf16[4,64,2048]{2,1,0:T(8,128)(2,1)}, u32[]{:S(2)}, u32[]{:S(2)}) %collective-permute-start.1) | collective-permute-done | bytes 1048608 | tf_op jit(solution)/shard_map/ppermute | solution.py:225
  132.9 4.7 all-to-all-start.1
  147.0 3.8 collective-permute-start.12
  151.1 2.9 collective-permute-done.9
  154.4 53.7 %all-to-all-done.1 = bf16[8,64,1408]{2,1,0:T(8,128)(2,1)} async-done(((bf16[8,64,1408]{2,1,0:T(8,128)(2,1)}), bf16[8,64,1408]{2,1,0:T(8,128)(2,1)}, u32[]{:S(2)}, u32[]{:S(2)}) %all-to-all-start.1) | async-done | bytes 1441824 | tf_op jit(solution)/shard_map/all_to_all | solution.py:363
  210.3 5.7 select_bitcast_fusion.1
  216.0 7.6 %pad_maximum_fusion = bf16[4,2,4,64,2048]{4,3,2,1,0:T(8,128)(2,1)} fusion(bf16[4,1,4,64,2048]{4,3,2,1,0:T(8,128)(2,1)} %get-tuple-element.138, bf16[4,1,4,64,2048]{4,3,2,1,0:T(8,128)(2,1)} %get-tuple-element.137), kind=kLoop, calls=%fused_computation.1 | loop fusion | flops 4194304 | bytes 16777216 | tf_op jit(solution)/shard_map/stack | solution.py:257
  223.7 15.1 %shard_map.204 = (bf16[2,80,2048]{2,1,0:T(8,128)(2,1)S(1)}, f32[2,80,2048]{2,1,0:T(8,128)S(1)}, f32[2,80,2048]{2,1,0:T(8,128)S(1)}) custom-call(bf16[2,80,2048]{2,1,0:T(8,128)(2,1)S(1)} %pad_maximum_fusion.13.q_ref, bf16[2,2560,256]{2,1,0:T(8,128)(2,1)} %all-gather.8.cloned.1.call-done.kv_ref, s32[2,80,2]{2,1,0:T(8,128)S(1)} %bitcast.354, ...), custom_call_target="tpu_custom_call" | custom-call | flops 3355443200 | bytes 5242880 | tf_op jit(solution)/shard_map/pallas_call | solution.py:111
  252.5 13.0 %collective-permute-done.16 = bf16[176,2048]{1,0:T(8,128)(2,1)} collective-permute-done((bf16[176,2048]{1,0:T(8,128)(2,1)}, bf16[176,2048]{1,0:T(8,128)(2,1)}, u32[]{:S(2)}, u32[]{:S(2)}) %collective-permute-start.16) | collective-permute-done | bytes 720928 | tf_op jit(solution)/shard_map/ppermute | solution.py:225
  267.5 26.1 %collective-permute-done.17 = bf16[176,2048]{1,0:T(8,128)(2,1)} collective-permute-done((bf16[176,2048]{1,0:T(8,128)(2,1)}, bf16[176,2048]{1,0:T(8,128)(2,1)}, u32[]{:S(2)}, u32[]{:S(2)}) %collective-permute-start.17) | collective-permute-done | bytes 720928 | tf_op jit(solution)/shard_map/ppermute | solution.py:225
  303.9 11.9 %collective-permute-done.19 = bf16[8,64,1408]{2,1,0:T(8,128)(2,1)S(1)} collective-permute-done((bf16[8,64,1408]{2,1,0:T(8,128)(2,1)}, bf16[8,64,1408]{2,1,0:T(8,128)(2,1)S(1)}, u32[]{:S(2)}, u32[]{:S(2)}) %collective-permute-start.19) | collective-permute-done | bytes 1441824 | tf_op jit(solution)/shard_map/ppermute | solution.py:225
  331.7 12.9 %fusion.96 = f32[1280,1408]{0,1:T(8,128)S(1)} fusion(bf16[1280,2048]{1,0:T(8,128)(2,1)} %bitcast.402, bf16[2048,1408]{1,0:T(8,128)(2,1)} %bitcast.365), kind=kOutput, calls=%fused_computation.316 | convolution fusion | flops 7381975040 | bytes 18219008 | tf_op jit(solution)/shard_map/dot_general | solution.py:60
  344.6 8.5 %multiply_convert_fusion.2 = (bf16[1280,704]{0,1:T(8,128)(2,1)S(1)}, bf16[1280,704]{0,1:T(8,128)(2,1)S(1)}, bf16[1280,704]{0,1:T(8,128)(2,1)}) fusion(f32[1280,1408]{0,1:T(8,128)S(1)} %fusion.96, bf16[1280,2048]{1,0:T(8,128)(2,1)S(1)} %bitcast.369, bf16[704,2048]{1,0:T(8,128)(2,1)} %bitcast.47), kind=kOutput, calls=%fused_computation.18 | convolution fusion | flops 3705405440 | bytes 20742144 | tf_op jit(solution)/shard_map/dot_general | solution.py:60
  353.2 13.4 %convolution_convert_fusion.2 = bf16[1280,2048]{1,0:T(8,128)(2,1)} fusion(bf16[2048,1408]{1,0:T(8,128)(2,1)} %bitcast.366, bf16[1280,704]{0,1:T(8,128)(2,1)S(1)} %get-tuple-element.136, bf16[1280,704]{0,1:T(8,128)(2,1)S(1)} %get-tuple-element.135), kind=kOutput, calls=%fused_computation.8 | convolution fusion | flops 7391805440 | bytes 14614528 | tf_op jit(solution)/shard_map/dot_general | solution.py:60
  368.4 11.4 %convolution_convert_fusion = bf16[2048,1408]{1,0:T(8,128)(2,1)S(1)} fusion(bf16[1280,2048]{1,0:T(8,128)(2,1)} %bitcast.403, bf16[1280,704]{0,1:T(8,128)(2,1)} %copy-done.51, bf16[1280,704]{0,1:T(8,128)(2,1)} %copy-done.50), kind=kOutput, calls=%fused_computation.6 | convolution fusion | flops 7392067584 | bytes 14614528 | tf_op jit(solution)/shard_map/dot_general | solution.py:60
  386.0 6.7 %convolution_convert_fusion.3 = bf16[704,2048]{1,0:T(8,128)(2,1)S(1)} fusion(bf16[1280,704]{0,1:T(8,128)(2,1)S(1)} %copy-done.49, bf16[1280,2048]{1,0:T(8,128)(2,1)} %bitcast.368), kind=kOutput, calls=%fused_computation.20 | convolution fusion | flops 3692429312 | bytes 9928704 | tf_op jit(solution)/shard_map/dot_general | solution.py:60
  394.4 7.8 %convolution_convert_fusion.1 = bf16[1280,2048]{1,0:T(8,128)(2,1)} fusion(bf16[1280,704]{0,1:T(8,128)(2,1)S(1)} %copy-done.49, bf16[704,2048]{1,0:T(8,128)(2,1)} %bitcast.47), kind=kOutput, calls=%fused_computation.7 | convolution fusion | flops 3693608960 | bytes 9928704 | tf_op jit(solution)/shard_map/dot_general | solution.py:60
  402.2 25.5 %reduce-scatter.4.cloned.1.call-done = bf16[1,2,80,2048]{3,2,1,0:T(8,128)(2,1)} async-done(((bf16[8,2,80,2048]{3,2,1,0:T(8,128)(2,1)}), bf16[1,2,80,2048]{3,2,1,0:T(8,128)(2,1)}) %reduce-scatter.4.cloned.1.call-update) | async-done | bytes 655376 | tf_op jit(solution)/shard_map/reduce_scatter | solution.py:414
  430.0 5.6 collective-permute-done.24
  435.6 2.8 gather.13
  438.5 4.3 broadcast_select_fusion.keys_ref
  454.4 4.1 add_convert_fusion
  458.5 2.9 fusion.9.g_ref
  461.4 4.3 all-to-all-start.2
  467.4 12.4 %collective-permute-done.34 = bf16[2,80,512]{2,1,0:T(8,128)(2,1)} collective-permute-done((bf16[2,80,512]{2,1,0:T(8,128)(2,1)}, bf16[2,80,512]{2,1,0:T(8,128)(2,1)}, u32[]{:S(2)}, u32[]{:S(2)}) %collective-permute-start.34) | collective-permute-done | bytes 163872 | tf_op jit(solution)/shard_map/ppermute | solution.py:225
  481.2 3.8 bitcast_convert_fusion.1
  486.3 27.6 %shard_map.205 = (bf16[2,80,2048]{2,1,0:T(8,128)(2,1)S(1)}, f32[2,2560,256]{2,1,0:T(8,128)}) custom-call(bf16[2,80,2048]{2,1,0:T(8,128)(2,1)S(1)} %pad_maximum_fusion.13.q_ref, bf16[2,80,2048]{2,1,0:T(8,128)(2,1)S(1)} %fusion.9.g_ref, f32[2,80,2048]{2,1,0:T(8,128)S(1)} %get-tuple-element.100.wide_ref, f32[2,80,2048]{2,1,0:T(8,128)S(1)} %copy-done.1, ...), custom_call_target="tpu_custom_call" | custom-call | flops 8388608000 | bytes 5242880 | tf_op jit(solution)/shard_map/pallas_call | solution.py:192
  515.6 2.9 convert_add_fusion.1
  519.0 2.9 collective-permute-start.39
  523.6 16.7 %collective-permute-done.45 = bf16[4,4,64,512]{3,2,1,0:T(8,128)(2,1)S(1)} collective-permute-done((bf16[4,4,64,512]{3,2,1,0:T(8,128)(2,1)S(1)}, bf16[4,4,64,512]{3,2,1,0:T(8,128)(2,1)S(1)}, u32[]{:S(2)}, u32[]{:S(2)}) %collective-permute-start.45) | collective-permute-done | bytes 1048608 | tf_op jit(solution)/shard_map/ppermute | solution.py:225
  542.4 4.1 collective-permute-done.38
  548.6 2.9 fusion.25
  568.7 5.4 collective-permute-done.29
  574.9 6.1 collective-permute-done.28
  587.6 3.2 bitcast_convert_fusion
  606.5 3.0 reshape_reshape.31
  610.8 3.4 fusion.23
  619.5 3.1 collective-permute-done.56
  622.6 4.5 collective-permute-done.55
  640.5 4.4 fusion.17
  (400 shorter events, 199.3 us)
Async XLA Ops:
  7.2 70.5 %all-gather.10.cloned.1.call-start = ((), (), s32[]{:S(2)}) async-start(), calls=%async_computation.10 | async-start | bytes 2359296 | tf_op jit(solution)/shard_map/all_gather | solution.py:322
  11.4 19.7 %collective-permute-start.5 = (bf16[2,80,2048]{2,1,0:T(8,128)(2,1)}, bf16[2,80,2048]{2,1,0:T(8,128)(2,1)S(1)}, u32[]{:S(2)}, u32[]{:S(2)}) collective-permute-start(bf16[2,80,2048]{2,1,0:T(8,128)(2,1)} %fusion.14), channel_id=1, source_target_pairs={{0,24},{8,16},{16,8},{24,0},{1,25},{9,17},{17,9},{25,1},{2,26},{10... | collective-permute-start | bytes 1966088 | tf_op jit(solution)/shard_map/ppermute | solution.py:225
  15.3 30.0 %collective-permute-start.4 = (bf16[2,80,2048]{2,1,0:T(8,128)(2,1)}, bf16[2,80,2048]{2,1,0:T(8,128)(2,1)}, u32[]{:S(2)}, u32[]{:S(2)}) collective-permute-start(bf16[2,80,2048]{2,1,0:T(8,128)(2,1)} %fusion.14), channel_id=1, source_target_pairs={{0,16},{8,24},{16,0},{24,8},{1,17},{9,25},{17,1},{25,9},{2,18},{10... | collective-permute-start | bytes 1966088 | tf_op jit(solution)/shard_map/ppermute | solution.py:225
  15.8 30.0 %collective-permute-start.3 = (bf16[2,80,2048]{2,1,0:T(8,128)(2,1)}, bf16[2,80,2048]{2,1,0:T(8,128)(2,1)}, u32[]{:S(2)}, u32[]{:S(2)}) collective-permute-start(bf16[2,80,2048]{2,1,0:T(8,128)(2,1)} %fusion.14), channel_id=1, source_target_pairs={{0,8},{8,0},{16,24},{24,16},{1,9},{9,1},{17,25},{25,17},{2,10},{10... | collective-permute-start | bytes 1966088 | tf_op jit(solution)/shard_map/ppermute | solution.py:225
  15.9 46.7 %collective-permute-start.6 = (bf16[2,80,2048]{2,1,0:T(8,128)(2,1)S(1)}, bf16[2,80,2048]{2,1,0:T(8,128)(2,1)}, u32[]{:S(2)}, u32[]{:S(2)}) collective-permute-start(bf16[2,80,2048]{2,1,0:T(8,128)(2,1)S(1)} %copy-done.21), channel_id=1, source_target_pairs={{0,2},{1,3},{2,0},{3,1},{4,6},{5,7},{6,4},{7,5},{8,10},{9,11},{10,... | collective-permute-start | bytes 1966088 | tf_op jit(solution)/shard_map/ppermute | solution.py:225
  17.9 47.3 %collective-permute-start.7 = (bf16[2,80,2048]{2,1,0:T(8,128)(2,1)S(1)}, bf16[2,80,2048]{2,1,0:T(8,128)(2,1)}, u32[]{:S(2)}, u32[]{:S(2)}) collective-permute-start(bf16[2,80,2048]{2,1,0:T(8,128)(2,1)S(1)} %copy-done.21), channel_id=1, source_target_pairs={{0,4},{1,5},{2,6},{3,7},{4,0},{5,1},{6,2},{7,3},{8,12},{9,13},{10,... | collective-permute-start | bytes 1966088 | tf_op jit(solution)/shard_map/ppermute | solution.py:225
  22.0 26.9 %all-to-all-start = ((bf16[4,64,768]{2,1,0:T(8,128)(2,1)}), bf16[4,64,768]{2,1,0:T(8,128)(2,1)}, u32[]{:S(2)}, u32[]{:S(2)}) async-start(bf16[4,64,768]{2,1,0:T(8,128)(2,1)} %copy.233), calls=%async_computation | async-start | bytes 786432 | tf_op jit(solution)/shard_map/all_to_all | solution.py:326
  26.1 77.7 %all-gather.12.cloned.1.call-start = ((), (), s32[]{:S(2)}) async-start(), calls=%async_computation.11 | async-start | bytes 3538944 | tf_op jit(solution)/shard_map/all_gather | solution.py:332
  65.2 158.4 %all-gather.8.cloned.1.call-start = ((), (), s32[]{:S(2)}) async-start(), calls=%async_computation.6 | async-start | bytes 2949120 | tf_op jit(solution)/shard_map/all_gather | solution.py:362
  80.0 32.2 %collective-permute-start = (bf16[4,64,2048]{2,1,0:T(8,128)(2,1)}, bf16[4,64,2048]{2,1,0:T(8,128)(2,1)}, u32[]{:S(2)}, u32[]{:S(2)}) collective-permute-start(bf16[4,64,2048]{2,1,0:T(8,128)(2,1)} %dynamic-slice_bitcast_fusion.6), channel_id=1, source_target_pairs={{0,8},{8,0},{16,24},{24,16},{1,9},{9,1},{17,25},{25,17},{2,10},{10... | collective-permute-start | bytes 3145736 | tf_op jit(solution)/shard_map/ppermute | solution.py:225
  81.5 43.2 %collective-permute-start.1 = (bf16[4,64,2048]{2,1,0:T(8,128)(2,1)}, bf16[4,64,2048]{2,1,0:T(8,128)(2,1)}, u32[]{:S(2)}, u32[]{:S(2)}) collective-permute-start(bf16[4,64,2048]{2,1,0:T(8,128)(2,1)} %dynamic-slice_bitcast_fusion.6), channel_id=1, source_target_pairs={{0,16},{8,24},{16,0},{24,8},{1,17},{9,25},{17,1},{25,9},{2,18},{10... | collective-permute-start | bytes 3145736 | tf_op jit(solution)/shard_map/ppermute | solution.py:225
  83.0 41.7 %collective-permute-start.2 = (bf16[4,64,2048]{2,1,0:T(8,128)(2,1)}, bf16[4,64,2048]{2,1,0:T(8,128)(2,1)}, u32[]{:S(2)}, u32[]{:S(2)}) collective-permute-start(bf16[4,64,2048]{2,1,0:T(8,128)(2,1)} %dynamic-slice_bitcast_fusion.6), channel_id=1, source_target_pairs={{0,24},{8,16},{16,8},{24,0},{1,25},{9,17},{17,9},{25,1},{2,26},{10... | collective-permute-start | bytes 3145736 | tf_op jit(solution)/shard_map/ppermute | solution.py:225
  130.2 80.1 %collective-permute-start.11 = (bf16[4,4,64,2048]{3,2,1,0:T(8,128)(2,1)}, bf16[4,4,64,2048]{3,2,1,0:T(8,128)(2,1)}, u32[]{:S(2)}, u32[]{:S(2)}) collective-permute-start(bf16[4,4,64,2048]{3,2,1,0:T(8,128)(2,1)} %pad_maximum_fusion.2), channel_id=1, source_target_pairs={{0,1},{1,0},{2,3},{3,2},{4,5},{5,4},{6,7},{7,6},{8,9},{9,8},{10,11... | collective-permute-start | bytes 12582920 | tf_op jit(solution)/shard_map/ppermute | solution.py:225
  132.9 75.2 %all-to-all-start.1 = ((bf16[8,64,1408]{2,1,0:T(8,128)(2,1)}), bf16[8,64,1408]{2,1,0:T(8,128)(2,1)}, u32[]{:S(2)}, u32[]{:S(2)}) async-start(bf16[8,64,1408]{2,1,0:T(8,128)(2,1)} %copy.242), calls=%async_computation.1 | async-start | bytes 2883584 | tf_op jit(solution)/shard_map/all_to_all | solution.py:363
  137.5 190.2 %all-gather.14.cloned.1.call-start = ((), (), s32[]{:S(2)}) async-start(), calls=%async_computation.12 | async-start | bytes 5898240 | tf_op jit(solution)/shard_map/all_gather | solution.py:397
  147.0 76.6 %collective-permute-start.12 = (bf16[2,80,2048]{2,1,0:T(8,128)(2,1)S(1)}, bf16[2,80,2048]{2,1,0:T(8,128)(2,1)}, u32[]{:S(2)}, u32[]{:S(2)}) collective-permute-start(bf16[2,80,2048]{2,1,0:T(8,128)(2,1)S(1)} %copy-done.21), channel_id=1, source_target_pairs={{0,6},{1,7},{2,4},{3,5},{4,2},{5,3},{6,0},{7,1},{8,14},{9,15},{10,... | collective-permute-start | bytes 1966088 | tf_op jit(solution)/shard_map/ppermute | solution.py:225
  208.1 33.4 %collective-permute-start.13 = (bf16[8,64,1408]{2,1,0:T(8,128)(2,1)}, bf16[8,64,1408]{2,1,0:T(8,128)(2,1)}, u32[]{:S(2)}, u32[]{:S(2)}) collective-permute-start(bf16[8,64,1408]{2,1,0:T(8,128)(2,1)} %all-to-all-done.1), channel_id=1, source_target_pairs={{0,8},{8,0},{16,24},{24,16},{1,9},{9,1},{17,25},{25,17},{2,10},{10... | collective-permute-start | bytes 4325384 | tf_op jit(solution)/shard_map/ppermute | solution.py:225
  209.4 32.8 %collective-permute-start.14 = (bf16[8,64,1408]{2,1,0:T(8,128)(2,1)}, bf16[8,64,1408]{2,1,0:T(8,128)(2,1)}, u32[]{:S(2)}, u32[]{:S(2)}) collective-permute-start(bf16[8,64,1408]{2,1,0:T(8,128)(2,1)} %all-to-all-done.1), channel_id=1, source_target_pairs={{0,16},{8,24},{16,0},{24,8},{1,17},{9,25},{17,1},{25,9},{2,18},{10... | collective-permute-start | bytes 4325384 | tf_op jit(solution)/shard_map/ppermute | solution.py:225
  246.0 181.7 %reduce-scatter.4.cloned.1.call-start = ((), (), s32[]{:S(2)}) async-start(), calls=%async_computation.7 | async-start | bytes 5898240 | tf_op jit(solution)/shard_map/reduce_scatter | solution.py:414
  246.0 19.5 %collective-permute-start.16 = (bf16[176,2048]{1,0:T(8,128)(2,1)}, bf16[176,2048]{1,0:T(8,128)(2,1)}, u32[]{:S(2)}, u32[]{:S(2)}) collective-permute-start(bf16[176,2048]{1,0:T(8,128)(2,1)} %param.21), channel_id=1, source_target_pairs={{0,8},{8,0},{16,24},{24,16},{1,9},{9,1},{17,25},{25,17},{2,10},{10... | collective-permute-start | bytes 2162696 | tf_op jit(solution)/shard_map/ppermute | solution.py:225
  247.0 46.6 %collective-permute-start.17 = (bf16[176,2048]{1,0:T(8,128)(2,1)}, bf16[176,2048]{1,0:T(8,128)(2,1)}, u32[]{:S(2)}, u32[]{:S(2)}) collective-permute-start(bf16[176,2048]{1,0:T(8,128)(2,1)} %param.21), channel_id=1, source_target_pairs={{0,16},{8,24},{16,0},{24,8},{1,17},{9,25},{17,1},{25,9},{2,18},{10... | collective-permute-start | bytes 2162696 | tf_op jit(solution)/shard_map/ppermute | solution.py:225
  248.6 51.7 %collective-permute-start.18 = (bf16[176,2048]{1,0:T(8,128)(2,1)}, bf16[176,2048]{1,0:T(8,128)(2,1)}, u32[]{:S(2)}, u32[]{:S(2)}) collective-permute-start(bf16[176,2048]{1,0:T(8,128)(2,1)} %param.21), channel_id=1, source_target_pairs={{0,24},{8,16},{16,8},{24,0},{1,25},{9,17},{17,9},{25,1},{2,26},{10... | collective-permute-start | bytes 2162696 | tf_op jit(solution)/shard_map/ppermute | solution.py:225
  295.7 20.1 %collective-permute-start.19 = (bf16[8,64,1408]{2,1,0:T(8,128)(2,1)}, bf16[8,64,1408]{2,1,0:T(8,128)(2,1)S(1)}, u32[]{:S(2)}, u32[]{:S(2)}) collective-permute-start(bf16[8,64,1408]{2,1,0:T(8,128)(2,1)} %all-to-all-done.1), channel_id=1, source_target_pairs={{0,24},{8,16},{16,8},{24,0},{1,25},{9,17},{17,9},{25,1},{2,26},{10... | collective-permute-start | bytes 4325384 | tf_op jit(solution)/shard_map/ppermute | solution.py:225
  300.3 23.6 %collective-permute-start.15 = (bf16[4,2,80,2048]{3,2,1,0:T(8,128)(2,1)S(1)}, bf16[4,2,80,2048]{3,2,1,0:T(8,128)(2,1)S(1)}, u32[]{:S(2)}, u32[]{:S(2)}) collective-permute-start(bf16[4,2,80,2048]{3,2,1,0:T(8,128)(2,1)S(1)} %pad_maximum_fusion.5), channel_id=1, source_target_pairs={{0,1},{1,0},{2,3},{3,2},{4,5},{5,4},{6,7},{7,6},{8,9},{9,8},{10,11... | collective-permute-start | bytes 7864328 | tf_op jit(solution)/shard_map/ppermute | solution.py:225
  327.8 38.8 %collective-permute-start.22 = (bf16[2,80,2048]{2,1,0:T(8,128)(2,1)S(1)}, bf16[2,80,2048]{2,1,0:T(8,128)(2,1)S(1)}, u32[]{:S(2)}, u32[]{:S(2)}) collective-permute-start(bf16[2,80,2048]{2,1,0:T(8,128)(2,1)S(1)} %get-tuple-element.94), channel_id=1, source_target_pairs={{0,24},{8,16},{16,8},{24,0},{1,25},{9,17},{17,9},{25,1},{2,26},{10... | collective-permute-start | bytes 1966088 | tf_op jit(solution)/shard_map/ppermute | solution.py:225
  330.2 36.3 %collective-permute-start.21 = (bf16[2,80,2048]{2,1,0:T(8,128)(2,1)S(1)}, bf16[2,80,2048]{2,1,0:T(8,128)(2,1)S(1)}, u32[]{:S(2)}, u32[]{:S(2)}) collective-permute-start(bf16[2,80,2048]{2,1,0:T(8,128)(2,1)S(1)} %get-tuple-element.94), channel_id=1, source_target_pairs={{0,16},{8,24},{16,0},{24,8},{1,17},{9,25},{17,1},{25,9},{2,18},{10... | collective-permute-start | bytes 1966088 | tf_op jit(solution)/shard_map/ppermute | solution.py:225
  330.2 36.3 %collective-permute-start.20 = (bf16[2,80,2048]{2,1,0:T(8,128)(2,1)S(1)}, bf16[2,80,2048]{2,1,0:T(8,128)(2,1)S(1)}, u32[]{:S(2)}, u32[]{:S(2)}) collective-permute-start(bf16[2,80,2048]{2,1,0:T(8,128)(2,1)S(1)} %get-tuple-element.94), channel_id=1, source_target_pairs={{0,8},{8,0},{16,24},{24,16},{1,9},{9,1},{17,25},{25,17},{2,10},{10... | collective-permute-start | bytes 1966088 | tf_op jit(solution)/shard_map/ppermute | solution.py:225
  368.4 180.2 %reduce-scatter.6.cloned.1.call-start = ((), (), s32[]{:S(2)}) async-start(), calls=%async_computation.8 | async-start | bytes 5898240 | tf_op jit(solution)/shard_map/reduce_scatter | solution.py:437
  382.5 47.4 %collective-permute-start.23 = (bf16[8,64,1408]{2,1,0:T(8,128)(2,1)}, bf16[8,64,1408]{2,1,0:T(8,128)(2,1)}, u32[]{:S(2)}, u32[]{:S(2)}) collective-permute-start(bf16[8,64,1408]{2,1,0:T(8,128)(2,1)} %get-tuple-element.142), channel_id=1, source_target_pairs={{0,8},{8,0},{16,24},{24,16},{1,9},{9,1},{17,25},{25,17},{2,10},{10... | collective-permute-start | bytes 4325384 | tf_op jit(solution)/shard_map/ppermute | solution.py:225
  383.1 52.5 %collective-permute-start.24 = (bf16[8,64,1408]{2,1,0:T(8,128)(2,1)}, bf16[8,64,1408]{2,1,0:T(8,128)(2,1)}, u32[]{:S(2)}, u32[]{:S(2)}) collective-permute-start(bf16[8,64,1408]{2,1,0:T(8,128)(2,1)} %get-tuple-element.141), channel_id=1, source_target_pairs={{0,16},{8,24},{16,0},{24,8},{1,17},{9,25},{17,1},{25,9},{2,18},{10... | collective-permute-start | bytes 4325384 | tf_op jit(solution)/shard_map/ppermute | solution.py:225
  385.1 50.4 %collective-permute-start.25 = (bf16[8,64,1408]{2,1,0:T(8,128)(2,1)}, bf16[8,64,1408]{2,1,0:T(8,128)(2,1)}, u32[]{:S(2)}, u32[]{:S(2)}) collective-permute-start(bf16[8,64,1408]{2,1,0:T(8,128)(2,1)} %get-tuple-element.140), channel_id=1, source_target_pairs={{0,24},{8,16},{16,8},{24,0},{1,25},{9,17},{17,9},{25,1},{2,26},{10... | collective-permute-start | bytes 4325384 | tf_op jit(solution)/shard_map/ppermute | solution.py:225
  446.0 39.1 %collective-permute-start.62 = (bf16[176,2048]{1,0:T(8,128)(2,1)}, bf16[176,2048]{1,0:T(8,128)(2,1)}, u32[]{:S(2)}, u32[]{:S(2)}) collective-permute-start(bf16[176,2048]{1,0:T(8,128)(2,1)} %get-tuple-element.151), channel_id=1, source_target_pairs={{0,24},{8,16},{16,8},{24,0},{1,25},{9,17},{17,9},{25,1},{2,26},{10... | collective-permute-start | bytes 2162696 | tf_op jit(solution)/shard_map/ppermute | solution.py:225
  447.1 39.0 %collective-permute-start.61 = (bf16[176,2048]{1,0:T(8,128)(2,1)}, bf16[176,2048]{1,0:T(8,128)(2,1)}, u32[]{:S(2)}, u32[]{:S(2)}) collective-permute-start(bf16[176,2048]{1,0:T(8,128)(2,1)} %get-tuple-element.152), channel_id=1, source_target_pairs={{0,16},{8,24},{16,0},{24,8},{1,17},{9,25},{17,1},{25,9},{2,18},{10... | collective-permute-start | bytes 2162696 | tf_op jit(solution)/shard_map/ppermute | solution.py:225
  452.0 27.7 %collective-permute-start.34 = (bf16[2,80,512]{2,1,0:T(8,128)(2,1)}, bf16[2,80,512]{2,1,0:T(8,128)(2,1)}, u32[]{:S(2)}, u32[]{:S(2)}) collective-permute-start(bf16[2,80,512]{2,1,0:T(8,128)(2,1)} %get-tuple-element.197), channel_id=1, source_target_pairs={{0,16},{8,24},{16,0},{24,8},{1,17},{9,25},{17,1},{25,9},{2,18},{10... | collective-permute-start | bytes 491528 | tf_op jit(solution)/shard_map/ppermute | solution.py:225
  453.9 25.9 %collective-permute-start.33 = (bf16[2,80,512]{2,1,0:T(8,128)(2,1)}, bf16[2,80,512]{2,1,0:T(8,128)(2,1)}, u32[]{:S(2)}, u32[]{:S(2)}) collective-permute-start(bf16[2,80,512]{2,1,0:T(8,128)(2,1)} %get-tuple-element.196), channel_id=1, source_target_pairs={{0,8},{8,0},{16,24},{24,16},{1,9},{9,1},{17,25},{25,17},{2,10},{10... | collective-permute-start | bytes 491528 | tf_op jit(solution)/shard_map/ppermute | solution.py:225
  461.4 165.7 %all-to-all-start.2 = ((bf16[8,64,1408]{2,1,0:T(8,128)(2,1)}), bf16[8,64,1408]{2,1,0:T(8,128)(2,1)}, u32[]{:S(2)}, u32[]{:S(2)}) async-start(bf16[8,64,1408]{2,1,0:T(8,128)(2,1)} %add_convert_fusion), calls=%async_computation.5 | async-start | bytes 2883584 | tf_op jit(solution)/shard_map/all_to_all | solution.py:436
  465.7 162.1 %reduce-scatter.8.cloned.1.call-start = ((), (), s32[]{:S(2)}) async-start(), calls=%async_computation.9 | async-start | bytes 2359296 | tf_op jit(solution)/shard_map/reduce_scatter | solution.py:490
  465.8 48.2 %collective-permute-start.60 = (bf16[176,2048]{1,0:T(8,128)(2,1)}, bf16[176,2048]{1,0:T(8,128)(2,1)S(1)}, u32[]{:S(2)}, u32[]{:S(2)}) collective-permute-start(bf16[176,2048]{1,0:T(8,128)(2,1)} %get-tuple-element.150), channel_id=1, source_target_pairs={{0,8},{8,0},{16,24},{24,16},{1,9},{9,1},{17,25},{25,17},{2,10},{10... | collective-permute-start | bytes 2162696 | tf_op jit(solution)/shard_map/ppermute | solution.py:225
  479.7 42.2 %collective-permute-start.40 = (bf16[4,4,64,512]{3,2,1,0:T(8,128)(2,1)}, bf16[4,4,64,512]{3,2,1,0:T(8,128)(2,1)S(1)}, u32[]{:S(2)}, u32[]{:S(2)}) collective-permute-start(bf16[4,4,64,512]{3,2,1,0:T(8,128)(2,1)} %dynamic-slice_bitcast_fusion.5), channel_id=1, source_target_pairs={{0,1},{1,0},{2,3},{3,2},{4,5},{5,4},{6,7},{7,6},{8,9},{9,8},{10,11... | collective-permute-start | bytes 3145736 | tf_op jit(solution)/shard_map/ppermute | solution.py:225
  479.8 38.7 %collective-permute-start.41 = (bf16[4,4,64,512]{3,2,1,0:T(8,128)(2,1)}, bf16[4,4,64,512]{3,2,1,0:T(8,128)(2,1)S(1)}, u32[]{:S(2)}, u32[]{:S(2)}) collective-permute-start(bf16[4,4,64,512]{3,2,1,0:T(8,128)(2,1)} %dynamic-slice_bitcast_fusion.5), channel_id=1, source_target_pairs={{0,8},{8,0},{16,24},{24,16},{1,9},{9,1},{17,25},{25,17},{2,10},{10... | collective-permute-start | bytes 3145736 | tf_op jit(solution)/shard_map/ppermute | solution.py:225
  485.1 37.8 %collective-permute-start.43 = (bf16[4,4,64,512]{3,2,1,0:T(8,128)(2,1)S(1)}, bf16[4,4,64,512]{3,2,1,0:T(8,128)(2,1)}, u32[]{:S(2)}, u32[]{:S(2)}) collective-permute-start(bf16[4,4,64,512]{3,2,1,0:T(8,128)(2,1)S(1)} %copy-done.26), channel_id=1, source_target_pairs={{0,16},{8,24},{16,0},{24,8},{1,17},{9,25},{17,1},{25,9},{2,18},{10... | collective-permute-start | bytes 3145736 | tf_op jit(solution)/shard_map/ppermute | solution.py:225
  486.1 32.4 %collective-permute-start.36 = (bf16[4,4,64,512]{3,2,1,0:T(8,128)(2,1)S(1)}, bf16[4,4,64,512]{3,2,1,0:T(8,128)(2,1)S(1)}, u32[]{:S(2)}, u32[]{:S(2)}) collective-permute-start(bf16[4,4,64,512]{3,2,1,0:T(8,128)(2,1)S(1)} %dynamic-slice_bitcast_fusion.4), channel_id=1, source_target_pairs={{0,1},{1,0},{2,3},{3,2},{4,5},{5,4},{6,7},{7,6},{8,9},{9,8},{10,11... | collective-permute-start | bytes 3145736 | tf_op jit(solution)/shard_map/ppermute | solution.py:225
  514.0 26.3 %collective-permute-start.45 = (bf16[4,4,64,512]{3,2,1,0:T(8,128)(2,1)S(1)}, bf16[4,4,64,512]{3,2,1,0:T(8,128)(2,1)S(1)}, u32[]{:S(2)}, u32[]{:S(2)}) collective-permute-start(bf16[4,4,64,512]{3,2,1,0:T(8,128)(2,1)S(1)} %copy-done.26), channel_id=1, source_target_pairs={{0,24},{8,16},{16,8},{24,0},{1,25},{9,17},{17,9},{25,1},{2,26},{10... | collective-permute-start | bytes 3145736 | tf_op jit(solution)/shard_map/ppermute | solution.py:225
  518.5 28.1 %collective-permute-start.42 = (bf16[4,4,64,512]{3,2,1,0:T(8,128)(2,1)S(1)}, bf16[4,4,64,512]{3,2,1,0:T(8,128)(2,1)S(1)}, u32[]{:S(2)}, u32[]{:S(2)}) collective-permute-start(bf16[4,4,64,512]{3,2,1,0:T(8,128)(2,1)S(1)} %collective-permute-done.41), channel_id=1, source_target_pairs={{0,1},{1,0},{2,3},{3,2},{4,5},{5,4},{6,7},{7,6},{8,9},{9,8},{10,11... | collective-permute-start | bytes 3145736 | tf_op jit(solution)/shard_map/ppermute | solution.py:225
  519.0 22.8 %collective-permute-start.39 = (bf16[4,64,512]{2,1,0:T(8,128)(2,1)S(1)}, bf16[4,64,512]{2,1,0:T(8,128)(2,1)S(1)}, u32[]{:S(2)}, u32[]{:S(2)}) collective-permute-start(bf16[4,64,512]{2,1,0:T(8,128)(2,1)S(1)} %get-tuple-element.187), channel_id=1, source_target_pairs={{0,6},{1,7},{2,4},{3,5},{4,2},{5,3},{6,0},{7,1},{8,14},{9,15},{10,... | collective-permute-start | bytes 786440 | tf_op jit(solution)/shard_map/ppermute | solution.py:225
  521.9 24.5 %collective-permute-start.38 = (bf16[4,64,512]{2,1,0:T(8,128)(2,1)S(1)}, bf16[4,64,512]{2,1,0:T(8,128)(2,1)S(1)}, u32[]{:S(2)}, u32[]{:S(2)}) collective-permute-start(bf16[4,64,512]{2,1,0:T(8,128)(2,1)S(1)} %get-tuple-element.188), channel_id=1, source_target_pairs={{0,4},{1,5},{2,6},{3,7},{4,0},{5,1},{6,2},{7,3},{8,12},{9,13},{10,... | collective-permute-start | bytes 786440 | tf_op jit(solution)/shard_map/ppermute | solution.py:225
  522.9 23.5 %collective-permute-start.37 = (bf16[4,64,512]{2,1,0:T(8,128)(2,1)S(1)}, bf16[4,64,512]{2,1,0:T(8,128)(2,1)S(1)}, u32[]{:S(2)}, u32[]{:S(2)}) collective-permute-start(bf16[4,64,512]{2,1,0:T(8,128)(2,1)S(1)} %get-tuple-element.186), channel_id=1, source_target_pairs={{0,2},{1,3},{2,0},{3,1},{4,6},{5,7},{6,4},{7,5},{8,10},{9,11},{10,... | collective-permute-start | bytes 786440 | tf_op jit(solution)/shard_map/ppermute | solution.py:225
  568.1 19.5 %collective-permute-start.48 = (bf16[2,80,512]{2,1,0:T(8,128)(2,1)S(1)}, bf16[2,80,512]{2,1,0:T(8,128)(2,1)S(1)}, u32[]{:S(2)}, u32[]{:S(2)}) collective-permute-start(bf16[2,80,512]{2,1,0:T(8,128)(2,1)S(1)} %broadcast_select_fusion.22), channel_id=1, source_target_pairs={{0,16},{8,24},{16,0},{24,8},{1,17},{9,25},{17,1},{25,9},{2,18},{10... | collective-permute-start | bytes 491528 | tf_op jit(solution)/shard_map/ppermute | solution.py:225
  (79 other events, 718.1 us)
Sparse Core Ops, SparseCore 0:
  9.7 50.6 all-gather.9
  65.4 38.3 all-gather.11
  130.4 74.1 all-gather.7
  246.1 54.6 all-gather.13
  368.5 59.1 reduce-scatter.3
  435.7 79.0 reduce-scatter.5
  590.9 36.8 reduce-scatter.7

commit v3 on v2

--- a/solution.py
+++ b/solution.py
@@ -182,35 +182,37 @@
         ).astype(low)
 
 
-def attend_back(query, grads, att_wide, mass, keyval, own, keys):
+def attend_back(query, grads, att_wide, mass, keyval, own, keys, batch):
     batches, count, width = query.shape
     slots, kv_width = keyval.shape[1:]
     heads = heads_per_step(slots)
     own = jnp.tile(own, (1, 1, heads))
-    spec = pl.BlockSpec((None, count, heads * HEAD_WIDTH), lambda b, g: (b, 0, g))
-    kv_spec = pl.BlockSpec((None, slots, kv_width), lambda b, g: (b, 0, 0))
+    spec = pl.BlockSpec((None, count, heads * HEAD_WIDTH), lambda b, g: (batch, 0, g))
     return pl.pallas_call(
         functools.partial(attend_back_kernel, heads, min(512, slots)),
-        grid=(batches, HQ // heads),
+        grid=(1, HQ // heads),
         in_specs=[
             spec,
             spec,
             spec,
             spec,
-            kv_spec,
-            pl.BlockSpec((None, 2, heads * count), lambda b, g: (b, 0, 0)),
-            pl.BlockSpec((None, slots, 1), lambda b, g: (b, 0, 0)),
+            pl.BlockSpec((None, slots, kv_width), lambda b, g: (batch, 0, 0)),
+            pl.BlockSpec((None, 2, heads * count), lambda b, g: (batch, 0, 0)),
+            pl.BlockSpec((None, slots, 1), lambda b, g: (batch, 0, 0)),
         ],
-        out_specs=[spec, kv_spec],
+        out_specs=[
+            pl.BlockSpec((None, count, heads * HEAD_WIDTH), lambda b, g: (b, 0, g)),
+            pl.BlockSpec((None, slots, kv_width), lambda b, g: (b, 0, 0)),
+        ],
         out_shape=[
-            jax.ShapeDtypeStruct(query.shape, low),
-            jax.ShapeDtypeStruct(keyval.shape, wide),
+            jax.ShapeDtypeStruct((1, count, width), low),
+            jax.ShapeDtypeStruct((1, slots, kv_width), wide),
         ],
         scratch_shapes=[pltpu.VMEM((slots, heads * count), wide)],
         cost_estimate=pl.CostEstimate(
-            flops=10 * batches * count * width * slots,
-            transcendentals=batches * HQ * count * slots,
-            bytes_accessed=16 * batches * count * width,
+            flops=10 * count * width * slots,
+            transcendentals=HQ * count * slots,
+            bytes_accessed=16 * count * width,
         ),
         compiler_params=pltpu.CompilerParams(vmem_limit_bytes=48 << 20),
     )(query, grads, att_wide, mass, keyval, own, keys)
@@ -242,6 +244,39 @@
     return trade_au([values] * lax.axis_size("au"))
 
 
+def bits_of(members):
+    return [1 << i for i in range(members.bit_length() - 1)]
+
+
+def reduce_send(held, bit):
+    keys = [k for k in sorted(held) if k & bit]
+    return exchange(jnp.stack([held[k] for k in keys]).astype(low), "au", bit)
+
+
+def reduce_add(held, bit, got):
+    keys = [k for k in sorted(held) if k & bit]
+    return {
+        k ^ bit: held[k ^ bit].astype(wide) + got[i].astype(wide) for i, k in enumerate(keys)
+    }
+
+
+def reduce_au_first(lists):
+    bits = bits_of(lax.axis_size("au"))
+    return [reduce_send(dict(enumerate(lists[i])), bits[i % len(bits)]) for i in range(2)]
+
+
+def reduce_au_rest(lists, got):
+    bits = bits_of(lax.axis_size("au"))
+    done = []
+    for i in range(2):
+        held = reduce_add(dict(enumerate(lists[i])), bits[i % len(bits)], got[i])
+        for j in range(1, len(bits)):
+            bit = bits[(i + j) % len(bits)]
+            held = reduce_add(held, bit, reduce_send(held, bit))
+        done.append(held[0])
+    return done
+
+
 def core_rows(values):
     core = lax.axis_index("row") % 2
     blocks = values.reshape((values.shape[0] // 2, 2) + values.shape[1:])
@@ -251,15 +286,16 @@
     )
 
 
-def join_cores(here):
-    other = exchange(here, "row", 1)
+def by_core(values):
+    rows = lax.axis_size("row")
+    blocks = values.reshape(values.shape[:-1] + (rows // 2, 2, values.shape[-1] // rows))
     first = lax.axis_index("row") % 2 == 0
-    pairs = jnp.stack([jnp.where(first, here, other), jnp.where(first, other, here)], axis=1)
-    return pairs.reshape((-1,) + here.shape[1:])
-
-
-def join_rows(parts):
-    return join_cores(jnp.stack(by_index(parts, lax.axis_index("row") // 2)))
+    low_rows, high_rows = blocks[..., 0, :], blocks[..., 1, :]
+    flat = values.shape[:-1] + (values.shape[-1] // 2,)
+    return (
+        jnp.where(first, low_rows, high_rows).reshape(flat),
+        jnp.where(first, high_rows, low_rows).reshape(flat),
+    )
 
 
 def reduce_cores(blocks):
@@ -326,9 +362,13 @@
     column_blocks = lax.all_to_all(
         jnp.concatenate([column_blocks, keyval_blocks], axis=-1), "au", 0, 0
     )
-    far_offsets = list(range(2, rows, 2))
-    grad_parts = [out_grad] + [exchange(out_grad, "row", k) for k in far_offsets[:-1]]
-    column_blocks, unit_group, *grad_parts = together(column_blocks, unit_group, *grad_parts)
+    ff_blocks = jnp.concatenate(
+        [gate_scaled.reshape(own_width, rows, ff_here), up_scaled.reshape(own_width, rows, ff_here)],
+        axis=-1,
+    ).transpose(1, 0, 2)
+    column_blocks, unit_group, out_rows, ff_blocks = together(
+        column_blocks, unit_group, out_rows, ff_blocks
+    )
     column_rows = lax.all_gather(column_blocks, "row", axis=0)
     columns = column_rows.reshape(width, q_here + kv_width)
 
@@ -348,53 +388,81 @@
     cosine = group_cosine[0]
     sine = group_sine[0]
 
-    ff_blocks = jnp.concatenate(
-        [gate_scaled.reshape(own_width, rows, ff_here), up_scaled.reshape(own_width, rows, ff_here)],
-        axis=-1,
-    ).transpose(1, 0, 2)
-    columns, ff_blocks = together(columns, ff_blocks)
+    out_parts = gather_au(core_rows(out_rows)[0])
+    columns, ff_blocks, out_parts[1] = together(columns, ff_blocks, out_parts[1])
+    ff_rows = lax.all_to_all(ff_blocks, "row", 0, 0)
     projected = dot32(unit_group, columns, ((3,), (0,)))
     key_group = rotate(projected[..., q_here : q_here + HEAD_WIDTH], group_cosine, group_sine)
     keyval = jnp.concatenate([key_group, projected[..., q_here + HEAD_WIDTH :]], axis=-1)
     keyval = keyval.astype(low).transpose(1, 0, 2, 3).reshape(batches, group_rows, kv_width)
-    query_group, keyval = together(projected[..., :q_here], keyval)
-    keyval_gate = query_group
+    query_group, keyval, w_down, *out_parts = together(
+        projected[..., :q_here], keyval, w_down, *out_parts
+    )
+    down_parts = gather_au(w_down)
     keyval_all = lax.all_gather(keyval, "row", axis=1, tiled=True)
-    ff_rows = lax.all_to_all(ff_blocks, "row", 0, 0)
-    *out_parts, keyval_gate = together(*gather_au(core_rows(out_rows)[0]), keyval_gate)
-    out_half = jnp.stack(by_index(out_parts, au_index), axis=1)
-    out_full = join_cores(out_half).reshape(q_width, width)
-
-    query_group = keyval_gate.reshape(
+    query_group = query_group.reshape(
         across, batches, local_rows, q_here // HEAD_WIDTH, HEAD_WIDTH
     )
     query_group = rotate(query_group, group_cosine[:, :, :, None], group_sine[:, :, :, None])
     query_group = query_group.astype(low).reshape(across, batches, local_rows, q_here)
     query = jnp.concatenate(by_index(trade_au(list(query_group)), au_index), axis=-1)
 
+    out_half = jnp.zeros((rows // 2, across, own_width, width), low)
+    for k, part in enumerate(out_parts):
+        out_half = lax.dynamic_update_index_in_dim(out_half, part, au_index ^ k, 1)
+    out_half = out_half.reshape(-1, width)
+    out_other = exchange(out_half, "row", 1)
+
+    down_full = jnp.zeros((across, ff_own, width), low)
+    for k, part in enumerate(down_parts):
+        down_full = lax.dynamic_update_index_in_dim(down_full, part, au_index ^ k, 0)
+    down_full = down_full.reshape(-1, width)
+
+    key_columns = key_places[:, :, None]
+    (
+        grads_own,
+        keyval_all,
+        ff_rows,
+        query,
+        out_other,
+        down_full,
+        key_columns,
+    ) = together(out_grad, keyval_all, ff_rows, query, out_other, down_full, key_columns)
+    grad_rows = lax.all_gather(grads_own, "row", axis=0).reshape(-1, width)
     ff_parts = gather_au(ff_rows)
-    grad_parts.append(exchange(grad_parts[0], "row", far_offsets[-1]))
-    query, out_full, ff_rows, *grad_parts = together(query, out_full, ff_rows, *grad_parts)
-    grad_rows = join_rows(grad_parts).reshape(-1, width)
     attended, att_wide, log_mass = attend(
         query, keyval_all, own.transpose(0, 2, 1), key_places[:, None, :]
     )
     ff_parts[0] = ff_rows
     attended, ff_parts[1], ff_parts[2] = together(attended, ff_parts[1], ff_parts[2])
-    attended_kept, *ff_parts = together(attended, *ff_parts)
+    attended_kept = attended
     ff_full = jnp.zeros((rows, across, own_width, 2 * ff_here), low)
     for k, part in enumerate(ff_parts):
         ff_full = lax.dynamic_update_index_in_dim(ff_full, part, au_index ^ k, 1)
     ff_full = ff_full.reshape(width, 2 * ff_here)
-    down_full = jnp.zeros((across, ff_own, width), low)
-    for k, part in enumerate(gather_au(w_down)):
-        down_full = lax.dynamic_update_index_in_dim(down_full, part, au_index ^ k, 0)
-    down_full = down_full.reshape(-1, width)
-
-    hidden = inputs_wide + dot32(attended, out_full, ((2,), (0,)))
+    attended_mine, attended_other = by_core(attended)
+    hidden = inputs_wide + (
+        dot32(attended_mine, out_half, ((2,), (0,))) + dot32(attended_other, out_other, ((2,), (0,)))
+    )
     inverse_two = lax.rsqrt(jnp.mean(hidden * hidden, axis=-1, keepdims=True) + norm_eps)
     unit_two = hidden * inverse_two
-    unit_rows = lax.all_gather(unit_two.astype(low), "row", axis=0).reshape(-1, width)
+    unit_low, attended_kept, query_columns = together(
+        unit_two.astype(low), attended_kept, core_rows(column_rows[..., :q_here])[0]
+    )
+    unit_low, grad_rows = together(unit_low, grad_rows)
+    unit_rows = lax.all_gather(unit_low, "row", axis=0).reshape(-1, width)
+    attended_group = jnp.stack(gather_au(attended_kept))
+    query_half = gather_au(query_columns)
+    pair = lax.dynamic_update_index_in_dim(
+        jnp.zeros((rows // 2, 2) + (across * own_width, width), low),
+        out_half.reshape(rows // 2, -1, width),
+        row_index % 2,
+        1,
+    )
+    out_full = lax.dynamic_update_index_in_dim(
+        pair, out_other.reshape(rows // 2, -1, width), 1 - row_index % 2, 1
+    ).reshape(q_width, width)
+    unit_rows, out_full = together(unit_rows, out_full)
 
     both = dot32(unit_rows, ff_full, NN)
     gate = both[:, :ff_here]
@@ -406,11 +474,7 @@
     grad_up = grad_inner * gate * sigmoid_gate
     grad_both = jnp.concatenate([grad_gate.astype(low), grad_up.astype(low)], axis=1)
     scaled_two = dot32(grad_both, ff_full, NT).astype(low)
-    attended_kept, query_columns, unit_rows = together(
-        attended_kept, core_rows(column_rows[..., :q_here])[0], unit_rows
-    )
-    attended_group = jnp.stack(gather_au(attended_kept))
-    scaled_two, attended_group = together(scaled_two, attended_group)
+    scaled_two, attended_group, *query_half = together(scaled_two, attended_group, *query_half)
     scaled_two = lax.psum_scatter(
         scaled_two.reshape(rows, batches, local_rows, width), "row"
     ).astype(wide)
@@ -420,20 +484,29 @@
     both_parts = [
         lax.dynamic_index_in_dim(both_term, au_index ^ k, 1, False) for k in range(across)
     ]
-    both_parts = trade_au(both_parts)
+    half_rows = own_width // 2
+    both_lists = [
+        [part[:, i * half_rows : (i + 1) * half_rows] for part in both_parts] for i in range(2)
+    ]
+    both_first = reduce_au_first(both_lists)
     down_term = dot32(inner, grad_rows, TN).astype(low).reshape(across, ff_own, width)
     down_parts = [
         lax.dynamic_index_in_dim(down_term, au_index ^ k, 0, False) for k in range(across)
     ]
-    down_parts = trade_au(down_parts)
     result_part = dot32(inner, down_full, NN).astype(low)
     result_part = result_part.reshape(rows, batches, local_rows, width)
-    scaled_two, result_part, down_parts[0], query_columns, *both_parts = together(
-        scaled_two, result_part, down_parts[0], query_columns, *both_parts
-    )
-    query_half = gather_au(query_columns)
-    both_term = sum(part.astype(wide) for part in both_parts).astype(low)
-    both_term = lax.all_to_all(both_term, "row", 0, 0)
+    query_half = jnp.stack(query_half).reshape(across, rows // 2, -1, q_here)
+    query_other = exchange(query_half, "row", 1)
+    pair = lax.dynamic_update_index_in_dim(
+        jnp.zeros((across, rows // 2, 2) + query_half.shape[2:], low), query_half, row_index % 2, 2
+    )
+    query_full = lax.dynamic_update_index_in_dim(pair, query_other, 1 - row_index % 2, 2)
+    query_full = query_full.reshape(across, width, q_here)
+    scaled_two, result_part, down_parts, both_first, query_full = together(
+        scaled_two, result_part, down_parts, both_first, query_full
+    )
+    both_term = jnp.concatenate(reduce_au_rest(both_lists, both_first), axis=1).astype(low)
+    down_parts = trade_au(down_parts)
     result_part = lax.psum_scatter(result_part, "row")
 
     grad_hidden = out_grad.astype(wide) + inverse_two * (
@@ -441,7 +514,6 @@
     )
     grad_branch = grad_hidden.astype(low)
     grad_att = dot32(grad_branch, out_full, ((2,), (1,))).astype(low)
-    query_full = [join_cores(part).reshape(width, q_here) for part in query_half]
 
     def column_trade(values):
         size = values.shape[-1] // across
@@ -458,65 +530,84 @@
 
     group_dims = ((0, 1, 2), (0, 1, 2))
     branch_columns = column_trade(grad_branch)
-    out_term = dot32(attended_group, branch_columns, group_dims).astype(low)
-    out_term = reduce_chips(reduce_cores(out_term.reshape(rows, across, own_width, -1)))
-
-    grad_query_heads, grad_keyval_term = attend_back(
-        query, grad_att, att_wide, log_mass, keyval_all, own, key_places[:, :, None]
-    )
-    result_part, grad_query_heads, grad_keyval_term = together(
-        result_part, grad_query_heads, grad_keyval_term
-    )
+    grad_query_heads = []
+    grad_keyval_term = []
+    for b in range(batches):
+        grad_query_b, grad_keyval_b = attend_back(
+            query, grad_att, att_wide, log_mass, keyval_all, own, key_columns, b
+        )
+        blocks = grad_keyval_b.reshape(rows, across, local_rows, kv_width)
+        mine, others = core_rows(blocks)
+        others = exchange(others.astype(low), "row", 1)
+        if b == 0:
+            grad_query_b, branch_columns, grad_att, both_term = together(
+                grad_query_b, branch_columns, grad_att, both_term
+            )
+            both_term = lax.all_to_all(both_term, "row", 0, 0)
+            out_term = dot32(attended_group, branch_columns, group_dims).astype(low)
+            grad_att, out_term = together(grad_att, out_term)
+            out_term = lax.psum_scatter(out_term.reshape(rows, across, own_width, -1), "row")
+        grad_query_heads.append(grad_query_b)
+        grad_keyval_term.append(mine + others.astype(wide))
+    grad_query_heads = jnp.concatenate(grad_query_heads)
+    here = jnp.stack(grad_keyval_term, axis=1)
+    grad_query_heads, down_parts[1] = together(grad_query_heads, down_parts[1])
+
+    grad_query_pre = rotate_back(
+        grad_query_heads.reshape(batches, local_rows, HQ, HEAD_WIDTH).astype(wide),
+        cosine[:, :, None],
+        sine[:, :, None],
+    )
+    grad_query_pre = grad_query_pre.astype(low).reshape(batches, local_rows, q_width)
+    query_term = dot32(unit_group, column_trade(grad_query_pre), group_dims).astype(low)
+    query_term, result_part = together(query_term, result_part)
     result = hidden + result_part.astype(wide)
-    blocks = grad_keyval_term.reshape(batches, rows, across, local_rows, kv_width)
-    here = reduce_cores(blocks.transpose(1, 0, 2, 3, 4))
+
     parts = [here[:, :, k] for k in range(across)]
     parts = trade_au([parts[0]] + [part.astype(low) for part in parts[1:]])
     grad_keyval_local = reduce_chips(sum(part.astype(wide) for part in parts))
-    grad_keyval_local, out_term = together(grad_keyval_local, out_term)
+    grad_keyval_local, both_term = together(grad_keyval_local, both_term)
     grad_keyval_local = (grad_keyval_local + kv_partner.astype(wide)).astype(low)
     grad_key_pre = rotate_back(grad_keyval_local[..., :HEAD_WIDTH].astype(wide), cosine, sine)
     grad_keyval_pre = jnp.concatenate(
         [grad_key_pre, grad_keyval_local[..., HEAD_WIDTH:].astype(wide)], axis=-1
     ).astype(low)
-    grad_query_pre = rotate_back(
-        grad_query_heads.reshape(batches, local_rows, HQ, HEAD_WIDTH).astype(wide),
-        cosine[:, :, None],
-        sine[:, :, None],
-    )
-    grad_query_pre = grad_query_pre.astype(low).reshape(batches, local_rows, q_width)
-
-    query_term = dot32(unit_group, column_trade(grad_query_pre), group_dims).astype(low)
     query_term = lax.psum_scatter(query_term.reshape(rows, across, own_width, -1), "row")
-    keyval_term = dot32(unit_group, column_trade(grad_keyval_pre), group_dims)
-    keyval_term = reduce_chips(reduce_cores(keyval_term.reshape(rows, across, own_width, -1)))
-    query_term, both_term = together(query_term, both_term)
+    keyval_term = dot32(unit_one.astype(low), grad_keyval_pre, ((0, 1), (0, 1))).astype(low)
+    keyval_term = keyval_term.reshape(rows, across, own_width, kv_width)
+    parts = [
+        lax.dynamic_index_in_dim(keyval_term, au_index ^ k, 1, False) for k in range(across)
+    ]
+    keyval_term = sum(part.astype(wide) for part in trade_au(parts))
+    keyval_term = reduce_chips(reduce_cores(keyval_term))
     both_term = both_term.astype(wide)
-    shard_out, query_term, keyval_term = owner_columns(
-        jnp.concatenate([out_term.astype(low), query_term, keyval_term.astype(low)], axis=-1),
-        [q_here, q_here, kv_width // across],
+    shard_out, query_term = owner_columns(
+        jnp.concatenate([out_term, query_term], axis=-1), [q_here, q_here]
     )
 
     gate_term = both_term[..., :ff_here].transpose(1, 0, 2).reshape(own_width, ff)
     up_term = both_term[..., ff_here:].transpose(1, 0, 2).reshape(own_width, ff)
+    shard_down = sum(part.astype(wide) for part in down_parts)
     shard_gain_two = jnp.sum(
         gate_term * w_gate.astype(wide) + up_term * w_up.astype(wide), axis=1
     )
     shard_gate = gate_term * gain_two
     shard_up = up_term * gain_two
-    shard_down = sum(part.astype(wide) for part in down_parts)
     shard_gain_one = jnp.sum(query_term * w_query.astype(wide), axis=1) + jnp.sum(
         keyval_term * w_keyval.astype(wide), axis=1
     )
     shard_query = query_term * gain_one
     shard_keyval = keyval_term * gain_one
 
-    scaled_one = dot32(grad_keyval_pre, columns[:, q_here:], ((2,), (1,)))
-    grad_query_parts = by_index(
-        [grad_query_pre[..., i * q_here : (i + 1) * q_here] for i in range(across)], au_index
-    )
-    for part, weight in zip(grad_query_parts, query_full):
-        scaled_one = scaled_one + dot32(part, weight, ((2,), (1,)))
+    grad_query_parts = jnp.stack(
+        by_index(
+            [grad_query_pre[..., i * q_here : (i + 1) * q_here] for i in range(across)], au_index
+        )
+    )
+    grad_query_parts, grad_keyval_pre = together(grad_query_parts, grad_keyval_pre)
+    scaled_one = dot32(grad_keyval_pre, columns[:, q_here:], ((2,), (1,))) + dot32(
+        grad_query_parts, query_full, ((0, 3), (0, 2))
+    )
     grad_inputs = grad_hidden + inverse_one * (
         scaled_one - unit_one * jnp.mean(scaled_one * unit_one, axis=-1, keepdims=True)
     )

time: 665 us -> 594 us (0.89)
  waiting for transfers between devices: 269 us -> 210 us
  other arithmetic: 88 us -> 65.4 us
  local copies, waits for them, and re-layouts: 69.6 us -> 79.5 us
  starting transfers between devices: 87.5 us -> 79 us
    all_to_all x1, waiting for transfers between devices: 53.7 us -> 0.01 us  [on_device(): ff_rows = lax.all_to_all(ff_blocks, 'row', 0, 0)]
    another operation x21 -> x13, other arithmetic: 35.5 us -> 15.8 us  [the longest x12 22.6 us: join_cores(): jnp.stack([jnp.where(first, here, other), jnp.where(first, other, here)],...]
    dynamic_update_slice x0 -> x7, local copies, waits for them, and re-layouts: none -> 15 us  [the longest x4 6.82 us: on_device(): out_half = lax.dynamic_update_index_in_dim(out_half, part, au_index ^ k, 1)]
    ppermute x63 -> x54, waiting for transfers between devices: 167 us -> 180 us  [exchange(): return lax.ppermute(values, axis, [(i, i ^ offset) for i in range(members)])]
    reduce_scatter x1, waiting for transfers between devices: 25.5 us -> 12.6 us  [on_device(): lax.psum_scatter(scaled_two.reshape(rows, batches, local_rows, width), 'r...]
    all_gather x1, waiting for transfers between devices: 20.3 us -> 11.1 us  [on_device(): column_rows = lax.all_gather(column_blocks, 'row', axis=0)]
    ppermute x63 -> x54, starting transfers between devices: 73.9 us -> 65.1 us  [exchange(): return lax.ppermute(values, axis, [(i, i ^ offset) for i in range(members)])]
    broadcast_in_dim x0 -> x3, local copies, waits for them, and re-layouts: none -> 7.88 us  [the longest x1 4.27 us: on_device(): jnp.zeros((across, rows // 2, 2) + query_half.shape[2:], low)]
  transfers between devices with their start and end apart: 73 -> 66, of which waited for: 30 -> 26; matrix products, arithmetic and copies ran while one was open for 33% -> 38% of each run, Pallas kernels for 7% -> 8%
where the time goes in v3:
time: 594 us; the launch traced here: 585 us
  waiting for transfers between devices  210 us (35%)
  matrix products  89.9 us (15%)
  local copies, waits for them, and re-layouts  79.5 us (13%)
  starting transfers between devices  79 us (13%)
  other arithmetic  65.4 us (11%)
  Pallas kernels  45.7 us (8%)
  between operations  15.4 us (3%)
    ppermute x54, waiting for transfers between devices, exchange(): return lax.ppermute(values, axis, [(i, i ^ offset) for i in range(members)])  180 us
    dot_general x15, matrix products, dot32(): lax.dot_general(left, right, (dims, ((), ())), preferred_element_type=jnp...  89.9 us
    ppermute x54, starting transfers between devices, exchange(): return lax.ppermute(values, axis, [(i, i ^ offset) for i in range(members)])  65.1 us
    pallas_call x2, Pallas kernels, attend_back(): pl.pallas_call(functools.partial(attend_back_kernel, heads, min(512, slot...  30.7 us
    pallas_call x1, Pallas kernels, attend(): pl.pallas_call(functools.partial(attend_kernel, heads), grid=(batches, HQ...  14.9 us
    reduce_scatter x1, waiting for transfers between devices, on_device(): lax.psum_scatter(scaled_two.reshape(rows, batches, local_rows, width), 'r...  12.6 us
  transfers between devices with their start and end apart: 66, of which 26 were waited for; matrix products, arithmetic and copies ran while one was open for 38% of the time, Pallas kernels for 8%

profile of v3, /device:TPU:0, one launch (start us, length us, event | category | flops | bytes accessed | tf_op | source)
XLA Modules:
  0.0 585.0 jit_solution(10589010769378588590)
XLA Ops:
  11.4 3.9 collective-permute-start.2
  17.3 4.2 all-to-all-start
  25.1 6.0 %collective-permute-done.2 = bf16[2,80,2048]{2,1,0:T(8,128)(2,1)} collective-permute-done((bf16[2,80,2048]{2,1,0:T(8,128)(2,1)}, bf16[2,80,2048]{2,1,0:T(8,128)(2,1)}, u32[]{:S(2)}, u32[]{:S(2)}) %collective-permute-start.2) | collective-permute-done | bytes 655392 | tf_op jit(solution)/shard_map/ppermute | solution.py:227
  31.2 14.1 %collective-permute-done.1 = bf16[2,80,2048]{2,1,0:T(8,128)(2,1)} collective-permute-done((bf16[2,80,2048]{2,1,0:T(8,128)(2,1)}, bf16[2,80,2048]{2,1,0:T(8,128)(2,1)}, u32[]{:S(2)}, u32[]{:S(2)}) %collective-permute-start.1) | collective-permute-done | bytes 655392 | tf_op jit(solution)/shard_map/ppermute | solution.py:227
  45.8 3.3 pad_maximum_fusion.3
  55.8 21.6 %collective-permute-done.3 = bf16[4,64,2048]{2,1,0:T(8,128)(2,1)S(1)} collective-permute-done((bf16[4,64,2048]{2,1,0:T(8,128)(2,1)S(1)}, bf16[4,64,2048]{2,1,0:T(8,128)(2,1)S(1)}, u32[]{:S(2)}, u32[]{:S(2)}) %collective-permute-start.3) | collective-permute-done | bytes 1048608 | tf_op jit(solution)/shard_map/ppermute | solution.py:227
  77.4 11.1 %all-gather.14.cloned.1.call-done = bf16[32,64,768]{2,1,0:T(8,128)(2,1)} async-done(((bf16[4,64,768]{2,1,0:T(8,128)(2,1)}), bf16[32,64,768]{2,1,0:T(8,128)(2,1)}) %all-gather.14.cloned.1.call-update) | async-done | bytes 3145744 | tf_op jit(solution)/shard_map/all_gather | solution.py:372
  88.5 4.9 fusion.6
  96.5 3.4 collective-permute-done.4
  114.5 5.1 all-to-all-start.1
  136.5 13.8 %collective-permute-done.10 = bf16[176,2048]{1,0:T(8,128)(2,1)S(1)} collective-permute-done((bf16[176,2048]{1,0:T(8,128)(2,1)}, bf16[176,2048]{1,0:T(8,128)(2,1)S(1)}, u32[]{:S(2)}, u32[]{:S(2)}) %collective-permute-start.10) | collective-permute-done | bytes 720928 | tf_op jit(solution)/shard_map/ppermute | solution.py:227
  151.1 14.8 %collective-permute-done.11 = bf16[176,2048]{1,0:T(8,128)(2,1)S(1)} collective-permute-done((bf16[176,2048]{1,0:T(8,128)(2,1)}, bf16[176,2048]{1,0:T(8,128)(2,1)S(1)}, u32[]{:S(2)}, u32[]{:S(2)}) %collective-permute-start.11) | collective-permute-done | bytes 720928 | tf_op jit(solution)/shard_map/ppermute | solution.py:227
  172.6 14.9 %shard_map.204 = (bf16[2,80,2048]{2,1,0:T(8,128)(2,1)S(1)}, f32[2,80,2048]{2,1,0:T(8,128)S(1)}, f32[2,80,2048]{2,1,0:T(8,128)S(1)}) custom-call(bf16[2,80,2048]{2,1,0:T(8,128)(2,1)S(1)} %pad_maximum_fusion.12.q_ref, bf16[2,2560,256]{2,1,0:T(8,128)(2,1)} %all-gather.10.cloned.1.call-done.kv_ref, s32[2,80,2]{2,1,0:T(8,128)S(1)} %bitcast.386, ...), custom_call_target="tpu_custom_call" | custom-call | flops 3355443200 | bytes 5242880 | tf_op jit(solution)/shard_map/pallas_call | solution.py:111
  188.7 11.4 %collective-permute-done.13 = bf16[8,64,1408]{2,1,0:T(8,128)(2,1)} collective-permute-done((bf16[8,64,1408]{2,1,0:T(8,128)(2,1)}, bf16[8,64,1408]{2,1,0:T(8,128)(2,1)}, u32[]{:S(2)}, u32[]{:S(2)}) %collective-permute-start.13) | collective-permute-done | bytes 1441824 | tf_op jit(solution)/shard_map/ppermute | solution.py:227
  210.1 3.2 fusion.99
  213.3 3.3 multiply_reduce_fusion.1
  218.7 5.5 all-gather.16.cloned.1.call-done
  225.5 2.8 bitcast_dynamic-update-slice_fusion.1
  233.1 3.1 constant_dynamic-update-slice_fusion
  243.6 20.4 %collective-permute-done.15 = bf16[8,64,1408]{2,1,0:T(8,128)(2,1)S(1)} collective-permute-done((bf16[8,64,1408]{2,1,0:T(8,128)(2,1)}, bf16[8,64,1408]{2,1,0:T(8,128)(2,1)S(1)}, u32[]{:S(2)}, u32[]{:S(2)}) %collective-permute-start.15) | collective-permute-done | bytes 1441824 | tf_op jit(solution)/shard_map/ppermute | solution.py:227
  265.7 12.3 %collective-permute-done.18 = bf16[2,80,2048]{2,1,0:T(8,128)(2,1)S(1)} collective-permute-done((bf16[2,80,2048]{2,1,0:T(8,128)(2,1)S(1)}, bf16[2,80,2048]{2,1,0:T(8,128)(2,1)S(1)}, u32[]{:S(2)}, u32[]{:S(2)}) %collective-permute-start.18) | collective-permute-done | bytes 655392 | tf_op jit(solution)/shard_map/ppermute | solution.py:227
  280.3 11.0 %collective-permute-done.17 = bf16[2,80,2048]{2,1,0:T(8,128)(2,1)S(1)} collective-permute-done((bf16[2,80,2048]{2,1,0:T(8,128)(2,1)S(1)}, bf16[2,80,2048]{2,1,0:T(8,128)(2,1)S(1)}, u32[]{:S(2)}, u32[]{:S(2)}) %collective-permute-start.17) | collective-permute-done | bytes 655392 | tf_op jit(solution)/shard_map/ppermute | solution.py:227
  293.8 11.9 %fusion.100 = f32[1280,1408]{0,1:T(8,128)S(1)} fusion(bf16[1280,2048]{1,0:T(8,128)(2,1)} %bitcast.437, bf16[2048,1408]{1,0:T(8,128)(2,1)} %bitcast.390), kind=kOutput, calls=%fused_computation.297 | convolution fusion | flops 7381975040 | bytes 18219008 | tf_op jit(solution)/shard_map/dot_general | solution.py:60
  305.7 10.0 %multiply_convert_fusion.2 = (bf16[1280,704]{0,1:T(8,128)(2,1)S(1)}, bf16[1280,704]{0,1:T(8,128)(2,1)S(1)}, bf16[1280,704]{0,1:T(8,128)(2,1)}) fusion(f32[1280,1408]{0,1:T(8,128)S(1)} %fusion.100, bf16[1280,2048]{1,0:T(8,128)(2,1)} %bitcast.433, bf16[704,2048]{1,0:T(8,128)(2,1)} %bitcast.32), kind=kOutput, calls=%fused_computation.19 | convolution fusion | flops 3705405440 | bytes 20742144 | tf_op jit(solution)/shard_map/dot_general | solution.py:60
  315.7 10.2 %convolution_convert_fusion.2 = bf16[1280,2048]{1,0:T(8,128)(2,1)} fusion(bf16[2048,1408]{1,0:T(8,128)(2,1)S(1)} %bitcast.391, bf16[1280,704]{0,1:T(8,128)(2,1)S(1)} %get-tuple-element.154, bf16[1280,704]{0,1:T(8,128)(2,1)S(1)} %get-tuple-element.153), kind=kOutput, calls=%fused_computation.7 | convolution fusion | flops 7391805440 | bytes 14614528 | tf_op jit(solution)/shard_map/dot_general | solution.py:60
  325.9 10.4 %collective-permute-done.21 = bf16[4,4,64,512]{3,2,1,0:T(8,128)(2,1)} collective-permute-done((bf16[4,4,64,512]{3,2,1,0:T(8,128)(2,1)}, bf16[4,4,64,512]{3,2,1,0:T(8,128)(2,1)}, u32[]{:S(2)}, u32[]{:S(2)}) %collective-permute-start.21) | collective-permute-done | bytes 1048608 | tf_op jit(solution)/shard_map/ppermute | solution.py:227
  339.9 10.7 %convolution_convert_fusion = bf16[2048,1408]{1,0:T(8,128)(2,1)S(1)} fusion(bf16[1280,2048]{1,0:T(8,128)(2,1)} %bitcast.438, bf16[1280,704]{0,1:T(8,128)(2,1)S(1)} %copy-done.52, bf16[1280,704]{0,1:T(8,128)(2,1)S(1)} %copy-done.50), kind=kOutput, calls=%fused_computation.5 | convolution fusion | flops 7392067584 | bytes 14614528 | tf_op jit(solution)/shard_map/dot_general | solution.py:60
  358.5 8.0 %convolution_convert_fusion.1 = bf16[1280,2048]{1,0:T(8,128)(2,1)} fusion(bf16[1280,704]{0,1:T(8,128)(2,1)S(1)} %copy-done.48, bf16[704,2048]{1,0:T(8,128)(2,1)} %bitcast.32), kind=kOutput, calls=%fused_computation.6 | convolution fusion | flops 3693608960 | bytes 9928704 | tf_op jit(solution)/shard_map/dot_general | solution.py:60
  366.5 4.1 convolution_convert_fusion.3
  372.3 4.3 broadcast_in_dim.150
  376.6 3.8 maximum_dynamic-update-slice_fusion
  382.6 12.6 %reduce-scatter.5.cloned.1.call-done = bf16[1,2,80,2048]{3,2,1,0:T(8,128)(2,1)} async-done(((bf16[8,2,80,2048]{3,2,1,0:T(8,128)(2,1)}), bf16[1,2,80,2048]{3,2,1,0:T(8,128)(2,1)}) %reduce-scatter.5.cloned.1.call-update) | async-done | bytes 655376 | tf_op jit(solution)/shard_map/reduce_scatter | solution.py:478
  404.5 6.4 %fusion.22.g_ref = bf16[2,80,2048]{2,1,0:T(8,128)(2,1)S(1)} fusion(bf16[2,80,2048]{2,1,0:T(8,128)(2,1)S(1)} %fusion.87, bf16[2048,2048]{1,0:T(8,128)(2,1)} %bitcast.387), kind=kOutput, calls=%fused_computation.36 | convolution fusion | flops 1342504960 | bytes 9699328 | tf_op jit(solution)/shard_map/dot_general | solution.py:60
  414.6 15.6 %shard_map.205 = (bf16[1,80,2048]{2,1,0:T(8,128)(2,1)S(1)}, f32[1,2560,256]{2,1,0:T(8,128)}) custom-call(bf16[2,80,2048]{2,1,0:T(8,128)(2,1)S(1)} %pad_maximum_fusion.12.q_ref, bf16[2,80,2048]{2,1,0:T(8,128)(2,1)S(1)} %fusion.22.g_ref, f32[2,80,2048]{2,1,0:T(8,128)S(1)} %get-tuple-element.114.wide_ref, f32[2,80,2048]{2,1,0:T(8,128)S(1)} %copy-done.1, ...), custom_call_target="tpu_custom_call" | custom-call | flops 4194304000 | bytes 2621440 | tf_op jit(solution)/shard_map/pallas_call | solution.py:191
  436.8 3.2 bitcast_convert_fusion.1
  444.5 2.8 fusion.43
  447.3 15.2 %shard_map.206 = (bf16[1,80,2048]{2,1,0:T(8,128)(2,1)S(1)}, f32[1,2560,256]{2,1,0:T(8,128)}) custom-call(bf16[2,80,2048]{2,1,0:T(8,128)(2,1)S(1)} %pad_maximum_fusion.12.q_ref, bf16[2,80,2048]{2,1,0:T(8,128)(2,1)S(1)} %fusion.22.g_ref, f32[2,80,2048]{2,1,0:T(8,128)S(1)} %get-tuple-element.114.wide_ref, f32[2,80,2048]{2,1,0:T(8,128)S(1)} %copy-done.2, ...), custom_call_target="tpu_custom_call" | custom-call | flops 4194304000 | bytes 2621440 | tf_op jit(solution)/shard_map/pallas_call | solution.py:191
  465.6 3.6 all-to-all-start.2
  477.3 11.0 %collective-permute-done.52 = bf16[176,2048]{1,0:T(8,128)(2,1)} collective-permute-done((bf16[176,2048]{1,0:T(8,128)(2,1)}, bf16[176,2048]{1,0:T(8,128)(2,1)}, u32[]{:S(2)}, u32[]{:S(2)}) %collective-permute-start.52) | collective-permute-done | bytes 720928 | tf_op jit(solution)/shard_map/ppermute | solution.py:227
  489.2 2.9 convert_add_fusion.6
  493.4 4.3 collective-permute-done.37
  500.0 3.2 collective-permute-start.39
  503.2 3.2 bitcast_convert_fusion
  506.5 5.5 collective-permute-done.41
  512.0 12.1 %collective-permute-done.40 = bf16[2,80,256]{2,1,0:T(8,128)(2,1)S(1)} collective-permute-done((bf16[2,80,256]{2,1,0:T(8,128)(2,1)S(1)}, bf16[2,80,256]{2,1,0:T(8,128)(2,1)S(1)}, u32[]{:S(2)}, u32[]{:S(2)}) %collective-permute-start.40) | collective-permute-done | bytes 81952 | tf_op jit(solution)/shard_map/ppermute | solution.py:227
  534.5 7.5 %fusion.36 = (f32[2,80]{1,0:T(2,128)S(1)}, f32[2,80,2048]{2,1,0:T(8,128)}) fusion(bf16[2,80,2048]{2,1,0:T(8,128)(2,1)S(1)} %copy-done.8, f32[2,80]{1,0:T(2,128)S(1)} %copy-done.39, f32[2,80,2048]{2,1,0:T(8,128)S(1)} %fusion.44, bf16[4,2,80,512]{3,2,1,0:T(8,128)(2,1)S(1)} %fusion.53, bf16[4,2048,512]{2,1,0:T(8,128)(2,1)} %bitcast.82), kind=kOutput, calls=%fused_computation.75 | convolution fusion | flops 1343815552 | bytes 12322048 | tf_op jit(solution)/shard_map/dot_general | solution.py:60
  552.0 4.3 fusion.30
  570.3 3.3 fusion.40
  (388 shorter events, 185.6 us)
Async XLA Ops:
  7.2 41.9 %all-gather.12.cloned.1.call-start = ((), (), s32[]{:S(2)}) async-start(), calls=%async_computation.12 | async-start | bytes 2359296 | tf_op jit(solution)/shard_map/all_gather | solution.py:358
  11.4 19.8 %collective-permute-start.2 = (bf16[2,80,2048]{2,1,0:T(8,128)(2,1)}, bf16[2,80,2048]{2,1,0:T(8,128)(2,1)}, u32[]{:S(2)}, u32[]{:S(2)}) collective-permute-start(bf16[2,80,2048]{2,1,0:T(8,128)(2,1)} %fusion.27), channel_id=1, source_target_pairs={{0,24},{8,16},{16,8},{24,0},{1,25},{9,17},{17,9},{25,1},{2,26},{10... | collective-permute-start | bytes 1966088 | tf_op jit(solution)/shard_map/ppermute | solution.py:227
  15.3 30.0 %collective-permute-start.1 = (bf16[2,80,2048]{2,1,0:T(8,128)(2,1)}, bf16[2,80,2048]{2,1,0:T(8,128)(2,1)}, u32[]{:S(2)}, u32[]{:S(2)}) collective-permute-start(bf16[2,80,2048]{2,1,0:T(8,128)(2,1)} %fusion.27), channel_id=1, source_target_pairs={{0,16},{8,24},{16,0},{24,8},{1,17},{9,25},{17,1},{25,9},{2,18},{10... | collective-permute-start | bytes 1966088 | tf_op jit(solution)/shard_map/ppermute | solution.py:227
  15.8 30.0 %collective-permute-start = (bf16[2,80,2048]{2,1,0:T(8,128)(2,1)}, bf16[2,80,2048]{2,1,0:T(8,128)(2,1)}, u32[]{:S(2)}, u32[]{:S(2)}) collective-permute-start(bf16[2,80,2048]{2,1,0:T(8,128)(2,1)} %fusion.27), channel_id=1, source_target_pairs={{0,8},{8,0},{16,24},{24,16},{1,9},{9,1},{17,25},{25,17},{2,10},{10... | collective-permute-start | bytes 1966088 | tf_op jit(solution)/shard_map/ppermute | solution.py:227
  17.3 31.8 %all-to-all-start = ((bf16[4,64,768]{2,1,0:T(8,128)(2,1)}), bf16[4,64,768]{2,1,0:T(8,128)(2,1)}, u32[]{:S(2)}, u32[]{:S(2)}) async-start(bf16[4,64,768]{2,1,0:T(8,128)(2,1)} %copy.198), calls=%async_computation | async-start | bytes 786432 | tf_op jit(solution)/shard_map/all_to_all | solution.py:362
  21.5 67.0 %all-gather.14.cloned.1.call-start = ((), (), s32[]{:S(2)}) async-start(), calls=%async_computation.13 | async-start | bytes 3538944 | tf_op jit(solution)/shard_map/all_gather | solution.py:372
  49.2 118.6 %all-gather.10.cloned.1.call-start = ((), (), s32[]{:S(2)}) async-start(), calls=%async_computation.7 | async-start | bytes 2949120 | tf_op jit(solution)/shard_map/all_gather | solution.py:402
  51.3 26.2 %collective-permute-start.3 = (bf16[4,64,2048]{2,1,0:T(8,128)(2,1)S(1)}, bf16[4,64,2048]{2,1,0:T(8,128)(2,1)S(1)}, u32[]{:S(2)}, u32[]{:S(2)}) collective-permute-start(bf16[4,64,2048]{2,1,0:T(8,128)(2,1)S(1)} %dynamic-slice_bitcast_fusion.5), channel_id=1, source_target_pairs={{0,8},{8,0},{16,24},{24,16},{1,9},{9,1},{17,25},{25,17},{2,10},{10... | collective-permute-start | bytes 3145736 | tf_op jit(solution)/shard_map/ppermute | solution.py:227
  53.7 46.2 %collective-permute-start.4 = (bf16[4,64,2048]{2,1,0:T(8,128)(2,1)S(1)}, bf16[4,64,2048]{2,1,0:T(8,128)(2,1)}, u32[]{:S(2)}, u32[]{:S(2)}) collective-permute-start(bf16[4,64,2048]{2,1,0:T(8,128)(2,1)S(1)} %dynamic-slice_bitcast_fusion.5), channel_id=1, source_target_pairs={{0,16},{8,24},{16,0},{24,8},{1,17},{9,25},{17,1},{25,9},{2,18},{10... | collective-permute-start | bytes 3145736 | tf_op jit(solution)/shard_map/ppermute | solution.py:227
  55.1 44.9 %collective-permute-start.5 = (bf16[4,64,2048]{2,1,0:T(8,128)(2,1)S(1)}, bf16[4,64,2048]{2,1,0:T(8,128)(2,1)}, u32[]{:S(2)}, u32[]{:S(2)}) collective-permute-start(bf16[4,64,2048]{2,1,0:T(8,128)(2,1)S(1)} %dynamic-slice_bitcast_fusion.5), channel_id=1, source_target_pairs={{0,24},{8,16},{16,8},{24,0},{1,25},{9,17},{17,9},{25,1},{2,26},{10... | collective-permute-start | bytes 3145736 | tf_op jit(solution)/shard_map/ppermute | solution.py:227
  109.4 58.3 %collective-permute-start.9 = (bf16[1024,2048]{1,0:T(8,128)(2,1)}, bf16[1024,2048]{1,0:T(8,128)(2,1)}, u32[]{:S(2)}, u32[]{:S(2)}) collective-permute-start(bf16[1024,2048]{1,0:T(8,128)(2,1)} %bitcast.27), channel_id=1, source_target_pairs={{0,1},{1,0},{2,3},{3,2},{4,5},{5,4},{6,7},{7,6},{8,9},{9,8},{10,11... | collective-permute-start | bytes 12582920 | tf_op jit(solution)/shard_map/ppermute | solution.py:227
  114.5 53.2 %all-to-all-start.1 = ((bf16[8,64,1408]{2,1,0:T(8,128)(2,1)}), bf16[8,64,1408]{2,1,0:T(8,128)(2,1)}, u32[]{:S(2)}, u32[]{:S(2)}) async-start(bf16[8,64,1408]{2,1,0:T(8,128)(2,1)} %copy.203), calls=%async_computation.1 | async-start | bytes 2883584 | tf_op jit(solution)/shard_map/all_to_all | solution.py:393
  119.7 104.5 %all-gather.16.cloned.1.call-start = ((), (), s32[]{:S(2)}) async-start(), calls=%async_computation.14 | async-start | bytes 5898240 | tf_op jit(solution)/shard_map/all_gather | solution.py:431
  127.2 23.0 %collective-permute-start.10 = (bf16[176,2048]{1,0:T(8,128)(2,1)}, bf16[176,2048]{1,0:T(8,128)(2,1)S(1)}, u32[]{:S(2)}, u32[]{:S(2)}) collective-permute-start(bf16[176,2048]{1,0:T(8,128)(2,1)} %param.21), channel_id=1, source_target_pairs={{0,8},{8,0},{16,24},{24,16},{1,9},{9,1},{17,25},{25,17},{2,10},{10... | collective-permute-start | bytes 2162696 | tf_op jit(solution)/shard_map/ppermute | solution.py:227
  132.8 33.1 %collective-permute-start.11 = (bf16[176,2048]{1,0:T(8,128)(2,1)}, bf16[176,2048]{1,0:T(8,128)(2,1)S(1)}, u32[]{:S(2)}, u32[]{:S(2)}) collective-permute-start(bf16[176,2048]{1,0:T(8,128)(2,1)} %param.21), channel_id=1, source_target_pairs={{0,16},{8,24},{16,0},{24,8},{1,17},{9,25},{17,1},{25,9},{2,18},{10... | collective-permute-start | bytes 2162696 | tf_op jit(solution)/shard_map/ppermute | solution.py:227
  134.4 32.4 %collective-permute-start.12 = (bf16[176,2048]{1,0:T(8,128)(2,1)}, bf16[176,2048]{1,0:T(8,128)(2,1)S(1)}, u32[]{:S(2)}, u32[]{:S(2)}) collective-permute-start(bf16[176,2048]{1,0:T(8,128)(2,1)} %param.21), channel_id=1, source_target_pairs={{0,24},{8,16},{16,8},{24,0},{1,25},{9,17},{17,9},{25,1},{2,26},{10... | collective-permute-start | bytes 2162696 | tf_op jit(solution)/shard_map/ppermute | solution.py:227
  167.8 126.1 %all-gather.18.cloned.1.call-start = ((), (), s32[]{:S(2)}) async-start(), calls=%async_computation.15 | async-start | bytes 5898240 | tf_op jit(solution)/shard_map/all_gather | solution.py:453
  167.9 32.1 %collective-permute-start.13 = (bf16[8,64,1408]{2,1,0:T(8,128)(2,1)}, bf16[8,64,1408]{2,1,0:T(8,128)(2,1)}, u32[]{:S(2)}, u32[]{:S(2)}) collective-permute-start(bf16[8,64,1408]{2,1,0:T(8,128)(2,1)} %all-to-all-done.1), channel_id=1, source_target_pairs={{0,8},{8,0},{16,24},{24,16},{1,9},{9,1},{17,25},{25,17},{2,10},{10... | collective-permute-start | bytes 4325384 | tf_op jit(solution)/shard_map/ppermute | solution.py:227
  168.1 33.2 %collective-permute-start.14 = (bf16[8,64,1408]{2,1,0:T(8,128)(2,1)}, bf16[8,64,1408]{2,1,0:T(8,128)(2,1)}, u32[]{:S(2)}, u32[]{:S(2)}) collective-permute-start(bf16[8,64,1408]{2,1,0:T(8,128)(2,1)} %all-to-all-done.1), channel_id=1, source_target_pairs={{0,16},{8,24},{16,0},{24,8},{1,17},{9,25},{17,1},{25,9},{2,18},{10... | collective-permute-start | bytes 4325384 | tf_op jit(solution)/shard_map/ppermute | solution.py:227
  224.1 171.1 %reduce-scatter.5.cloned.1.call-start = ((), (), s32[]{:S(2)}) async-start(), calls=%async_computation.8 | async-start | bytes 5898240 | tf_op jit(solution)/shard_map/reduce_scatter | solution.py:478
  228.3 35.7 %collective-permute-start.15 = (bf16[8,64,1408]{2,1,0:T(8,128)(2,1)}, bf16[8,64,1408]{2,1,0:T(8,128)(2,1)S(1)}, u32[]{:S(2)}, u32[]{:S(2)}) collective-permute-start(bf16[8,64,1408]{2,1,0:T(8,128)(2,1)} %all-to-all-done.1), channel_id=1, source_target_pairs={{0,24},{8,16},{16,8},{24,0},{1,25},{9,17},{17,9},{25,1},{2,26},{10... | collective-permute-start | bytes 4325384 | tf_op jit(solution)/shard_map/ppermute | solution.py:227
  236.2 41.7 %collective-permute-start.18 = (bf16[2,80,2048]{2,1,0:T(8,128)(2,1)S(1)}, bf16[2,80,2048]{2,1,0:T(8,128)(2,1)S(1)}, u32[]{:S(2)}, u32[]{:S(2)}) collective-permute-start(bf16[2,80,2048]{2,1,0:T(8,128)(2,1)S(1)} %get-tuple-element.105), channel_id=1, source_target_pairs={{0,24},{8,16},{16,8},{24,0},{1,25},{9,17},{17,9},{25,1},{2,26},{10... | collective-permute-start | bytes 1966088 | tf_op jit(solution)/shard_map/ppermute | solution.py:227
  236.7 54.6 %collective-permute-start.17 = (bf16[2,80,2048]{2,1,0:T(8,128)(2,1)S(1)}, bf16[2,80,2048]{2,1,0:T(8,128)(2,1)S(1)}, u32[]{:S(2)}, u32[]{:S(2)}) collective-permute-start(bf16[2,80,2048]{2,1,0:T(8,128)(2,1)S(1)} %get-tuple-element.105), channel_id=1, source_target_pairs={{0,16},{8,24},{16,0},{24,8},{1,17},{9,25},{17,1},{25,9},{2,18},{10... | collective-permute-start | bytes 1966088 | tf_op jit(solution)/shard_map/ppermute | solution.py:227
  238.4 53.6 %collective-permute-start.16 = (bf16[2,80,2048]{2,1,0:T(8,128)(2,1)S(1)}, bf16[2,80,2048]{2,1,0:T(8,128)(2,1)S(1)}, u32[]{:S(2)}, u32[]{:S(2)}) collective-permute-start(bf16[2,80,2048]{2,1,0:T(8,128)(2,1)S(1)} %get-tuple-element.105), channel_id=1, source_target_pairs={{0,8},{8,0},{16,24},{24,16},{1,9},{9,1},{17,25},{25,17},{2,10},{10... | collective-permute-start | bytes 1966088 | tf_op jit(solution)/shard_map/ppermute | solution.py:227
  239.8 86.1 %collective-permute-start.19 = (bf16[4,4,64,512]{3,2,1,0:T(8,128)(2,1)}, bf16[4,4,64,512]{3,2,1,0:T(8,128)(2,1)}, u32[]{:S(2)}, u32[]{:S(2)}) collective-permute-start(bf16[4,4,64,512]{3,2,1,0:T(8,128)(2,1)} %dynamic-slice_bitcast_fusion.4), channel_id=1, source_target_pairs={{0,8},{8,0},{16,24},{24,16},{1,9},{9,1},{17,25},{25,17},{2,10},{10... | collective-permute-start | bytes 3145736 | tf_op jit(solution)/shard_map/ppermute | solution.py:227
  264.0 62.0 %collective-permute-start.20 = (bf16[4,4,64,512]{3,2,1,0:T(8,128)(2,1)}, bf16[4,4,64,512]{3,2,1,0:T(8,128)(2,1)}, u32[]{:S(2)}, u32[]{:S(2)}) collective-permute-start(bf16[4,4,64,512]{3,2,1,0:T(8,128)(2,1)} %dynamic-slice_bitcast_fusion.4), channel_id=1, source_target_pairs={{0,16},{8,24},{16,0},{24,8},{1,17},{9,25},{17,1},{25,9},{2,18},{10... | collective-permute-start | bytes 3145736 | tf_op jit(solution)/shard_map/ppermute | solution.py:227
  278.0 58.4 %collective-permute-start.21 = (bf16[4,4,64,512]{3,2,1,0:T(8,128)(2,1)}, bf16[4,4,64,512]{3,2,1,0:T(8,128)(2,1)}, u32[]{:S(2)}, u32[]{:S(2)}) collective-permute-start(bf16[4,4,64,512]{3,2,1,0:T(8,128)(2,1)} %dynamic-slice_bitcast_fusion.4), channel_id=1, source_target_pairs={{0,24},{8,16},{16,8},{24,0},{1,25},{9,17},{17,9},{25,1},{2,26},{10... | collective-permute-start | bytes 3145736 | tf_op jit(solution)/shard_map/ppermute | solution.py:227
  336.4 170.1 %reduce-scatter.7.cloned.1.call-start = ((), (), s32[]{:S(2)}) async-start(), calls=%async_computation.9 | async-start | bytes 5898240 | tf_op jit(solution)/shard_map/reduce_scatter | solution.py:510
  339.2 41.1 %collective-permute-start.24 = (bf16[4,4,256,512]{3,2,1,0:T(8,128)(2,1)S(1)}, bf16[4,4,256,512]{3,2,1,0:T(8,128)(2,1)S(1)}, u32[]{:S(2)}, u32[]{:S(2)}) collective-permute-start(bf16[4,4,256,512]{3,2,1,0:T(8,128)(2,1)S(1)} %pad_maximum_fusion), channel_id=1, source_target_pairs={{0,1},{1,0},{2,3},{3,2},{4,5},{5,4},{6,7},{7,6},{8,9},{9,8},{10,11... | collective-permute-start | bytes 12582920 | tf_op jit(solution)/shard_map/ppermute | solution.py:227
  354.5 41.9 %collective-permute-start.22 = (bf16[2,8,32,1408]{3,2,1,0:T(8,128)(2,1)}, bf16[2,8,32,1408]{3,2,1,0:T(8,128)(2,1)}, u32[]{:S(2)}, u32[]{:S(2)}) collective-permute-start(bf16[2,8,32,1408]{3,2,1,0:T(8,128)(2,1)} %pad_maximum_fusion.7), channel_id=1, source_target_pairs={{0,8},{8,0},{16,24},{24,16},{1,9},{9,1},{17,25},{25,17},{2,10},{10... | collective-permute-start | bytes 4325384 | tf_op jit(solution)/shard_map/ppermute | solution.py:227
  357.0 39.4 %collective-permute-start.23 = (bf16[2,8,32,1408]{3,2,1,0:T(8,128)(2,1)}, bf16[2,8,32,1408]{3,2,1,0:T(8,128)(2,1)}, u32[]{:S(2)}, u32[]{:S(2)}) collective-permute-start(bf16[2,8,32,1408]{3,2,1,0:T(8,128)(2,1)} %pad_maximum_fusion.8), channel_id=1, source_target_pairs={{0,16},{8,24},{16,0},{24,8},{1,17},{9,25},{17,1},{25,9},{2,18},{10... | collective-permute-start | bytes 4325384 | tf_op jit(solution)/shard_map/ppermute | solution.py:227
  396.5 167.7 %reduce-scatter.9.cloned.1.call-start = ((), (), s32[]{:S(2)}) async-start(), calls=%async_computation.10 | async-start | bytes 2359296 | tf_op jit(solution)/shard_map/reduce_scatter | solution.py:549
  399.4 33.2 %collective-permute-start.28 = (bf16[1,8,32,1408]{3,2,1,0:T(8,128)(2,1)S(1)}, bf16[1,8,32,1408]{3,2,1,0:T(8,128)(2,1)S(1)}, u32[]{:S(2)}, u32[]{:S(2)}) collective-permute-start(bf16[1,8,32,1408]{3,2,1,0:T(8,128)(2,1)S(1)} %fusion.47), channel_id=1, source_target_pairs={{0,16},{8,24},{16,0},{24,8},{1,17},{9,25},{17,1},{25,9},{2,18},{10... | collective-permute-start | bytes 2162696 | tf_op jit(solution)/shard_map/ppermute | solution.py:227
  402.4 30.2 %collective-permute-start.29 = (bf16[1,8,32,1408]{3,2,1,0:T(8,128)(2,1)S(1)}, bf16[1,8,32,1408]{3,2,1,0:T(8,128)(2,1)S(1)}, u32[]{:S(2)}, u32[]{:S(2)}) collective-permute-start(bf16[1,8,32,1408]{3,2,1,0:T(8,128)(2,1)S(1)} %fusion.48), channel_id=1, source_target_pairs={{0,8},{8,0},{16,24},{24,16},{1,9},{9,1},{17,25},{25,17},{2,10},{10... | collective-permute-start | bytes 2162696 | tf_op jit(solution)/shard_map/ppermute | solution.py:227
  411.0 21.5 %collective-permute-start.27 = (bf16[2,80,512]{2,1,0:T(8,128)(2,1)S(1)}, bf16[2,80,512]{2,1,0:T(8,128)(2,1)S(1)}, u32[]{:S(2)}, u32[]{:S(2)}) collective-permute-start(bf16[2,80,512]{2,1,0:T(8,128)(2,1)S(1)} %get-tuple-element.207), channel_id=1, source_target_pairs={{0,24},{8,16},{16,8},{24,0},{1,25},{9,17},{17,9},{25,1},{2,26},{10... | collective-permute-start | bytes 491528 | tf_op jit(solution)/shard_map/ppermute | solution.py:227
  411.9 20.6 %collective-permute-start.26 = (bf16[2,80,512]{2,1,0:T(8,128)(2,1)S(1)}, bf16[2,80,512]{2,1,0:T(8,128)(2,1)S(1)}, u32[]{:S(2)}, u32[]{:S(2)}) collective-permute-start(bf16[2,80,512]{2,1,0:T(8,128)(2,1)S(1)} %get-tuple-element.206), channel_id=1, source_target_pairs={{0,16},{8,24},{16,0},{24,8},{1,17},{9,25},{17,1},{25,9},{2,18},{10... | collective-permute-start | bytes 491528 | tf_op jit(solution)/shard_map/ppermute | solution.py:227
  441.0 21.6 %collective-permute-start.30 = (bf16[176,2048]{1,0:T(8,128)(2,1)}, bf16[176,2048]{1,0:T(8,128)(2,1)S(1)}, u32[]{:S(2)}, u32[]{:S(2)}) collective-permute-start(bf16[176,2048]{1,0:T(8,128)(2,1)} %get-tuple-element.126), channel_id=1, source_target_pairs={{0,8},{8,0},{16,24},{24,16},{1,9},{9,1},{17,25},{25,17},{2,10},{10... | collective-permute-start | bytes 2162696 | tf_op jit(solution)/shard_map/ppermute | solution.py:227
  441.7 34.0 %collective-permute-start.53 = (bf16[176,2048]{1,0:T(8,128)(2,1)}, bf16[176,2048]{1,0:T(8,128)(2,1)}, u32[]{:S(2)}, u32[]{:S(2)}) collective-permute-start(bf16[176,2048]{1,0:T(8,128)(2,1)} %get-tuple-element.143), channel_id=1, source_target_pairs={{0,24},{8,16},{16,8},{24,0},{1,25},{9,17},{17,9},{25,1},{2,26},{10... | collective-permute-start | bytes 2162696 | tf_op jit(solution)/shard_map/ppermute | solution.py:227
  443.0 45.3 %collective-permute-start.52 = (bf16[176,2048]{1,0:T(8,128)(2,1)}, bf16[176,2048]{1,0:T(8,128)(2,1)}, u32[]{:S(2)}, u32[]{:S(2)}) collective-permute-start(bf16[176,2048]{1,0:T(8,128)(2,1)} %get-tuple-element.142), channel_id=1, source_target_pairs={{0,16},{8,24},{16,0},{24,8},{1,17},{9,25},{17,1},{25,9},{2,18},{10... | collective-permute-start | bytes 2162696 | tf_op jit(solution)/shard_map/ppermute | solution.py:227
  465.6 59.5 %all-to-all-start.2 = ((bf16[8,64,1408]{2,1,0:T(8,128)(2,1)}), bf16[8,64,1408]{2,1,0:T(8,128)(2,1)S(1)}, u32[]{:S(2)}, u32[]{:S(2)}) async-start(bf16[8,64,1408]{2,1,0:T(8,128)(2,1)} %pad_maximum_fusion.9), calls=%async_computation.4 | async-start | bytes 2883584 | tf_op jit(solution)/shard_map/all_to_all | solution.py:546
  469.2 95.1 %reduce-scatter.11.cloned.1.call-start = ((), (), s32[]{:S(2)}) async-start(), calls=%async_computation.11 | async-start | bytes 2359296 | tf_op jit(solution)/shard_map/reduce_scatter | solution.py:575
  469.5 30.5 %collective-permute-start.33 = (bf16[2,80,512]{2,1,0:T(8,128)(2,1)S(1)}, bf16[2,80,512]{2,1,0:T(8,128)(2,1)S(1)}, u32[]{:S(2)}, u32[]{:S(2)}) collective-permute-start(bf16[2,80,512]{2,1,0:T(8,128)(2,1)S(1)} %get-tuple-element.203), channel_id=1, source_target_pairs={{0,24},{8,16},{16,8},{24,0},{1,25},{9,17},{17,9},{25,1},{2,26},{10... | collective-permute-start | bytes 491528 | tf_op jit(solution)/shard_map/ppermute | solution.py:227
  470.4 32.9 %collective-permute-start.32 = (bf16[2,80,512]{2,1,0:T(8,128)(2,1)S(1)}, bf16[2,80,512]{2,1,0:T(8,128)(2,1)S(1)}, u32[]{:S(2)}, u32[]{:S(2)}) collective-permute-start(bf16[2,80,512]{2,1,0:T(8,128)(2,1)S(1)} %get-tuple-element.202), channel_id=1, source_target_pairs={{0,16},{8,24},{16,0},{24,8},{1,17},{9,25},{17,1},{25,9},{2,18},{10... | collective-permute-start | bytes 491528 | tf_op jit(solution)/shard_map/ppermute | solution.py:227
  475.8 22.0 %collective-permute-start.37 = (bf16[4,2,80,256]{3,2,0,1:T(8,128)(2,1)S(1)}, bf16[4,2,80,256]{3,2,0,1:T(8,128)(2,1)S(1)}, u32[]{:S(2)}, u32[]{:S(2)}) collective-permute-start(bf16[4,2,80,256]{3,2,0,1:T(8,128)(2,1)S(1)} %get-tuple-element.183), channel_id=1, source_target_pairs={{0,16},{8,24},{16,0},{24,8},{1,17},{9,25},{17,1},{25,9},{2,18},{10... | collective-permute-start | bytes 983048 | tf_op jit(solution)/shard_map/ppermute | solution.py:227
  500.0 24.1 %collective-permute-start.40 = (bf16[2,80,256]{2,1,0:T(8,128)(2,1)S(1)}, bf16[2,80,256]{2,1,0:T(8,128)(2,1)S(1)}, u32[]{:S(2)}, u32[]{:S(2)}) collective-permute-start(bf16[2,80,256]{2,1,0:T(8,128)(2,1)S(1)} %get-tuple-element.218), channel_id=1, source_target_pairs={{0,4},{1,5},{2,6},{3,7},{4,0},{5,1},{6,2},{7,3},{8,12},{9,13},{10,... | collective-permute-start | bytes 245768 | tf_op jit(solution)/shard_map/ppermute | solution.py:227
  500.0 24.1 %collective-permute-start.39 = (bf16[2,80,256]{2,1,0:T(8,128)(2,1)S(1)}, bf16[2,80,256]{2,1,0:T(8,128)(2,1)S(1)}, u32[]{:S(2)}, u32[]{:S(2)}) collective-permute-start(bf16[2,80,256]{2,1,0:T(8,128)(2,1)S(1)} %get-tuple-element.216), channel_id=1, source_target_pairs={{0,2},{1,3},{2,0},{3,1},{4,6},{5,7},{6,4},{7,5},{8,10},{9,11},{10,... | collective-permute-start | bytes 245768 | tf_op jit(solution)/shard_map/ppermute | solution.py:227
  528.9 21.4 %collective-permute-start.47 = (bf16[8,64,256]{2,1,0:T(8,128)(2,1)}, bf16[8,64,256]{2,1,0:T(8,128)(2,1)}, u32[]{:S(2)}, u32[]{:S(2)}) collective-permute-start(bf16[8,64,256]{2,1,0:T(8,128)(2,1)} %get-tuple-element.191), channel_id=1, source_target_pairs={{0,24},{8,16},{16,8},{24,0},{1,25},{9,17},{17,9},{25,1},{2,26},{10... | collective-permute-start | bytes 786440 | tf_op jit(solution)/shard_map/ppermute | solution.py:227
  530.6 19.7 %collective-permute-start.46 = (bf16[8,64,256]{2,1,0:T(8,128)(2,1)}, bf16[8,64,256]{2,1,0:T(8,128)(2,1)}, u32[]{:S(2)}, u32[]{:S(2)}) collective-permute-start(bf16[8,64,256]{2,1,0:T(8,128)(2,1)} %get-tuple-element.192), channel_id=1, source_target_pairs={{0,16},{8,24},{16,0},{24,8},{1,17},{9,25},{17,1},{25,9},{2,18},{10... | collective-permute-start | bytes 786440 | tf_op jit(solution)/shard_map/ppermute | solution.py:227
  (74 other events, 585.5 us)
Sparse Core Ops, SparseCore 0:
  9.6 31.7 all-gather.11
  49.3 39.2 all-gather.13
  100.1 44.9 all-gather.9
  167.9 56.2 all-gather.15
  226.2 54.8 all-gather.17
  336.5 58.6 reduce-scatter.4
  397.5 58.2 reduce-scatter.6
  458.1 47.5 reduce-scatter.8
  508.0 48.6 reduce-scatter.10

commit v4 on v3

--- a/solution.py
+++ b/solution.py
@@ -407,11 +407,6 @@
     query_group = query_group.astype(low).reshape(across, batches, local_rows, q_here)
     query = jnp.concatenate(by_index(trade_au(list(query_group)), au_index), axis=-1)
 
-    out_half = jnp.zeros((rows // 2, across, own_width, width), low)
-    for k, part in enumerate(out_parts):
-        out_half = lax.dynamic_update_index_in_dim(out_half, part, au_index ^ k, 1)
-    out_half = out_half.reshape(-1, width)
-    out_other = exchange(out_half, "row", 1)
 
     down_full = jnp.zeros((across, ff_own, width), low)
     for k, part in enumerate(down_parts):
@@ -424,10 +419,15 @@
         keyval_all,
         ff_rows,
         query,
-        out_other,
         down_full,
         key_columns,
-    ) = together(out_grad, keyval_all, ff_rows, query, out_other, down_full, key_columns)
+        *out_parts,
+    ) = together(out_grad, keyval_all, ff_rows, query, down_full, key_columns, *out_parts)
+    out_half = jnp.zeros((rows // 2, across, own_width, width), low)
+    for k, part in enumerate(out_parts):
+        out_half = lax.dynamic_update_index_in_dim(out_half, part, au_index ^ k, 1)
+    out_half = out_half.reshape(-1, width)
+    out_other = exchange(out_half, "row", 1)
     grad_rows = lax.all_gather(grads_own, "row", axis=0).reshape(-1, width)
     ff_parts = gather_au(ff_rows)
     attended, att_wide, log_mass = attend(
@@ -451,7 +451,6 @@
     )
     unit_low, grad_rows = together(unit_low, grad_rows)
     unit_rows = lax.all_gather(unit_low, "row", axis=0).reshape(-1, width)
-    attended_group = jnp.stack(gather_au(attended_kept))
     query_half = gather_au(query_columns)
     pair = lax.dynamic_update_index_in_dim(
         jnp.zeros((rows // 2, 2) + (across * own_width, width), low),
@@ -474,7 +473,8 @@
     grad_up = grad_inner * gate * sigmoid_gate
     grad_both = jnp.concatenate([grad_gate.astype(low), grad_up.astype(low)], axis=1)
     scaled_two = dot32(grad_both, ff_full, NT).astype(low)
-    scaled_two, attended_group, *query_half = together(scaled_two, attended_group, *query_half)
+    scaled_two, attended_kept, *query_half = together(scaled_two, attended_kept, *query_half)
+    attended_group = jnp.stack(gather_au(attended_kept))
     scaled_two = lax.psum_scatter(
         scaled_two.reshape(rows, batches, local_rows, width), "row"
     ).astype(wide)
@@ -502,8 +502,8 @@
     )
     query_full = lax.dynamic_update_index_in_dim(pair, query_other, 1 - row_index % 2, 2)
     query_full = query_full.reshape(across, width, q_here)
-    scaled_two, result_part, down_parts, both_first, query_full = together(
-        scaled_two, result_part, down_parts, both_first, query_full
+    scaled_two, result_part, down_parts, both_first, query_full, attended_group = together(
+        scaled_two, result_part, down_parts, both_first, query_full, attended_group
     )
     both_term = jnp.concatenate(reduce_au_rest(both_lists, both_first), axis=1).astype(low)
     down_parts = trade_au(down_parts)
@@ -565,8 +565,9 @@
 
     parts = [here[:, :, k] for k in range(across)]
     parts = trade_au([parts[0]] + [part.astype(low) for part in parts[1:]])
+    *parts, both_term = together(*parts, both_term)
     grad_keyval_local = reduce_chips(sum(part.astype(wide) for part in parts))
-    grad_keyval_local, both_term = together(grad_keyval_local, both_term)
+    grad_keyval_local, *down_parts = together(grad_keyval_local, *down_parts)
     grad_keyval_local = (grad_keyval_local + kv_partner.astype(wide)).astype(low)
     grad_key_pre = rotate_back(grad_keyval_local[..., :HEAD_WIDTH].astype(wide), cosine, sine)
     grad_keyval_pre = jnp.concatenate(

time: 594 us -> 573 us (0.965)
  waiting for transfers between devices: 210 us -> 179 us
  local copies, waits for them, and re-layouts: 79.5 us -> 88.3 us
    ppermute x54, waiting for transfers between devices: 180 us -> 128 us  [exchange(): return lax.ppermute(values, axis, [(i, i ^ offset) for i in range(members)])]
    all_to_all x1, waiting for transfers between devices: 0.01 us -> 16.9 us  [on_device(): ff_rows = lax.all_to_all(ff_blocks, 'row', 0, 0)]
    all_gather x1, waiting for transfers between devices: 0.01 us -> 10.2 us  [on_device(): unit_rows = lax.all_gather(unit_low, 'row', axis=0).reshape(-1, width)]
  transfers between devices with their start and end apart: 66 -> 66, of which waited for: 26 -> 26; matrix products, arithmetic and copies ran while one was open for 38% -> 41% of each run, Pallas kernels for 8% -> 8%
where the time goes in v4:
time: 573 us; the launch traced here: 564 us
  waiting for transfers between devices  179 us (31%)
  matrix products  90.9 us (16%)
  local copies, waits for them, and re-layouts  88.3 us (15%)
  starting transfers between devices  78 us (14%)
  other arithmetic  66 us (12%)
  Pallas kernels  45.4 us (8%)
  between operations  15.6 us (3%)
    ppermute x54, waiting for transfers between devices, exchange(): return lax.ppermute(values, axis, [(i, i ^ offset) for i in range(members)])  128 us
    dot_general x15, matrix products, dot32(): lax.dot_general(left, right, (dims, ((), ())), preferred_element_type=jnp...  90.9 us
    ppermute x54, starting transfers between devices, exchange(): return lax.ppermute(values, axis, [(i, i ^ offset) for i in range(members)])  63.2 us
    pallas_call x2, Pallas kernels, attend_back(): pl.pallas_call(functools.partial(attend_back_kernel, heads, min(512, slot...  30.5 us
    all_to_all x1, waiting for transfers between devices, on_device(): ff_rows = lax.all_to_all(ff_blocks, 'row', 0, 0)  16.9 us
    pallas_call x1, Pallas kernels, attend(): pl.pallas_call(functools.partial(attend_kernel, heads), grid=(batches, HQ...  14.9 us
  transfers between devices with their start and end apart: 66, of which 26 were waited for; matrix products, arithmetic and copies ran while one was open for 41% of the time, Pallas kernels for 8%

profile of v4, /device:TPU:0, one launch (start us, length us, event | category | flops | bytes accessed | tf_op | source)
XLA Modules:
  0.0 563.7 jit_solution(2916251952469934322)
XLA Ops:
  11.4 3.9 collective-permute-start.2
  17.3 4.2 all-to-all-start
  24.9 6.3 %collective-permute-done.2 = bf16[2,80,2048]{2,1,0:T(8,128)(2,1)} collective-permute-done((bf16[2,80,2048]{2,1,0:T(8,128)(2,1)}, bf16[2,80,2048]{2,1,0:T(8,128)(2,1)}, u32[]{:S(2)}, u32[]{:S(2)}) %collective-permute-start.2) | collective-permute-done | bytes 655392 | tf_op jit(solution)/shard_map/ppermute | solution.py:227
  31.2 14.1 %collective-permute-done.1 = bf16[2,80,2048]{2,1,0:T(8,128)(2,1)} collective-permute-done((bf16[2,80,2048]{2,1,0:T(8,128)(2,1)}, bf16[2,80,2048]{2,1,0:T(8,128)(2,1)}, u32[]{:S(2)}, u32[]{:S(2)}) %collective-permute-start.1) | collective-permute-done | bytes 655392 | tf_op jit(solution)/shard_map/ppermute | solution.py:227
  45.8 3.3 pad_maximum_fusion.3
  56.6 21.6 %collective-permute-done.3 = bf16[4,64,2048]{2,1,0:T(8,128)(2,1)S(1)} collective-permute-done((bf16[4,64,2048]{2,1,0:T(8,128)(2,1)S(1)}, bf16[4,64,2048]{2,1,0:T(8,128)(2,1)S(1)}, u32[]{:S(2)}, u32[]{:S(2)}) %collective-permute-start.3) | collective-permute-done | bytes 1048608 | tf_op jit(solution)/shard_map/ppermute | solution.py:227
  78.2 11.0 %all-gather.14.cloned.1.call-done = bf16[32,64,768]{2,1,0:T(8,128)(2,1)} async-done(((bf16[4,64,768]{2,1,0:T(8,128)(2,1)}), bf16[32,64,768]{2,1,0:T(8,128)(2,1)}) %all-gather.14.cloned.1.call-update) | async-done | bytes 3145744 | tf_op jit(solution)/shard_map/all_gather | solution.py:372
  89.2 4.9 fusion.6
  96.5 4.2 collective-permute-done.4
  109.0 5.0 all-to-all-start.1
  124.0 2.8 collective-permute-done.6
  127.0 18.2 %collective-permute-done.7 = bf16[2,80,512]{2,1,0:T(8,128)(2,1)S(1)} collective-permute-done((bf16[2,80,512]{2,1,0:T(8,128)(2,1)}, bf16[2,80,512]{2,1,0:T(8,128)(2,1)S(1)}, u32[]{:S(2)}, u32[]{:S(2)}) %collective-permute-start.7) | collective-permute-done | bytes 163872 | tf_op jit(solution)/shard_map/ppermute | solution.py:227
  148.7 16.9 %all-to-all-done.1 = bf16[8,64,1408]{2,1,0:T(8,128)(2,1)} async-done(((bf16[8,64,1408]{2,1,0:T(8,128)(2,1)}), bf16[8,64,1408]{2,1,0:T(8,128)(2,1)}, u32[]{:S(2)}, u32[]{:S(2)}) %all-to-all-start.1) | async-done | bytes 1441824 | tf_op jit(solution)/shard_map/all_to_all | solution.py:393
  182.1 14.9 %shard_map.204 = (bf16[2,80,2048]{2,1,0:T(8,128)(2,1)S(1)}, f32[2,80,2048]{2,1,0:T(8,128)S(1)}, f32[2,80,2048]{2,1,0:T(8,128)S(1)}) custom-call(bf16[2,80,2048]{2,1,0:T(8,128)(2,1)S(1)} %pad_maximum_fusion.12.q_ref, bf16[2,2560,256]{2,1,0:T(8,128)(2,1)} %all-gather.10.cloned.1.call-done.kv_ref, s32[2,80,2]{2,1,0:T(8,128)S(1)} %bitcast.383, ...), custom_call_target="tpu_custom_call" | custom-call | flops 3355443200 | bytes 5242880 | tf_op jit(solution)/shard_map/pallas_call | solution.py:111
  198.1 12.1 %collective-permute-done.12 = bf16[8,64,1408]{2,1,0:T(8,128)(2,1)} collective-permute-done((bf16[8,64,1408]{2,1,0:T(8,128)(2,1)}, bf16[8,64,1408]{2,1,0:T(8,128)(2,1)}, u32[]{:S(2)}, u32[]{:S(2)}) %collective-permute-start.12) | collective-permute-done | bytes 1441824 | tf_op jit(solution)/shard_map/ppermute | solution.py:227
  215.3 3.2 fusion.95
  218.5 3.4 multiply_reduce_fusion.1
  225.9 3.3 broadcast_in_dim.145
  231.9 4.3 broadcast_in_dim.142
  236.2 4.7 bitcast_dynamic-update-slice_fusion
  246.1 12.2 %collective-permute-done.15 = bf16[8,64,1408]{2,1,0:T(8,128)(2,1)S(1)} collective-permute-done((bf16[8,64,1408]{2,1,0:T(8,128)(2,1)}, bf16[8,64,1408]{2,1,0:T(8,128)(2,1)S(1)}, u32[]{:S(2)}, u32[]{:S(2)}) %collective-permute-start.15) | collective-permute-done | bytes 1441824 | tf_op jit(solution)/shard_map/ppermute | solution.py:227
  262.9 4.8 constant_dynamic-update-slice_fusion
  267.7 10.2 %all-gather.18.cloned.1.call-done = bf16[16,80,2048]{2,1,0:T(8,128)(2,1)} async-done(((bf16[2,80,2048]{2,1,0:T(8,128)(2,1)}), bf16[16,80,2048]{2,1,0:T(8,128)(2,1)}) %all-gather.18.cloned.1.call-update) | async-done | bytes 5242896 | tf_op jit(solution)/shard_map/all_gather | solution.py:453
  277.9 12.9 %fusion.96 = f32[1280,1408]{0,1:T(8,128)S(1)} fusion(bf16[1280,2048]{1,0:T(8,128)(2,1)} %bitcast.433, bf16[2048,1408]{1,0:T(8,128)(2,1)} %bitcast.53), kind=kOutput, calls=%fused_computation.295 | convolution fusion | flops 7381975040 | bytes 18219008 | tf_op jit(solution)/shard_map/dot_general | solution.py:60
  290.9 9.1 %multiply_convert_fusion.2 = (bf16[1280,704]{0,1:T(8,128)(2,1)S(1)}, bf16[1280,704]{0,1:T(8,128)(2,1)S(1)}, bf16[1280,704]{0,1:T(8,128)(2,1)}) fusion(f32[1280,1408]{0,1:T(8,128)S(1)} %fusion.96, bf16[1280,2048]{1,0:T(8,128)(2,1)} %bitcast.429, bf16[704,2048]{1,0:T(8,128)(2,1)S(1)} %bitcast.394), kind=kOutput, calls=%fused_computation.19 | convolution fusion | flops 3705405440 | bytes 20742144 | tf_op jit(solution)/shard_map/dot_general | solution.py:60
  299.9 13.3 %convolution_convert_fusion.2 = bf16[1280,2048]{1,0:T(8,128)(2,1)} fusion(bf16[2048,1408]{1,0:T(8,128)(2,1)} %bitcast.53, bf16[1280,704]{0,1:T(8,128)(2,1)S(1)} %get-tuple-element.178, bf16[1280,704]{0,1:T(8,128)(2,1)S(1)} %get-tuple-element.177), kind=kOutput, calls=%fused_computation.7 | convolution fusion | flops 7391805440 | bytes 14614528 | tf_op jit(solution)/shard_map/dot_general | solution.py:60
  316.9 3.2 pad_maximum_fusion
  320.6 10.3 %convolution_convert_fusion = bf16[2048,1408]{1,0:T(8,128)(2,1)S(1)} fusion(bf16[1280,2048]{1,0:T(8,128)(2,1)} %bitcast.434, bf16[1280,704]{0,1:T(8,128)(2,1)S(1)} %copy-done.63, bf16[1280,704]{0,1:T(8,128)(2,1)S(1)} %copy-done.61), kind=kOutput, calls=%fused_computation.5 | convolution fusion | flops 7392067584 | bytes 14614528 | tf_op jit(solution)/shard_map/dot_general | solution.py:60
  336.6 6.1 %convolution_convert_fusion.1 = bf16[1280,2048]{1,0:T(8,128)(2,1)} fusion(bf16[1280,704]{0,1:T(8,128)(2,1)S(1)} %copy-done.59, bf16[704,2048]{1,0:T(8,128)(2,1)S(1)} %bitcast.395), kind=kOutput, calls=%fused_computation.6 | convolution fusion | flops 3693608960 | bytes 9928704 | tf_op jit(solution)/shard_map/dot_general | solution.py:60
  342.6 4.1 convolution_convert_fusion.3
  348.0 4.1 broadcast_in_dim.150
  352.2 3.7 maximum_dynamic-update-slice_fusion
  363.2 8.9 %reduce-scatter.5.cloned.1.call-done = bf16[1,2,80,2048]{3,2,1,0:T(8,128)(2,1)} async-done(((bf16[8,2,80,2048]{3,2,1,0:T(8,128)(2,1)}), bf16[1,2,80,2048]{3,2,1,0:T(8,128)(2,1)}) %reduce-scatter.5.cloned.1.call-update) | async-done | bytes 655376 | tf_op jit(solution)/shard_map/reduce_scatter | solution.py:478
  376.2 13.4 %collective-permute-done.20 = bf16[2,8,32,1408]{3,2,1,0:T(8,128)(2,1)} collective-permute-done((bf16[2,8,32,1408]{3,2,1,0:T(8,128)(2,1)}, bf16[2,8,32,1408]{3,2,1,0:T(8,128)(2,1)}, u32[]{:S(2)}, u32[]{:S(2)}) %collective-permute-start.20) | collective-permute-done | bytes 1441824 | tf_op jit(solution)/shard_map/ppermute | solution.py:227
  397.8 6.4 %fusion.22.g_ref = bf16[2,80,2048]{2,1,0:T(8,128)(2,1)S(1)} fusion(bf16[2,80,2048]{2,1,0:T(8,128)(2,1)S(1)} %fusion.84, bf16[2048,2048]{1,0:T(8,128)(2,1)} %bitcast.48), kind=kOutput, calls=%fused_computation.36 | convolution fusion | flops 1342504960 | bytes 9699328 | tf_op jit(solution)/shard_map/dot_general | solution.py:60
  407.8 15.2 %shard_map.205 = (bf16[1,80,2048]{2,1,0:T(8,128)(2,1)S(1)}, f32[1,2560,256]{2,1,0:T(8,128)}) custom-call(bf16[2,80,2048]{2,1,0:T(8,128)(2,1)S(1)} %pad_maximum_fusion.12.q_ref, bf16[2,80,2048]{2,1,0:T(8,128)(2,1)S(1)} %fusion.22.g_ref, f32[2,80,2048]{2,1,0:T(8,128)S(1)} %get-tuple-element.130.wide_ref, f32[2,80,2048]{2,1,0:T(8,128)S(1)} %copy-done.1, ...), custom_call_target="tpu_custom_call" | custom-call | flops 4194304000 | bytes 2621440 | tf_op jit(solution)/shard_map/pallas_call | solution.py:191
  429.6 3.2 bitcast_convert_fusion.1
  440.2 4.3 all-to-all-start.2
  445.9 15.3 %shard_map.206 = (bf16[1,80,2048]{2,1,0:T(8,128)(2,1)S(1)}, f32[1,2560,256]{2,1,0:T(8,128)}) custom-call(bf16[2,80,2048]{2,1,0:T(8,128)(2,1)S(1)} %pad_maximum_fusion.12.q_ref, bf16[2,80,2048]{2,1,0:T(8,128)(2,1)S(1)} %fusion.22.g_ref, f32[2,80,2048]{2,1,0:T(8,128)S(1)} %get-tuple-element.130.wide_ref, f32[2,80,2048]{2,1,0:T(8,128)S(1)} %copy-done.2, ...), custom_call_target="tpu_custom_call" | custom-call | flops 4194304000 | bytes 2621440 | tf_op jit(solution)/shard_map/pallas_call | solution.py:191
  469.5 3.0 collective-permute-done.33
  478.4 3.2 bitcast_convert_fusion
  483.2 8.9 %collective-permute-done.37 = bf16[4,2,80,256]{3,2,0,1:T(8,128)(2,1)S(1)} collective-permute-done((bf16[4,2,80,256]{3,2,0,1:T(8,128)(2,1)S(1)}, bf16[4,2,80,256]{3,2,0,1:T(8,128)(2,1)S(1)}, u32[]{:S(2)}, u32[]{:S(2)}) %collective-permute-start.37) | collective-permute-done | bytes 327712 | tf_op jit(solution)/shard_map/ppermute | solution.py:227
  496.2 3.5 collective-permute-start.39
  508.4 4.4 fusion.30
  522.1 7.6 %fusion.36 = (f32[2,80]{1,0:T(2,128)S(1)}, f32[2,80,2048]{2,1,0:T(8,128)}) fusion(bf16[2,80,2048]{2,1,0:T(8,128)(2,1)S(1)} %copy-done.8, f32[2,80]{1,0:T(2,128)S(1)} %copy-done.48, f32[2,80,2048]{2,1,0:T(8,128)S(1)} %fusion.44, bf16[4,2,80,512]{3,2,1,0:T(8,128)(2,1)S(1)} %copy-done.28, bf16[4,2048,512]{2,1,0:T(8,128)(2,1)} %bitcast.79), kind=kOutput, calls=%fused_computation.75 | convolution fusion | flops 1343815552 | bytes 12322048 | tf_op jit(solution)/shard_map/dot_general | solution.py:60
  530.8 3.1 convert_add_fusion.6
  535.5 2.9 collective-permute-start.51
  549.9 3.3 fusion.40
  (411 shorter events, 185.2 us)
Async XLA Ops:
  7.2 41.9 %all-gather.12.cloned.1.call-start = ((), (), s32[]{:S(2)}) async-start(), calls=%async_computation.12 | async-start | bytes 2359296 | tf_op jit(solution)/shard_map/all_gather | solution.py:358
  11.4 19.8 %collective-permute-start.2 = (bf16[2,80,2048]{2,1,0:T(8,128)(2,1)}, bf16[2,80,2048]{2,1,0:T(8,128)(2,1)}, u32[]{:S(2)}, u32[]{:S(2)}) collective-permute-start(bf16[2,80,2048]{2,1,0:T(8,128)(2,1)} %fusion.27), channel_id=1, source_target_pairs={{0,24},{8,16},{16,8},{24,0},{1,25},{9,17},{17,9},{25,1},{2,26},{10... | collective-permute-start | bytes 1966088 | tf_op jit(solution)/shard_map/ppermute | solution.py:227
  15.3 30.0 %collective-permute-start.1 = (bf16[2,80,2048]{2,1,0:T(8,128)(2,1)}, bf16[2,80,2048]{2,1,0:T(8,128)(2,1)}, u32[]{:S(2)}, u32[]{:S(2)}) collective-permute-start(bf16[2,80,2048]{2,1,0:T(8,128)(2,1)} %fusion.27), channel_id=1, source_target_pairs={{0,16},{8,24},{16,0},{24,8},{1,17},{9,25},{17,1},{25,9},{2,18},{10... | collective-permute-start | bytes 1966088 | tf_op jit(solution)/shard_map/ppermute | solution.py:227
  15.8 30.0 %collective-permute-start = (bf16[2,80,2048]{2,1,0:T(8,128)(2,1)}, bf16[2,80,2048]{2,1,0:T(8,128)(2,1)}, u32[]{:S(2)}, u32[]{:S(2)}) collective-permute-start(bf16[2,80,2048]{2,1,0:T(8,128)(2,1)} %fusion.27), channel_id=1, source_target_pairs={{0,8},{8,0},{16,24},{24,16},{1,9},{9,1},{17,25},{25,17},{2,10},{10... | collective-permute-start | bytes 1966088 | tf_op jit(solution)/shard_map/ppermute | solution.py:227
  17.3 31.8 %all-to-all-start = ((bf16[4,64,768]{2,1,0:T(8,128)(2,1)}), bf16[4,64,768]{2,1,0:T(8,128)(2,1)S(1)}, u32[]{:S(2)}, u32[]{:S(2)}) async-start(bf16[4,64,768]{2,1,0:T(8,128)(2,1)} %copy.210), calls=%async_computation | async-start | bytes 786432 | tf_op jit(solution)/shard_map/all_to_all | solution.py:362
  21.5 67.7 %all-gather.14.cloned.1.call-start = ((), (), s32[]{:S(2)}) async-start(), calls=%async_computation.13 | async-start | bytes 3538944 | tf_op jit(solution)/shard_map/all_gather | solution.py:372
  49.9 115.7 %all-gather.10.cloned.1.call-start = ((), (), s32[]{:S(2)}) async-start(), calls=%async_computation.7 | async-start | bytes 2949120 | tf_op jit(solution)/shard_map/all_gather | solution.py:402
  52.0 26.2 %collective-permute-start.3 = (bf16[4,64,2048]{2,1,0:T(8,128)(2,1)S(1)}, bf16[4,64,2048]{2,1,0:T(8,128)(2,1)S(1)}, u32[]{:S(2)}, u32[]{:S(2)}) collective-permute-start(bf16[4,64,2048]{2,1,0:T(8,128)(2,1)S(1)} %dynamic-slice_bitcast_fusion.5), channel_id=1, source_target_pairs={{0,8},{8,0},{16,24},{24,16},{1,9},{9,1},{17,25},{25,17},{2,10},{10... | collective-permute-start | bytes 3145736 | tf_op jit(solution)/shard_map/ppermute | solution.py:227
  54.5 46.2 %collective-permute-start.4 = (bf16[4,64,2048]{2,1,0:T(8,128)(2,1)S(1)}, bf16[4,64,2048]{2,1,0:T(8,128)(2,1)}, u32[]{:S(2)}, u32[]{:S(2)}) collective-permute-start(bf16[4,64,2048]{2,1,0:T(8,128)(2,1)S(1)} %dynamic-slice_bitcast_fusion.5), channel_id=1, source_target_pairs={{0,16},{8,24},{16,0},{24,8},{1,17},{9,25},{17,1},{25,9},{2,18},{10... | collective-permute-start | bytes 3145736 | tf_op jit(solution)/shard_map/ppermute | solution.py:227
  55.7 45.0 %collective-permute-start.5 = (bf16[4,64,2048]{2,1,0:T(8,128)(2,1)S(1)}, bf16[4,64,2048]{2,1,0:T(8,128)(2,1)}, u32[]{:S(2)}, u32[]{:S(2)}) collective-permute-start(bf16[4,64,2048]{2,1,0:T(8,128)(2,1)S(1)} %dynamic-slice_bitcast_fusion.5), channel_id=1, source_target_pairs={{0,24},{8,16},{16,8},{24,0},{1,25},{9,17},{17,9},{25,1},{2,26},{10... | collective-permute-start | bytes 3145736 | tf_op jit(solution)/shard_map/ppermute | solution.py:227
  104.7 41.5 %collective-permute-start.9 = (bf16[176,2048]{1,0:T(8,128)(2,1)}, bf16[176,2048]{1,0:T(8,128)(2,1)}, u32[]{:S(2)}, u32[]{:S(2)}) collective-permute-start(bf16[176,2048]{1,0:T(8,128)(2,1)} %param.21), channel_id=1, source_target_pairs={{0,8},{8,0},{16,24},{24,16},{1,9},{9,1},{17,25},{25,17},{2,10},{10... | collective-permute-start | bytes 2162696 | tf_op jit(solution)/shard_map/ppermute | solution.py:227
  106.0 41.4 %collective-permute-start.10 = (bf16[176,2048]{1,0:T(8,128)(2,1)}, bf16[176,2048]{1,0:T(8,128)(2,1)}, u32[]{:S(2)}, u32[]{:S(2)}) collective-permute-start(bf16[176,2048]{1,0:T(8,128)(2,1)} %param.21), channel_id=1, source_target_pairs={{0,16},{8,24},{16,0},{24,8},{1,17},{9,25},{17,1},{25,9},{2,18},{10... | collective-permute-start | bytes 2162696 | tf_op jit(solution)/shard_map/ppermute | solution.py:227
  109.0 56.6 %all-to-all-start.1 = ((bf16[8,64,1408]{2,1,0:T(8,128)(2,1)}), bf16[8,64,1408]{2,1,0:T(8,128)(2,1)}, u32[]{:S(2)}, u32[]{:S(2)}) async-start(bf16[8,64,1408]{2,1,0:T(8,128)(2,1)} %copy.216), calls=%async_computation.1 | async-start | bytes 2883584 | tf_op jit(solution)/shard_map/all_to_all | solution.py:393
  114.1 109.9 %all-gather.16.cloned.1.call-start = ((), (), s32[]{:S(2)}) async-start(), calls=%async_computation.14 | async-start | bytes 5898240 | tf_op jit(solution)/shard_map/all_gather | solution.py:431
  118.6 26.6 %collective-permute-start.7 = (bf16[2,80,512]{2,1,0:T(8,128)(2,1)}, bf16[2,80,512]{2,1,0:T(8,128)(2,1)S(1)}, u32[]{:S(2)}, u32[]{:S(2)}) collective-permute-start(bf16[2,80,512]{2,1,0:T(8,128)(2,1)} %unstack.43), channel_id=1, source_target_pairs={{0,16},{8,24},{16,0},{24,8},{1,17},{9,25},{17,1},{25,9},{2,18},{10... | collective-permute-start | bytes 491528 | tf_op jit(solution)/shard_map/ppermute | solution.py:227
  120.6 24.6 %collective-permute-start.8 = (bf16[2,80,512]{2,1,0:T(8,128)(2,1)}, bf16[2,80,512]{2,1,0:T(8,128)(2,1)}, u32[]{:S(2)}, u32[]{:S(2)}) collective-permute-start(bf16[2,80,512]{2,1,0:T(8,128)(2,1)} %unstack.45), channel_id=1, source_target_pairs={{0,8},{8,0},{16,24},{24,16},{1,9},{9,1},{17,25},{25,17},{2,10},{10... | collective-permute-start | bytes 491528 | tf_op jit(solution)/shard_map/ppermute | solution.py:227
  126.7 21.9 %collective-permute-start.11 = (bf16[176,2048]{1,0:T(8,128)(2,1)}, bf16[176,2048]{1,0:T(8,128)(2,1)S(1)}, u32[]{:S(2)}, u32[]{:S(2)}) collective-permute-start(bf16[176,2048]{1,0:T(8,128)(2,1)} %param.21), channel_id=1, source_target_pairs={{0,24},{8,16},{16,8},{24,0},{1,25},{9,17},{17,9},{25,1},{2,26},{10... | collective-permute-start | bytes 2162696 | tf_op jit(solution)/shard_map/ppermute | solution.py:227
  165.7 112.3 %all-gather.18.cloned.1.call-start = ((), (), s32[]{:S(2)}) async-start(), calls=%async_computation.15 | async-start | bytes 5898240 | tf_op jit(solution)/shard_map/all_gather | solution.py:453
  175.7 42.8 %collective-permute-start.14 = (bf16[1024,2048]{1,0:T(8,128)(2,1)}, bf16[1024,2048]{1,0:T(8,128)(2,1)}, u32[]{:S(2)}, u32[]{:S(2)}) collective-permute-start(bf16[1024,2048]{1,0:T(8,128)(2,1)} %bitcast.36), channel_id=1, source_target_pairs={{0,1},{1,0},{2,3},{3,2},{4,5},{5,4},{6,7},{7,6},{8,9},{9,8},{10,11... | collective-permute-start | bytes 12582920 | tf_op jit(solution)/shard_map/ppermute | solution.py:227
  175.9 34.3 %collective-permute-start.12 = (bf16[8,64,1408]{2,1,0:T(8,128)(2,1)}, bf16[8,64,1408]{2,1,0:T(8,128)(2,1)}, u32[]{:S(2)}, u32[]{:S(2)}) collective-permute-start(bf16[8,64,1408]{2,1,0:T(8,128)(2,1)} %all-to-all-done.1), channel_id=1, source_target_pairs={{0,8},{8,0},{16,24},{24,16},{1,9},{9,1},{17,25},{25,17},{2,10},{10... | collective-permute-start | bytes 4325384 | tf_op jit(solution)/shard_map/ppermute | solution.py:227
  177.5 33.9 %collective-permute-start.13 = (bf16[8,64,1408]{2,1,0:T(8,128)(2,1)}, bf16[8,64,1408]{2,1,0:T(8,128)(2,1)}, u32[]{:S(2)}, u32[]{:S(2)}) collective-permute-start(bf16[8,64,1408]{2,1,0:T(8,128)(2,1)} %all-to-all-done.1), channel_id=1, source_target_pairs={{0,16},{8,24},{16,0},{24,8},{1,17},{9,25},{17,1},{25,9},{2,18},{10... | collective-permute-start | bytes 4325384 | tf_op jit(solution)/shard_map/ppermute | solution.py:227
  223.9 148.2 %reduce-scatter.5.cloned.1.call-start = ((), (), s32[]{:S(2)}) async-start(), calls=%async_computation.8 | async-start | bytes 5898240 | tf_op jit(solution)/shard_map/reduce_scatter | solution.py:478
  224.4 33.9 %collective-permute-start.15 = (bf16[8,64,1408]{2,1,0:T(8,128)(2,1)}, bf16[8,64,1408]{2,1,0:T(8,128)(2,1)S(1)}, u32[]{:S(2)}, u32[]{:S(2)}) collective-permute-start(bf16[8,64,1408]{2,1,0:T(8,128)(2,1)} %all-to-all-done.1), channel_id=1, source_target_pairs={{0,24},{8,16},{16,8},{24,0},{1,25},{9,17},{17,9},{25,1},{2,26},{10... | collective-permute-start | bytes 4325384 | tf_op jit(solution)/shard_map/ppermute | solution.py:227
  259.5 53.8 %collective-permute-start.16 = (bf16[4,4,64,512]{3,2,1,0:T(8,128)(2,1)}, bf16[4,4,64,512]{3,2,1,0:T(8,128)(2,1)}, u32[]{:S(2)}, u32[]{:S(2)}) collective-permute-start(bf16[4,4,64,512]{3,2,1,0:T(8,128)(2,1)} %dynamic-slice_bitcast_fusion.4), channel_id=1, source_target_pairs={{0,8},{8,0},{16,24},{24,16},{1,9},{9,1},{17,25},{25,17},{2,10},{10... | collective-permute-start | bytes 3145736 | tf_op jit(solution)/shard_map/ppermute | solution.py:227
  260.1 53.2 %collective-permute-start.17 = (bf16[4,4,64,512]{3,2,1,0:T(8,128)(2,1)}, bf16[4,4,64,512]{3,2,1,0:T(8,128)(2,1)}, u32[]{:S(2)}, u32[]{:S(2)}) collective-permute-start(bf16[4,4,64,512]{3,2,1,0:T(8,128)(2,1)} %dynamic-slice_bitcast_fusion.4), channel_id=1, source_target_pairs={{0,16},{8,24},{16,0},{24,8},{1,17},{9,25},{17,1},{25,9},{2,18},{10... | collective-permute-start | bytes 3145736 | tf_op jit(solution)/shard_map/ppermute | solution.py:227
  261.6 51.7 %collective-permute-start.18 = (bf16[4,4,64,512]{3,2,1,0:T(8,128)(2,1)}, bf16[4,4,64,512]{3,2,1,0:T(8,128)(2,1)}, u32[]{:S(2)}, u32[]{:S(2)}) collective-permute-start(bf16[4,4,64,512]{3,2,1,0:T(8,128)(2,1)} %dynamic-slice_bitcast_fusion.4), channel_id=1, source_target_pairs={{0,24},{8,16},{16,8},{24,0},{1,25},{9,17},{17,9},{25,1},{2,26},{10... | collective-permute-start | bytes 3145736 | tf_op jit(solution)/shard_map/ppermute | solution.py:227
  313.3 193.7 %reduce-scatter.7.cloned.1.call-start = ((), (), s32[]{:S(2)}) async-start(), calls=%async_computation.9 | async-start | bytes 5898240 | tf_op jit(solution)/shard_map/reduce_scatter | solution.py:510
  313.3 42.6 %collective-permute-start.24 = (bf16[2,80,2048]{2,1,0:T(8,128)(2,1)S(1)}, bf16[2,80,2048]{2,1,0:T(8,128)(2,1)S(1)}, u32[]{:S(2)}, u32[]{:S(2)}) collective-permute-start(bf16[2,80,2048]{2,1,0:T(8,128)(2,1)S(1)} %get-tuple-element.127), channel_id=1, source_target_pairs={{0,24},{8,16},{16,8},{24,0},{1,25},{9,17},{17,9},{25,1},{2,26},{10... | collective-permute-start | bytes 1966088 | tf_op jit(solution)/shard_map/ppermute | solution.py:227
  315.8 43.3 %collective-permute-start.23 = (bf16[2,80,2048]{2,1,0:T(8,128)(2,1)S(1)}, bf16[2,80,2048]{2,1,0:T(8,128)(2,1)S(1)}, u32[]{:S(2)}, u32[]{:S(2)}) collective-permute-start(bf16[2,80,2048]{2,1,0:T(8,128)(2,1)S(1)} %get-tuple-element.127), channel_id=1, source_target_pairs={{0,16},{8,24},{16,0},{24,8},{1,17},{9,25},{17,1},{25,9},{2,18},{10... | collective-permute-start | bytes 1966088 | tf_op jit(solution)/shard_map/ppermute | solution.py:227
  316.3 42.7 %collective-permute-start.22 = (bf16[2,80,2048]{2,1,0:T(8,128)(2,1)S(1)}, bf16[2,80,2048]{2,1,0:T(8,128)(2,1)S(1)}, u32[]{:S(2)}, u32[]{:S(2)}) collective-permute-start(bf16[2,80,2048]{2,1,0:T(8,128)(2,1)S(1)} %get-tuple-element.127), channel_id=1, source_target_pairs={{0,8},{8,0},{16,24},{24,16},{1,9},{9,1},{17,25},{25,17},{2,10},{10... | collective-permute-start | bytes 1966088 | tf_op jit(solution)/shard_map/ppermute | solution.py:227
  320.1 40.7 %collective-permute-start.21 = (bf16[4,4,256,512]{3,2,1,0:T(8,128)(2,1)S(1)}, bf16[4,4,256,512]{3,2,1,0:T(8,128)(2,1)S(1)}, u32[]{:S(2)}, u32[]{:S(2)}) collective-permute-start(bf16[4,4,256,512]{3,2,1,0:T(8,128)(2,1)S(1)} %pad_maximum_fusion), channel_id=1, source_target_pairs={{0,1},{1,0},{2,3},{3,2},{4,5},{5,4},{6,7},{7,6},{8,9},{9,8},{10,11... | collective-permute-start | bytes 12582920 | tf_op jit(solution)/shard_map/ppermute | solution.py:227
  335.0 41.3 %collective-permute-start.19 = (bf16[2,8,32,1408]{3,2,1,0:T(8,128)(2,1)}, bf16[2,8,32,1408]{3,2,1,0:T(8,128)(2,1)}, u32[]{:S(2)}, u32[]{:S(2)}) collective-permute-start(bf16[2,8,32,1408]{3,2,1,0:T(8,128)(2,1)} %pad_maximum_fusion.7), channel_id=1, source_target_pairs={{0,8},{8,0},{16,24},{24,16},{1,9},{9,1},{17,25},{25,17},{2,10},{10... | collective-permute-start | bytes 4325384 | tf_op jit(solution)/shard_map/ppermute | solution.py:227
  355.9 33.8 %collective-permute-start.20 = (bf16[2,8,32,1408]{3,2,1,0:T(8,128)(2,1)}, bf16[2,8,32,1408]{3,2,1,0:T(8,128)(2,1)}, u32[]{:S(2)}, u32[]{:S(2)}) collective-permute-start(bf16[2,8,32,1408]{3,2,1,0:T(8,128)(2,1)} %pad_maximum_fusion.8), channel_id=1, source_target_pairs={{0,16},{8,24},{16,0},{24,8},{1,17},{9,25},{17,1},{25,9},{2,18},{10... | collective-permute-start | bytes 4325384 | tf_op jit(solution)/shard_map/ppermute | solution.py:227
  389.7 152.6 %reduce-scatter.9.cloned.1.call-start = ((), (), s32[]{:S(2)}) async-start(), calls=%async_computation.10 | async-start | bytes 2359296 | tf_op jit(solution)/shard_map/reduce_scatter | solution.py:549
  392.0 33.4 %collective-permute-start.28 = (bf16[1,8,32,1408]{3,2,1,0:T(8,128)(2,1)S(1)}, bf16[1,8,32,1408]{3,2,1,0:T(8,128)(2,1)S(1)}, u32[]{:S(2)}, u32[]{:S(2)}) collective-permute-start(bf16[1,8,32,1408]{3,2,1,0:T(8,128)(2,1)S(1)} %fusion.47), channel_id=1, source_target_pairs={{0,16},{8,24},{16,0},{24,8},{1,17},{9,25},{17,1},{25,9},{2,18},{10... | collective-permute-start | bytes 2162696 | tf_op jit(solution)/shard_map/ppermute | solution.py:227
  395.1 30.3 %collective-permute-start.29 = (bf16[1,8,32,1408]{3,2,1,0:T(8,128)(2,1)S(1)}, bf16[1,8,32,1408]{3,2,1,0:T(8,128)(2,1)S(1)}, u32[]{:S(2)}, u32[]{:S(2)}) collective-permute-start(bf16[1,8,32,1408]{3,2,1,0:T(8,128)(2,1)S(1)} %fusion.48), channel_id=1, source_target_pairs={{0,8},{8,0},{16,24},{24,16},{1,9},{9,1},{17,25},{25,17},{2,10},{10... | collective-permute-start | bytes 2162696 | tf_op jit(solution)/shard_map/ppermute | solution.py:227
  404.2 21.1 %collective-permute-start.27 = (bf16[2,80,512]{2,1,0:T(8,128)(2,1)S(1)}, bf16[2,80,512]{2,1,0:T(8,128)(2,1)S(1)}, u32[]{:S(2)}, u32[]{:S(2)}) collective-permute-start(bf16[2,80,512]{2,1,0:T(8,128)(2,1)S(1)} %get-tuple-element.231), channel_id=1, source_target_pairs={{0,24},{8,16},{16,8},{24,0},{1,25},{9,17},{17,9},{25,1},{2,26},{10... | collective-permute-start | bytes 491528 | tf_op jit(solution)/shard_map/ppermute | solution.py:227
  404.8 20.5 %collective-permute-start.26 = (bf16[2,80,512]{2,1,0:T(8,128)(2,1)S(1)}, bf16[2,80,512]{2,1,0:T(8,128)(2,1)S(1)}, u32[]{:S(2)}, u32[]{:S(2)}) collective-permute-start(bf16[2,80,512]{2,1,0:T(8,128)(2,1)S(1)} %get-tuple-element.230), channel_id=1, source_target_pairs={{0,16},{8,24},{16,0},{24,8},{1,17},{9,25},{17,1},{25,9},{2,18},{10... | collective-permute-start | bytes 491528 | tf_op jit(solution)/shard_map/ppermute | solution.py:227
  406.5 18.9 %collective-permute-start.25 = (bf16[2,80,512]{2,1,0:T(8,128)(2,1)S(1)}, bf16[2,80,512]{2,1,0:T(8,128)(2,1)S(1)}, u32[]{:S(2)}, u32[]{:S(2)}) collective-permute-start(bf16[2,80,512]{2,1,0:T(8,128)(2,1)S(1)} %get-tuple-element.229), channel_id=1, source_target_pairs={{0,8},{8,0},{16,24},{24,16},{1,9},{9,1},{17,25},{25,17},{2,10},{10... | collective-permute-start | bytes 491528 | tf_op jit(solution)/shard_map/ppermute | solution.py:227
  433.9 27.4 %collective-permute-start.30 = (bf16[176,2048]{1,0:T(8,128)(2,1)}, bf16[176,2048]{1,0:T(8,128)(2,1)}, u32[]{:S(2)}, u32[]{:S(2)}) collective-permute-start(bf16[176,2048]{1,0:T(8,128)(2,1)} %get-tuple-element.142), channel_id=1, source_target_pairs={{0,8},{8,0},{16,24},{24,16},{1,9},{9,1},{17,25},{25,17},{2,10},{10... | collective-permute-start | bytes 2162696 | tf_op jit(solution)/shard_map/ppermute | solution.py:227
  434.7 79.2 %collective-permute-start.42 = (bf16[176,2048]{1,0:T(8,128)(2,1)}, bf16[176,2048]{1,0:T(8,128)(2,1)}, u32[]{:S(2)}, u32[]{:S(2)}) collective-permute-start(bf16[176,2048]{1,0:T(8,128)(2,1)} %get-tuple-element.155), channel_id=1, source_target_pairs={{0,16},{8,24},{16,0},{24,8},{1,17},{9,25},{17,1},{25,9},{2,18},{10... | collective-permute-start | bytes 2162696 | tf_op jit(solution)/shard_map/ppermute | solution.py:227
  435.0 78.9 %collective-permute-start.43 = (bf16[176,2048]{1,0:T(8,128)(2,1)}, bf16[176,2048]{1,0:T(8,128)(2,1)}, u32[]{:S(2)}, u32[]{:S(2)}) collective-permute-start(bf16[176,2048]{1,0:T(8,128)(2,1)} %get-tuple-element.156), channel_id=1, source_target_pairs={{0,24},{8,16},{16,8},{24,0},{1,25},{9,17},{17,9},{25,1},{2,26},{10... | collective-permute-start | bytes 2162696 | tf_op jit(solution)/shard_map/ppermute | solution.py:227
  440.2 53.4 %all-to-all-start.2 = ((bf16[8,64,1408]{2,1,0:T(8,128)(2,1)}), bf16[8,64,1408]{2,1,0:T(8,128)(2,1)}, u32[]{:S(2)}, u32[]{:S(2)}) async-start(bf16[8,64,1408]{2,1,0:T(8,128)(2,1)} %pad_maximum_fusion.9), calls=%async_computation.4 | async-start | bytes 2883584 | tf_op jit(solution)/shard_map/all_to_all | solution.py:546
  444.5 99.4 %reduce-scatter.11.cloned.1.call-start = ((), (), s32[]{:S(2)}) async-start(), calls=%async_computation.11 | async-start | bytes 2359296 | tf_op jit(solution)/shard_map/reduce_scatter | solution.py:576
  475.6 16.5 %collective-permute-start.37 = (bf16[4,2,80,256]{3,2,0,1:T(8,128)(2,1)S(1)}, bf16[4,2,80,256]{3,2,0,1:T(8,128)(2,1)S(1)}, u32[]{:S(2)}, u32[]{:S(2)}) collective-permute-start(bf16[4,2,80,256]{3,2,0,1:T(8,128)(2,1)S(1)} %get-tuple-element.207), channel_id=1, source_target_pairs={{0,16},{8,24},{16,0},{24,8},{1,17},{9,25},{17,1},{25,9},{2,18},{10... | collective-permute-start | bytes 983048 | tf_op jit(solution)/shard_map/ppermute | solution.py:227
  495.3 17.5 %collective-permute-start.41 = (bf16[2,80,256]{2,1,0:T(8,128)(2,1)}, bf16[2,80,256]{2,1,0:T(8,128)(2,1)}, u32[]{:S(2)}, u32[]{:S(2)}) collective-permute-start(bf16[2,80,256]{2,1,0:T(8,128)(2,1)} %get-tuple-element.241), channel_id=1, source_target_pairs={{0,6},{1,7},{2,4},{3,5},{4,2},{5,3},{6,0},{7,1},{8,14},{9,15},{10,... | collective-permute-start | bytes 245768 | tf_op jit(solution)/shard_map/ppermute | solution.py:227
  496.2 16.6 %collective-permute-start.40 = (bf16[2,80,256]{2,1,0:T(8,128)(2,1)}, bf16[2,80,256]{2,1,0:T(8,128)(2,1)}, u32[]{:S(2)}, u32[]{:S(2)}) collective-permute-start(bf16[2,80,256]{2,1,0:T(8,128)(2,1)} %get-tuple-element.242), channel_id=1, source_target_pairs={{0,4},{1,5},{2,6},{3,7},{4,0},{5,1},{6,2},{7,3},{8,12},{9,13},{10,... | collective-permute-start | bytes 245768 | tf_op jit(solution)/shard_map/ppermute | solution.py:227
  496.2 16.6 %collective-permute-start.39 = (bf16[2,80,256]{2,1,0:T(8,128)(2,1)S(1)}, bf16[2,80,256]{2,1,0:T(8,128)(2,1)}, u32[]{:S(2)}, u32[]{:S(2)}) collective-permute-start(bf16[2,80,256]{2,1,0:T(8,128)(2,1)S(1)} %get-tuple-element.240), channel_id=1, source_target_pairs={{0,2},{1,3},{2,0},{3,1},{4,6},{5,7},{6,4},{7,5},{8,10},{9,11},{10,... | collective-permute-start | bytes 245768 | tf_op jit(solution)/shard_map/ppermute | solution.py:227
  (85 other events, 784.1 us)
Sparse Core Ops, SparseCore 0:
  9.6 31.7 all-gather.11
  50.0 39.1 all-gather.13
  100.8 51.6 all-gather.9
  165.8 54.8 all-gather.15
  224.1 53.8 all-gather.17
  313.4 58.6 reduce-scatter.4
  389.8 58.4 reduce-scatter.6
  450.6 48.8 reduce-scatter.8
  507.1 36.7 reduce-scatter.10

commit v5 on v4

--- a/solution.py
+++ b/solution.py
@@ -100,7 +100,7 @@
 
 
 def heads_per_step(slots):
-    return max(1, min(4, 4 * 2560 // slots))
+    return max(1, min(8, 8 * 2560 // slots))
 
 
 def attend(query, keyval, own, keys):

time: 573 us -> 573 us (level)
  transfers between devices with their start and end apart: 66 -> 66, of which waited for: 26 -> 27; matrix products, arithmetic and copies ran while one was open for 41% -> 41% of each run, Pallas kernels for 8% -> 7%
where the time goes in v5:
time: 573 us; the launch traced here: 564 us
  waiting for transfers between devices  184 us (32%)
  matrix products  90.9 us (16%)
  local copies, waits for them, and re-layouts  87.8 us (15%)
  starting transfers between devices  77.6 us (14%)
  other arithmetic  66.3 us (12%)
  Pallas kernels  42 us (7%)
  between operations  15.8 us (3%)
    ppermute x54, waiting for transfers between devices, exchange(): return lax.ppermute(values, axis, [(i, i ^ offset) for i in range(members)])  132 us
    dot_general x15, matrix products, dot32(): lax.dot_general(left, right, (dims, ((), ())), preferred_element_type=jnp...  90.9 us
    ppermute x54, starting transfers between devices, exchange(): return lax.ppermute(values, axis, [(i, i ^ offset) for i in range(members)])  63 us
    pallas_call x2, Pallas kernels, attend_back(): pl.pallas_call(functools.partial(attend_back_kernel, heads, min(512, slot...  28.3 us
    all_to_all x1, waiting for transfers between devices, on_device(): ff_rows = lax.all_to_all(ff_blocks, 'row', 0, 0)  16.9 us
    pallas_call x1, Pallas kernels, attend(): pl.pallas_call(functools.partial(attend_kernel, heads), grid=(batches, HQ...  13.7 us
  transfers between devices with their start and end apart: 66, of which 27 were waited for; matrix products, arithmetic and copies ran while one was open for 41% of the time, Pallas kernels for 7%

profile of v5, /device:TPU:0, one launch (start us, length us, event | category | flops | bytes accessed | tf_op | source)
XLA Modules:
  0.0 564.5 jit_solution(14119008519943645395)
XLA Ops:
  11.4 3.9 collective-permute-start.2
  17.3 4.2 all-to-all-start
  24.9 6.3 %collective-permute-done.2 = bf16[2,80,2048]{2,1,0:T(8,128)(2,1)} collective-permute-done((bf16[2,80,2048]{2,1,0:T(8,128)(2,1)}, bf16[2,80,2048]{2,1,0:T(8,128)(2,1)}, u32[]{:S(2)}, u32[]{:S(2)}) %collective-permute-start.2) | collective-permute-done | bytes 655392 | tf_op jit(solution)/shard_map/ppermute | solution.py:227
  31.2 14.1 %collective-permute-done.1 = bf16[2,80,2048]{2,1,0:T(8,128)(2,1)} collective-permute-done((bf16[2,80,2048]{2,1,0:T(8,128)(2,1)}, bf16[2,80,2048]{2,1,0:T(8,128)(2,1)}, u32[]{:S(2)}, u32[]{:S(2)}) %collective-permute-start.1) | collective-permute-done | bytes 655392 | tf_op jit(solution)/shard_map/ppermute | solution.py:227
  45.8 3.3 pad_maximum_fusion.3
  56.6 21.6 %collective-permute-done.3 = bf16[4,64,2048]{2,1,0:T(8,128)(2,1)S(1)} collective-permute-done((bf16[4,64,2048]{2,1,0:T(8,128)(2,1)S(1)}, bf16[4,64,2048]{2,1,0:T(8,128)(2,1)S(1)}, u32[]{:S(2)}, u32[]{:S(2)}) %collective-permute-start.3) | collective-permute-done | bytes 1048608 | tf_op jit(solution)/shard_map/ppermute | solution.py:227
  78.2 11.0 %all-gather.14.cloned.1.call-done = bf16[32,64,768]{2,1,0:T(8,128)(2,1)} async-done(((bf16[4,64,768]{2,1,0:T(8,128)(2,1)}), bf16[32,64,768]{2,1,0:T(8,128)(2,1)}) %all-gather.14.cloned.1.call-update) | async-done | bytes 3145744 | tf_op jit(solution)/shard_map/all_gather | solution.py:372
  89.2 4.9 fusion.6
  96.5 4.2 collective-permute-done.4
  109.0 5.0 all-to-all-start.1
  127.0 18.2 %collective-permute-done.7 = bf16[2,80,512]{2,1,0:T(8,128)(2,1)S(1)} collective-permute-done((bf16[2,80,512]{2,1,0:T(8,128)(2,1)}, bf16[2,80,512]{2,1,0:T(8,128)(2,1)S(1)}, u32[]{:S(2)}, u32[]{:S(2)}) %collective-permute-start.7) | collective-permute-done | bytes 163872 | tf_op jit(solution)/shard_map/ppermute | solution.py:227
  148.7 16.9 %all-to-all-done.1 = bf16[8,64,1408]{2,1,0:T(8,128)(2,1)} async-done(((bf16[8,64,1408]{2,1,0:T(8,128)(2,1)}), bf16[8,64,1408]{2,1,0:T(8,128)(2,1)}, u32[]{:S(2)}, u32[]{:S(2)}) %all-to-all-start.1) | async-done | bytes 1441824 | tf_op jit(solution)/shard_map/all_to_all | solution.py:393
  182.1 13.7 %shard_map.204 = (bf16[2,80,2048]{2,1,0:T(8,128)(2,1)S(1)}, f32[2,80,2048]{2,1,0:T(8,128)S(1)}, f32[2,80,2048]{2,1,0:T(8,128)S(1)}) custom-call(bf16[2,80,2048]{2,1,0:T(8,128)(2,1)S(1)} %pad_maximum_fusion.12.q_ref, bf16[2,2560,256]{2,1,0:T(8,128)(2,1)} %all-gather.10.cloned.1.call-done.kv_ref, s32[2,80,2]{2,1,0:T(8,128)S(1)} %bitcast.385, ...), custom_call_target="tpu_custom_call" | custom-call | flops 3355443200 | bytes 5242880 | tf_op jit(solution)/shard_map/pallas_call | solution.py:111
  196.8 13.4 %collective-permute-done.12 = bf16[8,64,1408]{2,1,0:T(8,128)(2,1)} collective-permute-done((bf16[8,64,1408]{2,1,0:T(8,128)(2,1)}, bf16[8,64,1408]{2,1,0:T(8,128)(2,1)}, u32[]{:S(2)}, u32[]{:S(2)}) %collective-permute-start.12) | collective-permute-done | bytes 1441824 | tf_op jit(solution)/shard_map/ppermute | solution.py:227
  215.3 3.2 fusion.95
  218.5 3.4 multiply_reduce_fusion.1
  225.9 3.3 broadcast_in_dim.145
  231.9 4.3 broadcast_in_dim.142
  236.2 4.7 bitcast_dynamic-update-slice_fusion
  246.1 12.2 %collective-permute-done.15 = bf16[8,64,1408]{2,1,0:T(8,128)(2,1)S(1)} collective-permute-done((bf16[8,64,1408]{2,1,0:T(8,128)(2,1)}, bf16[8,64,1408]{2,1,0:T(8,128)(2,1)S(1)}, u32[]{:S(2)}, u32[]{:S(2)}) %collective-permute-start.15) | collective-permute-done | bytes 1441824 | tf_op jit(solution)/shard_map/ppermute | solution.py:227
  262.9 4.8 constant_dynamic-update-slice_fusion
  267.7 10.2 %all-gather.18.cloned.1.call-done = bf16[16,80,2048]{2,1,0:T(8,128)(2,1)} async-done(((bf16[2,80,2048]{2,1,0:T(8,128)(2,1)}), bf16[16,80,2048]{2,1,0:T(8,128)(2,1)}) %all-gather.18.cloned.1.call-update) | async-done | bytes 5242896 | tf_op jit(solution)/shard_map/all_gather | solution.py:453
  277.9 12.9 %fusion.96 = f32[1280,1408]{0,1:T(8,128)S(1)} fusion(bf16[1280,2048]{1,0:T(8,128)(2,1)} %bitcast.435, bf16[2048,1408]{1,0:T(8,128)(2,1)} %bitcast.53), kind=kOutput, calls=%fused_computation.295 | convolution fusion | flops 7381975040 | bytes 18219008 | tf_op jit(solution)/shard_map/dot_general | solution.py:60
  290.9 9.1 %multiply_convert_fusion.2 = (bf16[1280,704]{0,1:T(8,128)(2,1)S(1)}, bf16[1280,704]{0,1:T(8,128)(2,1)S(1)}, bf16[1280,704]{0,1:T(8,128)(2,1)}) fusion(f32[1280,1408]{0,1:T(8,128)S(1)} %fusion.96, bf16[1280,2048]{1,0:T(8,128)(2,1)} %bitcast.431, bf16[704,2048]{1,0:T(8,128)(2,1)S(1)} %bitcast.396), kind=kOutput, calls=%fused_computation.19 | convolution fusion | flops 3705405440 | bytes 20742144 | tf_op jit(solution)/shard_map/dot_general | solution.py:60
  299.9 13.3 %convolution_convert_fusion.2 = bf16[1280,2048]{1,0:T(8,128)(2,1)} fusion(bf16[2048,1408]{1,0:T(8,128)(2,1)} %bitcast.53, bf16[1280,704]{0,1:T(8,128)(2,1)S(1)} %get-tuple-element.178, bf16[1280,704]{0,1:T(8,128)(2,1)S(1)} %get-tuple-element.177), kind=kOutput, calls=%fused_computation.7 | convolution fusion | flops 7391805440 | bytes 14614528 | tf_op jit(solution)/shard_map/dot_general | solution.py:60
  316.9 3.5 pad_maximum_fusion
  320.6 10.3 %convolution_convert_fusion = bf16[2048,1408]{1,0:T(8,128)(2,1)S(1)} fusion(bf16[1280,2048]{1,0:T(8,128)(2,1)} %bitcast.436, bf16[1280,704]{0,1:T(8,128)(2,1)S(1)} %copy-done.63, bf16[1280,704]{0,1:T(8,128)(2,1)S(1)} %copy-done.61), kind=kOutput, calls=%fused_computation.5 | convolution fusion | flops 7392067584 | bytes 14614528 | tf_op jit(solution)/shard_map/dot_general | solution.py:60
  336.6 6.1 %convolution_convert_fusion.1 = bf16[1280,2048]{1,0:T(8,128)(2,1)} fusion(bf16[1280,704]{0,1:T(8,128)(2,1)S(1)} %copy-done.59, bf16[704,2048]{1,0:T(8,128)(2,1)S(1)} %bitcast.397), kind=kOutput, calls=%fused_computation.6 | convolution fusion | flops 3693608960 | bytes 9928704 | tf_op jit(solution)/shard_map/dot_general | solution.py:60
  342.6 4.1 convolution_convert_fusion.3
  348.0 4.1 broadcast_in_dim.150
  352.2 3.7 maximum_dynamic-update-slice_fusion
  363.2 8.9 %reduce-scatter.5.cloned.1.call-done = bf16[1,2,80,2048]{3,2,1,0:T(8,128)(2,1)} async-done(((bf16[8,2,80,2048]{3,2,1,0:T(8,128)(2,1)}), bf16[1,2,80,2048]{3,2,1,0:T(8,128)(2,1)}) %reduce-scatter.5.cloned.1.call-update) | async-done | bytes 655376 | tf_op jit(solution)/shard_map/reduce_scatter | solution.py:478
  376.2 13.7 %collective-permute-done.20 = bf16[2,8,32,1408]{3,2,1,0:T(8,128)(2,1)} collective-permute-done((bf16[2,8,32,1408]{3,2,1,0:T(8,128)(2,1)}, bf16[2,8,32,1408]{3,2,1,0:T(8,128)(2,1)}, u32[]{:S(2)}, u32[]{:S(2)}) %collective-permute-start.20) | collective-permute-done | bytes 1441824 | tf_op jit(solution)/shard_map/ppermute | solution.py:227
  397.7 6.4 %fusion.22.g_ref = bf16[2,80,2048]{2,1,0:T(8,128)(2,1)S(1)} fusion(bf16[2,80,2048]{2,1,0:T(8,128)(2,1)S(1)} %fusion.84, bf16[2048,2048]{1,0:T(8,128)(2,1)} %bitcast.48), kind=kOutput, calls=%fused_computation.36 | convolution fusion | flops 1342504960 | bytes 9699328 | tf_op jit(solution)/shard_map/dot_general | solution.py:60
  407.8 14.1 %shard_map.205 = (bf16[1,80,2048]{2,1,0:T(8,128)(2,1)S(1)}, f32[1,2560,256]{2,1,0:T(8,128)}) custom-call(bf16[2,80,2048]{2,1,0:T(8,128)(2,1)S(1)} %pad_maximum_fusion.12.q_ref, bf16[2,80,2048]{2,1,0:T(8,128)(2,1)S(1)} %fusion.22.g_ref, f32[2,80,2048]{2,1,0:T(8,128)S(1)} %get-tuple-element.130.wide_ref, f32[2,80,2048]{2,1,0:T(8,128)S(1)} %copy-done.1, ...), custom_call_target="tpu_custom_call" | custom-call | flops 4194304000 | bytes 2621440 | tf_op jit(solution)/shard_map/pallas_call | solution.py:191
  428.5 3.2 bitcast_convert_fusion.1
  439.0 4.3 all-to-all-start.2
  444.7 14.2 %shard_map.206 = (bf16[1,80,2048]{2,1,0:T(8,128)(2,1)S(1)}, f32[1,2560,256]{2,1,0:T(8,128)}) custom-call(bf16[2,80,2048]{2,1,0:T(8,128)(2,1)S(1)} %pad_maximum_fusion.12.q_ref, bf16[2,80,2048]{2,1,0:T(8,128)(2,1)S(1)} %fusion.22.g_ref, f32[2,80,2048]{2,1,0:T(8,128)S(1)} %get-tuple-element.130.wide_ref, f32[2,80,2048]{2,1,0:T(8,128)S(1)} %copy-done.2, ...), custom_call_target="tpu_custom_call" | custom-call | flops 4194304000 | bytes 2621440 | tf_op jit(solution)/shard_map/pallas_call | solution.py:191
  467.5 3.5 collective-permute-done.33
  471.5 3.0 collective-permute-done.32
  477.2 3.2 bitcast_convert_fusion
  481.6 9.4 %collective-permute-done.37 = bf16[4,2,80,256]{3,2,0,1:T(8,128)(2,1)S(1)} collective-permute-done((bf16[4,2,80,256]{3,2,0,1:T(8,128)(2,1)S(1)}, bf16[4,2,80,256]{3,2,0,1:T(8,128)(2,1)S(1)}, u32[]{:S(2)}, u32[]{:S(2)}) %collective-permute-start.37) | collective-permute-done | bytes 327712 | tf_op jit(solution)/shard_map/ppermute | solution.py:227
  494.1 2.9 collective-permute-start.39
  505.7 4.4 fusion.30
  519.4 7.7 %fusion.36 = (f32[2,80]{1,0:T(2,128)S(1)}, f32[2,80,2048]{2,1,0:T(8,128)}) fusion(bf16[2,80,2048]{2,1,0:T(8,128)(2,1)S(1)} %copy-done.8, f32[2,80]{1,0:T(2,128)S(1)} %copy-done.48, f32[2,80,2048]{2,1,0:T(8,128)S(1)} %fusion.44, bf16[4,2,80,512]{3,2,1,0:T(8,128)(2,1)S(1)} %copy-done.28, bf16[4,2048,512]{2,1,0:T(8,128)(2,1)} %bitcast.79), kind=kOutput, calls=%fused_computation.75 | convolution fusion | flops 1343815552 | bytes 12322048 | tf_op jit(solution)/shard_map/dot_general | solution.py:60
  528.2 3.1 convert_add_fusion.6
  540.5 4.0 reduce-scatter.11.cloned.1.call-done
  550.5 3.3 fusion.40
  (411 shorter events, 185.7 us)
Async XLA Ops:
  7.2 41.9 %all-gather.12.cloned.1.call-start = ((), (), s32[]{:S(2)}) async-start(), calls=%async_computation.12 | async-start | bytes 2359296 | tf_op jit(solution)/shard_map/all_gather | solution.py:358
  11.4 19.8 %collective-permute-start.2 = (bf16[2,80,2048]{2,1,0:T(8,128)(2,1)}, bf16[2,80,2048]{2,1,0:T(8,128)(2,1)}, u32[]{:S(2)}, u32[]{:S(2)}) collective-permute-start(bf16[2,80,2048]{2,1,0:T(8,128)(2,1)} %fusion.27), channel_id=1, source_target_pairs={{0,24},{8,16},{16,8},{24,0},{1,25},{9,17},{17,9},{25,1},{2,26},{10... | collective-permute-start | bytes 1966088 | tf_op jit(solution)/shard_map/ppermute | solution.py:227
  15.3 30.0 %collective-permute-start.1 = (bf16[2,80,2048]{2,1,0:T(8,128)(2,1)}, bf16[2,80,2048]{2,1,0:T(8,128)(2,1)}, u32[]{:S(2)}, u32[]{:S(2)}) collective-permute-start(bf16[2,80,2048]{2,1,0:T(8,128)(2,1)} %fusion.27), channel_id=1, source_target_pairs={{0,16},{8,24},{16,0},{24,8},{1,17},{9,25},{17,1},{25,9},{2,18},{10... | collective-permute-start | bytes 1966088 | tf_op jit(solution)/shard_map/ppermute | solution.py:227
  15.8 30.0 %collective-permute-start = (bf16[2,80,2048]{2,1,0:T(8,128)(2,1)}, bf16[2,80,2048]{2,1,0:T(8,128)(2,1)}, u32[]{:S(2)}, u32[]{:S(2)}) collective-permute-start(bf16[2,80,2048]{2,1,0:T(8,128)(2,1)} %fusion.27), channel_id=1, source_target_pairs={{0,8},{8,0},{16,24},{24,16},{1,9},{9,1},{17,25},{25,17},{2,10},{10... | collective-permute-start | bytes 1966088 | tf_op jit(solution)/shard_map/ppermute | solution.py:227
  17.3 31.8 %all-to-all-start = ((bf16[4,64,768]{2,1,0:T(8,128)(2,1)}), bf16[4,64,768]{2,1,0:T(8,128)(2,1)S(1)}, u32[]{:S(2)}, u32[]{:S(2)}) async-start(bf16[4,64,768]{2,1,0:T(8,128)(2,1)} %copy.210), calls=%async_computation | async-start | bytes 786432 | tf_op jit(solution)/shard_map/all_to_all | solution.py:362
  21.5 67.7 %all-gather.14.cloned.1.call-start = ((), (), s32[]{:S(2)}) async-start(), calls=%async_computation.13 | async-start | bytes 3538944 | tf_op jit(solution)/shard_map/all_gather | solution.py:372
  49.9 115.7 %all-gather.10.cloned.1.call-start = ((), (), s32[]{:S(2)}) async-start(), calls=%async_computation.7 | async-start | bytes 2949120 | tf_op jit(solution)/shard_map/all_gather | solution.py:402
  52.0 26.2 %collective-permute-start.3 = (bf16[4,64,2048]{2,1,0:T(8,128)(2,1)S(1)}, bf16[4,64,2048]{2,1,0:T(8,128)(2,1)S(1)}, u32[]{:S(2)}, u32[]{:S(2)}) collective-permute-start(bf16[4,64,2048]{2,1,0:T(8,128)(2,1)S(1)} %dynamic-slice_bitcast_fusion.5), channel_id=1, source_target_pairs={{0,8},{8,0},{16,24},{24,16},{1,9},{9,1},{17,25},{25,17},{2,10},{10... | collective-permute-start | bytes 3145736 | tf_op jit(solution)/shard_map/ppermute | solution.py:227
  54.5 46.2 %collective-permute-start.4 = (bf16[4,64,2048]{2,1,0:T(8,128)(2,1)S(1)}, bf16[4,64,2048]{2,1,0:T(8,128)(2,1)}, u32[]{:S(2)}, u32[]{:S(2)}) collective-permute-start(bf16[4,64,2048]{2,1,0:T(8,128)(2,1)S(1)} %dynamic-slice_bitcast_fusion.5), channel_id=1, source_target_pairs={{0,16},{8,24},{16,0},{24,8},{1,17},{9,25},{17,1},{25,9},{2,18},{10... | collective-permute-start | bytes 3145736 | tf_op jit(solution)/shard_map/ppermute | solution.py:227
  55.7 45.0 %collective-permute-start.5 = (bf16[4,64,2048]{2,1,0:T(8,128)(2,1)S(1)}, bf16[4,64,2048]{2,1,0:T(8,128)(2,1)}, u32[]{:S(2)}, u32[]{:S(2)}) collective-permute-start(bf16[4,64,2048]{2,1,0:T(8,128)(2,1)S(1)} %dynamic-slice_bitcast_fusion.5), channel_id=1, source_target_pairs={{0,24},{8,16},{16,8},{24,0},{1,25},{9,17},{17,9},{25,1},{2,26},{10... | collective-permute-start | bytes 3145736 | tf_op jit(solution)/shard_map/ppermute | solution.py:227
  104.7 41.5 %collective-permute-start.9 = (bf16[176,2048]{1,0:T(8,128)(2,1)}, bf16[176,2048]{1,0:T(8,128)(2,1)}, u32[]{:S(2)}, u32[]{:S(2)}) collective-permute-start(bf16[176,2048]{1,0:T(8,128)(2,1)} %param.21), channel_id=1, source_target_pairs={{0,8},{8,0},{16,24},{24,16},{1,9},{9,1},{17,25},{25,17},{2,10},{10... | collective-permute-start | bytes 2162696 | tf_op jit(solution)/shard_map/ppermute | solution.py:227
  106.0 41.4 %collective-permute-start.10 = (bf16[176,2048]{1,0:T(8,128)(2,1)}, bf16[176,2048]{1,0:T(8,128)(2,1)}, u32[]{:S(2)}, u32[]{:S(2)}) collective-permute-start(bf16[176,2048]{1,0:T(8,128)(2,1)} %param.21), channel_id=1, source_target_pairs={{0,16},{8,24},{16,0},{24,8},{1,17},{9,25},{17,1},{25,9},{2,18},{10... | collective-permute-start | bytes 2162696 | tf_op jit(solution)/shard_map/ppermute | solution.py:227
  109.0 56.6 %all-to-all-start.1 = ((bf16[8,64,1408]{2,1,0:T(8,128)(2,1)}), bf16[8,64,1408]{2,1,0:T(8,128)(2,1)}, u32[]{:S(2)}, u32[]{:S(2)}) async-start(bf16[8,64,1408]{2,1,0:T(8,128)(2,1)} %copy.216), calls=%async_computation.1 | async-start | bytes 2883584 | tf_op jit(solution)/shard_map/all_to_all | solution.py:393
  114.1 109.9 %all-gather.16.cloned.1.call-start = ((), (), s32[]{:S(2)}) async-start(), calls=%async_computation.14 | async-start | bytes 5898240 | tf_op jit(solution)/shard_map/all_gather | solution.py:431
  118.6 26.6 %collective-permute-start.7 = (bf16[2,80,512]{2,1,0:T(8,128)(2,1)}, bf16[2,80,512]{2,1,0:T(8,128)(2,1)S(1)}, u32[]{:S(2)}, u32[]{:S(2)}) collective-permute-start(bf16[2,80,512]{2,1,0:T(8,128)(2,1)} %unstack.43), channel_id=1, source_target_pairs={{0,16},{8,24},{16,0},{24,8},{1,17},{9,25},{17,1},{25,9},{2,18},{10... | collective-permute-start | bytes 491528 | tf_op jit(solution)/shard_map/ppermute | solution.py:227
  120.6 24.6 %collective-permute-start.8 = (bf16[2,80,512]{2,1,0:T(8,128)(2,1)}, bf16[2,80,512]{2,1,0:T(8,128)(2,1)}, u32[]{:S(2)}, u32[]{:S(2)}) collective-permute-start(bf16[2,80,512]{2,1,0:T(8,128)(2,1)} %unstack.45), channel_id=1, source_target_pairs={{0,8},{8,0},{16,24},{24,16},{1,9},{9,1},{17,25},{25,17},{2,10},{10... | collective-permute-start | bytes 491528 | tf_op jit(solution)/shard_map/ppermute | solution.py:227
  126.7 21.9 %collective-permute-start.11 = (bf16[176,2048]{1,0:T(8,128)(2,1)}, bf16[176,2048]{1,0:T(8,128)(2,1)S(1)}, u32[]{:S(2)}, u32[]{:S(2)}) collective-permute-start(bf16[176,2048]{1,0:T(8,128)(2,1)} %param.21), channel_id=1, source_target_pairs={{0,24},{8,16},{16,8},{24,0},{1,25},{9,17},{17,9},{25,1},{2,26},{10... | collective-permute-start | bytes 2162696 | tf_op jit(solution)/shard_map/ppermute | solution.py:227
  165.7 112.3 %all-gather.18.cloned.1.call-start = ((), (), s32[]{:S(2)}) async-start(), calls=%async_computation.15 | async-start | bytes 5898240 | tf_op jit(solution)/shard_map/all_gather | solution.py:453
  175.7 42.8 %collective-permute-start.14 = (bf16[1024,2048]{1,0:T(8,128)(2,1)}, bf16[1024,2048]{1,0:T(8,128)(2,1)}, u32[]{:S(2)}, u32[]{:S(2)}) collective-permute-start(bf16[1024,2048]{1,0:T(8,128)(2,1)} %bitcast.36), channel_id=1, source_target_pairs={{0,1},{1,0},{2,3},{3,2},{4,5},{5,4},{6,7},{7,6},{8,9},{9,8},{10,11... | collective-permute-start | bytes 12582920 | tf_op jit(solution)/shard_map/ppermute | solution.py:227
  175.9 34.3 %collective-permute-start.12 = (bf16[8,64,1408]{2,1,0:T(8,128)(2,1)}, bf16[8,64,1408]{2,1,0:T(8,128)(2,1)}, u32[]{:S(2)}, u32[]{:S(2)}) collective-permute-start(bf16[8,64,1408]{2,1,0:T(8,128)(2,1)} %all-to-all-done.1), channel_id=1, source_target_pairs={{0,8},{8,0},{16,24},{24,16},{1,9},{9,1},{17,25},{25,17},{2,10},{10... | collective-permute-start | bytes 4325384 | tf_op jit(solution)/shard_map/ppermute | solution.py:227
  177.5 33.9 %collective-permute-start.13 = (bf16[8,64,1408]{2,1,0:T(8,128)(2,1)}, bf16[8,64,1408]{2,1,0:T(8,128)(2,1)}, u32[]{:S(2)}, u32[]{:S(2)}) collective-permute-start(bf16[8,64,1408]{2,1,0:T(8,128)(2,1)} %all-to-all-done.1), channel_id=1, source_target_pairs={{0,16},{8,24},{16,0},{24,8},{1,17},{9,25},{17,1},{25,9},{2,18},{10... | collective-permute-start | bytes 4325384 | tf_op jit(solution)/shard_map/ppermute | solution.py:227
  223.9 148.2 %reduce-scatter.5.cloned.1.call-start = ((), (), s32[]{:S(2)}) async-start(), calls=%async_computation.8 | async-start | bytes 5898240 | tf_op jit(solution)/shard_map/reduce_scatter | solution.py:478
  224.4 33.9 %collective-permute-start.15 = (bf16[8,64,1408]{2,1,0:T(8,128)(2,1)}, bf16[8,64,1408]{2,1,0:T(8,128)(2,1)S(1)}, u32[]{:S(2)}, u32[]{:S(2)}) collective-permute-start(bf16[8,64,1408]{2,1,0:T(8,128)(2,1)} %all-to-all-done.1), channel_id=1, source_target_pairs={{0,24},{8,16},{16,8},{24,0},{1,25},{9,17},{17,9},{25,1},{2,26},{10... | collective-permute-start | bytes 4325384 | tf_op jit(solution)/shard_map/ppermute | solution.py:227
  259.5 53.8 %collective-permute-start.16 = (bf16[4,4,64,512]{3,2,1,0:T(8,128)(2,1)}, bf16[4,4,64,512]{3,2,1,0:T(8,128)(2,1)}, u32[]{:S(2)}, u32[]{:S(2)}) collective-permute-start(bf16[4,4,64,512]{3,2,1,0:T(8,128)(2,1)} %dynamic-slice_bitcast_fusion.4), channel_id=1, source_target_pairs={{0,8},{8,0},{16,24},{24,16},{1,9},{9,1},{17,25},{25,17},{2,10},{10... | collective-permute-start | bytes 3145736 | tf_op jit(solution)/shard_map/ppermute | solution.py:227
  260.1 53.2 %collective-permute-start.17 = (bf16[4,4,64,512]{3,2,1,0:T(8,128)(2,1)}, bf16[4,4,64,512]{3,2,1,0:T(8,128)(2,1)}, u32[]{:S(2)}, u32[]{:S(2)}) collective-permute-start(bf16[4,4,64,512]{3,2,1,0:T(8,128)(2,1)} %dynamic-slice_bitcast_fusion.4), channel_id=1, source_target_pairs={{0,16},{8,24},{16,0},{24,8},{1,17},{9,25},{17,1},{25,9},{2,18},{10... | collective-permute-start | bytes 3145736 | tf_op jit(solution)/shard_map/ppermute | solution.py:227
  261.6 51.7 %collective-permute-start.18 = (bf16[4,4,64,512]{3,2,1,0:T(8,128)(2,1)}, bf16[4,4,64,512]{3,2,1,0:T(8,128)(2,1)}, u32[]{:S(2)}, u32[]{:S(2)}) collective-permute-start(bf16[4,4,64,512]{3,2,1,0:T(8,128)(2,1)} %dynamic-slice_bitcast_fusion.4), channel_id=1, source_target_pairs={{0,24},{8,16},{16,8},{24,0},{1,25},{9,17},{17,9},{25,1},{2,26},{10... | collective-permute-start | bytes 3145736 | tf_op jit(solution)/shard_map/ppermute | solution.py:227
  313.3 191.1 %reduce-scatter.7.cloned.1.call-start = ((), (), s32[]{:S(2)}) async-start(), calls=%async_computation.9 | async-start | bytes 5898240 | tf_op jit(solution)/shard_map/reduce_scatter | solution.py:510
  313.3 42.6 %collective-permute-start.24 = (bf16[2,80,2048]{2,1,0:T(8,128)(2,1)S(1)}, bf16[2,80,2048]{2,1,0:T(8,128)(2,1)S(1)}, u32[]{:S(2)}, u32[]{:S(2)}) collective-permute-start(bf16[2,80,2048]{2,1,0:T(8,128)(2,1)S(1)} %get-tuple-element.127), channel_id=1, source_target_pairs={{0,24},{8,16},{16,8},{24,0},{1,25},{9,17},{17,9},{25,1},{2,26},{10... | collective-permute-start | bytes 1966088 | tf_op jit(solution)/shard_map/ppermute | solution.py:227
  315.8 43.3 %collective-permute-start.23 = (bf16[2,80,2048]{2,1,0:T(8,128)(2,1)S(1)}, bf16[2,80,2048]{2,1,0:T(8,128)(2,1)S(1)}, u32[]{:S(2)}, u32[]{:S(2)}) collective-permute-start(bf16[2,80,2048]{2,1,0:T(8,128)(2,1)S(1)} %get-tuple-element.127), channel_id=1, source_target_pairs={{0,16},{8,24},{16,0},{24,8},{1,17},{9,25},{17,1},{25,9},{2,18},{10... | collective-permute-start | bytes 1966088 | tf_op jit(solution)/shard_map/ppermute | solution.py:227
  316.3 42.7 %collective-permute-start.22 = (bf16[2,80,2048]{2,1,0:T(8,128)(2,1)S(1)}, bf16[2,80,2048]{2,1,0:T(8,128)(2,1)S(1)}, u32[]{:S(2)}, u32[]{:S(2)}) collective-permute-start(bf16[2,80,2048]{2,1,0:T(8,128)(2,1)S(1)} %get-tuple-element.127), channel_id=1, source_target_pairs={{0,8},{8,0},{16,24},{24,16},{1,9},{9,1},{17,25},{25,17},{2,10},{10... | collective-permute-start | bytes 1966088 | tf_op jit(solution)/shard_map/ppermute | solution.py:227
  320.4 40.5 %collective-permute-start.21 = (bf16[4,4,256,512]{3,2,1,0:T(8,128)(2,1)S(1)}, bf16[4,4,256,512]{3,2,1,0:T(8,128)(2,1)S(1)}, u32[]{:S(2)}, u32[]{:S(2)}) collective-permute-start(bf16[4,4,256,512]{3,2,1,0:T(8,128)(2,1)S(1)} %pad_maximum_fusion), channel_id=1, source_target_pairs={{0,1},{1,0},{2,3},{3,2},{4,5},{5,4},{6,7},{7,6},{8,9},{9,8},{10,11... | collective-permute-start | bytes 12582920 | tf_op jit(solution)/shard_map/ppermute | solution.py:227
  335.0 41.3 %collective-permute-start.19 = (bf16[2,8,32,1408]{3,2,1,0:T(8,128)(2,1)}, bf16[2,8,32,1408]{3,2,1,0:T(8,128)(2,1)}, u32[]{:S(2)}, u32[]{:S(2)}) collective-permute-start(bf16[2,8,32,1408]{3,2,1,0:T(8,128)(2,1)} %pad_maximum_fusion.7), channel_id=1, source_target_pairs={{0,8},{8,0},{16,24},{24,16},{1,9},{9,1},{17,25},{25,17},{2,10},{10... | collective-permute-start | bytes 4325384 | tf_op jit(solution)/shard_map/ppermute | solution.py:227
  355.9 34.1 %collective-permute-start.20 = (bf16[2,8,32,1408]{3,2,1,0:T(8,128)(2,1)}, bf16[2,8,32,1408]{3,2,1,0:T(8,128)(2,1)}, u32[]{:S(2)}, u32[]{:S(2)}) collective-permute-start(bf16[2,8,32,1408]{3,2,1,0:T(8,128)(2,1)} %pad_maximum_fusion.8), channel_id=1, source_target_pairs={{0,16},{8,24},{16,0},{24,8},{1,17},{9,25},{17,1},{25,9},{2,18},{10... | collective-permute-start | bytes 4325384 | tf_op jit(solution)/shard_map/ppermute | solution.py:227
  390.0 150.5 %reduce-scatter.9.cloned.1.call-start = ((), (), s32[]{:S(2)}) async-start(), calls=%async_computation.10 | async-start | bytes 2359296 | tf_op jit(solution)/shard_map/reduce_scatter | solution.py:549
  392.1 32.3 %collective-permute-start.28 = (bf16[1,8,32,1408]{3,2,1,0:T(8,128)(2,1)S(1)}, bf16[1,8,32,1408]{3,2,1,0:T(8,128)(2,1)S(1)}, u32[]{:S(2)}, u32[]{:S(2)}) collective-permute-start(bf16[1,8,32,1408]{3,2,1,0:T(8,128)(2,1)S(1)} %fusion.47), channel_id=1, source_target_pairs={{0,16},{8,24},{16,0},{24,8},{1,17},{9,25},{17,1},{25,9},{2,18},{10... | collective-permute-start | bytes 2162696 | tf_op jit(solution)/shard_map/ppermute | solution.py:227
  395.1 29.2 %collective-permute-start.29 = (bf16[1,8,32,1408]{3,2,1,0:T(8,128)(2,1)S(1)}, bf16[1,8,32,1408]{3,2,1,0:T(8,128)(2,1)S(1)}, u32[]{:S(2)}, u32[]{:S(2)}) collective-permute-start(bf16[1,8,32,1408]{3,2,1,0:T(8,128)(2,1)S(1)} %fusion.48), channel_id=1, source_target_pairs={{0,8},{8,0},{16,24},{24,16},{1,9},{9,1},{17,25},{25,17},{2,10},{10... | collective-permute-start | bytes 2162696 | tf_op jit(solution)/shard_map/ppermute | solution.py:227
  404.2 20.0 %collective-permute-start.27 = (bf16[2,80,512]{2,1,0:T(8,128)(2,1)S(1)}, bf16[2,80,512]{2,1,0:T(8,128)(2,1)S(1)}, u32[]{:S(2)}, u32[]{:S(2)}) collective-permute-start(bf16[2,80,512]{2,1,0:T(8,128)(2,1)S(1)} %get-tuple-element.231), channel_id=1, source_target_pairs={{0,24},{8,16},{16,8},{24,0},{1,25},{9,17},{17,9},{25,1},{2,26},{10... | collective-permute-start | bytes 491528 | tf_op jit(solution)/shard_map/ppermute | solution.py:227
  404.8 19.4 %collective-permute-start.26 = (bf16[2,80,512]{2,1,0:T(8,128)(2,1)S(1)}, bf16[2,80,512]{2,1,0:T(8,128)(2,1)S(1)}, u32[]{:S(2)}, u32[]{:S(2)}) collective-permute-start(bf16[2,80,512]{2,1,0:T(8,128)(2,1)S(1)} %get-tuple-element.230), channel_id=1, source_target_pairs={{0,16},{8,24},{16,0},{24,8},{1,17},{9,25},{17,1},{25,9},{2,18},{10... | collective-permute-start | bytes 491528 | tf_op jit(solution)/shard_map/ppermute | solution.py:227
  406.5 17.7 %collective-permute-start.25 = (bf16[2,80,512]{2,1,0:T(8,128)(2,1)S(1)}, bf16[2,80,512]{2,1,0:T(8,128)(2,1)S(1)}, u32[]{:S(2)}, u32[]{:S(2)}) collective-permute-start(bf16[2,80,512]{2,1,0:T(8,128)(2,1)S(1)} %get-tuple-element.229), channel_id=1, source_target_pairs={{0,8},{8,0},{16,24},{24,16},{1,9},{9,1},{17,25},{25,17},{2,10},{10... | collective-permute-start | bytes 491528 | tf_op jit(solution)/shard_map/ppermute | solution.py:227
  432.8 26.3 %collective-permute-start.30 = (bf16[176,2048]{1,0:T(8,128)(2,1)}, bf16[176,2048]{1,0:T(8,128)(2,1)}, u32[]{:S(2)}, u32[]{:S(2)}) collective-permute-start(bf16[176,2048]{1,0:T(8,128)(2,1)} %get-tuple-element.142), channel_id=1, source_target_pairs={{0,8},{8,0},{16,24},{24,16},{1,9},{9,1},{17,25},{25,17},{2,10},{10... | collective-permute-start | bytes 2162696 | tf_op jit(solution)/shard_map/ppermute | solution.py:227
  433.6 77.6 %collective-permute-start.42 = (bf16[176,2048]{1,0:T(8,128)(2,1)}, bf16[176,2048]{1,0:T(8,128)(2,1)}, u32[]{:S(2)}, u32[]{:S(2)}) collective-permute-start(bf16[176,2048]{1,0:T(8,128)(2,1)} %get-tuple-element.155), channel_id=1, source_target_pairs={{0,16},{8,24},{16,0},{24,8},{1,17},{9,25},{17,1},{25,9},{2,18},{10... | collective-permute-start | bytes 2162696 | tf_op jit(solution)/shard_map/ppermute | solution.py:227
  433.9 77.3 %collective-permute-start.43 = (bf16[176,2048]{1,0:T(8,128)(2,1)}, bf16[176,2048]{1,0:T(8,128)(2,1)}, u32[]{:S(2)}, u32[]{:S(2)}) collective-permute-start(bf16[176,2048]{1,0:T(8,128)(2,1)} %get-tuple-element.156), channel_id=1, source_target_pairs={{0,24},{8,16},{16,8},{24,0},{1,25},{9,17},{17,9},{25,1},{2,26},{10... | collective-permute-start | bytes 2162696 | tf_op jit(solution)/shard_map/ppermute | solution.py:227
  439.0 52.0 %all-to-all-start.2 = ((bf16[8,64,1408]{2,1,0:T(8,128)(2,1)}), bf16[8,64,1408]{2,1,0:T(8,128)(2,1)}, u32[]{:S(2)}, u32[]{:S(2)}) async-start(bf16[8,64,1408]{2,1,0:T(8,128)(2,1)} %pad_maximum_fusion.9), calls=%async_computation.4 | async-start | bytes 2883584 | tf_op jit(solution)/shard_map/all_to_all | solution.py:546
  443.3 101.1 %reduce-scatter.11.cloned.1.call-start = ((), (), s32[]{:S(2)}) async-start(), calls=%async_computation.11 | async-start | bytes 2359296 | tf_op jit(solution)/shard_map/reduce_scatter | solution.py:576
  474.5 16.5 %collective-permute-start.37 = (bf16[4,2,80,256]{3,2,0,1:T(8,128)(2,1)S(1)}, bf16[4,2,80,256]{3,2,0,1:T(8,128)(2,1)S(1)}, u32[]{:S(2)}, u32[]{:S(2)}) collective-permute-start(bf16[4,2,80,256]{3,2,0,1:T(8,128)(2,1)S(1)} %get-tuple-element.207), channel_id=1, source_target_pairs={{0,16},{8,24},{16,0},{24,8},{1,17},{9,25},{17,1},{25,9},{2,18},{10... | collective-permute-start | bytes 983048 | tf_op jit(solution)/shard_map/ppermute | solution.py:227
  492.7 17.5 %collective-permute-start.41 = (bf16[2,80,256]{2,1,0:T(8,128)(2,1)}, bf16[2,80,256]{2,1,0:T(8,128)(2,1)}, u32[]{:S(2)}, u32[]{:S(2)}) collective-permute-start(bf16[2,80,256]{2,1,0:T(8,128)(2,1)} %get-tuple-element.241), channel_id=1, source_target_pairs={{0,6},{1,7},{2,4},{3,5},{4,2},{5,3},{6,0},{7,1},{8,14},{9,15},{10,... | collective-permute-start | bytes 245768 | tf_op jit(solution)/shard_map/ppermute | solution.py:227
  494.1 16.0 %collective-permute-start.40 = (bf16[2,80,256]{2,1,0:T(8,128)(2,1)}, bf16[2,80,256]{2,1,0:T(8,128)(2,1)}, u32[]{:S(2)}, u32[]{:S(2)}) collective-permute-start(bf16[2,80,256]{2,1,0:T(8,128)(2,1)} %get-tuple-element.242), channel_id=1, source_target_pairs={{0,4},{1,5},{2,6},{3,7},{4,0},{5,1},{6,2},{7,3},{8,12},{9,13},{10,... | collective-permute-start | bytes 245768 | tf_op jit(solution)/shard_map/ppermute | solution.py:227
  494.1 16.0 %collective-permute-start.39 = (bf16[2,80,256]{2,1,0:T(8,128)(2,1)S(1)}, bf16[2,80,256]{2,1,0:T(8,128)(2,1)}, u32[]{:S(2)}, u32[]{:S(2)}) collective-permute-start(bf16[2,80,256]{2,1,0:T(8,128)(2,1)S(1)} %get-tuple-element.240), channel_id=1, source_target_pairs={{0,2},{1,3},{2,0},{3,1},{4,6},{5,7},{6,4},{7,5},{8,10},{9,11},{10,... | collective-permute-start | bytes 245768 | tf_op jit(solution)/shard_map/ppermute | solution.py:227
  (85 other events, 801.7 us)
Sparse Core Ops, SparseCore 0:
  9.6 31.7 all-gather.11
  50.0 39.1 all-gather.13
  100.8 51.6 all-gather.9
  165.8 54.8 all-gather.15
  224.1 53.8 all-gather.17
  313.4 58.6 reduce-scatter.4
  390.1 58.2 reduce-scatter.6
  450.7 49.0 reduce-scatter.8
  504.5 39.9 reduce-scatter.10
